TPU v7x, 32 devices: a whole 2x2x4 slice. The times are simulated.
32 devices in a mesh: space: 8 (over z, y), rep: 4 (over x, core).
Axes of the slice: x: 2, y: 2, z: 4, core: 2. Of those that a mesh axis runs over, the one named last changes fastest.
Arguments:
- volumes: bfloat16 [4, 8, 8, 4, 16, 256], P('rep', 'space'), may hold values from -6 to 6
- grad_parts: bfloat16 [4, 2, 6912, 256], P('rep', None, 'space'), may hold values from -6 to 6
- master_weights: float32 [2, 6912, 256], P(None, 'space'), may hold values from -0.078125 to 0.078125
- moment_first: float32 [4, 2, 6912, 256], P('rep', None, 'space'), may hold values from -12 to 12
- moment_second: float32 [4, 2, 6912, 256], P('rep', None, 'space'), may hold values from 1 to 30
- owner: int32 [2, 32], replicated, may hold values from 0 to 3
Outputs:
- features: bfloat16 [4, 8, 8, 4, 16, 256], P('rep', 'space')
- new_weights: float32 [2, 1769472], P(None, ('space', 'rep'))
- moment_first_out: float32 [4, 2, 6912, 256], P('rep', None, 'space')
- moment_second_out: float32 [4, 2, 6912, 256], P('rep', None, 'space')
Inputs may be any that keep to these rules, and one draw needn't show every extreme that they name: owner[f, p] is the replica whose state slot holds the optimizer state of panel p of filter f, rows p * 216 to (p + 1) * 216 - 1; replicas may own unequal numbers of panels.
All inputs are finite; a program needn't handle non-finite values.
Results may differ from a plain program's by a relative error of at most 0.0095.
Values may be sent and summed in bfloat16 or wider, within the bound.
No kernel may reach another device: no remote copies, remote signals or barrier semaphores. Data moves between devices by JAX's collectives and lax.ppermute only.
A program may use at most 64 MiB of HBM per device.

v0:
```python
import functools

import jax
import jax.numpy as jnp
from jax import lax
from jax.experimental import pallas as pl
from jax.experimental.pallas import tpu as pltpu
from jax.sharding import PartitionSpec as P


GY = 2
GZ = 2
PANEL_ROWS = 216


def swap(value, axis, stride):
    count = lax.axis_size(axis)
    return lax.ppermute(value, axis, [(source, source ^ stride) for source in range(count)])


def passed_along(value, axis, steps):
    count = lax.axis_size(axis)
    first, last = (max(0, -steps), min(count, count - steps))
    return lax.ppermute(value, axis, [(source, source + steps) for source in range(first, last)])


def pick(flag, one, other):
    return jnp.where(flag, one, other)


def extend_brick(brick, coords, strides, grid):
    current = brick
    for dim in range(3):
        length = current.shape[dim]
        first = lax.slice_in_dim(current, 0, 1, 1, dim)
        last = lax.slice_in_dim(current, length - 1, length, 1, dim)
        if grid[dim] == 2:
            low = coords[dim] == 0
            came = swap(pick(low, last, first), "space", strides[dim])
            none = jnp.zeros_like(came)
            lower, upper = pick(low, none, came), pick(low, came, none)
        else:
            none = jnp.zeros_like(first)
            lower = pick(coords[dim] > 0, passed_along(last, "space", strides[dim]), none)
            upper = pick(
                coords[dim] < grid[dim] - 1, passed_along(first, "space", -strides[dim]), none
            )
        current = jnp.concatenate([lower, current, upper], axis=dim)
    return current


def place_of(row_shares):
    rep_pos = lax.axis_index("rep")
    return lax.axis_index("space"), (rep_pos >> 1) & (row_shares - 1), rep_pos & 1


def conv_kernel(places, span, field_ref, *refs):
    pieces, (out_ref, weights, lines) = refs[: len(places)], refs[len(places) :]
    rows_dev, height = span
    space_pos, row_pos, col_pos = place_of(rows_dev // height)
    extent_x, extent_y, extent_z, channels = out_ref.shape
    for piece_ref, place in zip(pieces, places):
        for slot, (space_mask, row_mask, col_mask) in enumerate(place):
            start = (space_pos ^ space_mask) * rows_dev + (row_pos ^ row_mask) * height
            weights[col_pos ^ col_mask, pl.ds(pl.multiple_of(start, 8), height), :] = piece_ref[slot]
    for along_x in range(extent_x + 2):
        field = field_ref[along_x].astype(jnp.float32)
        for shift in range(3):
            lines[along_x, :, :, shift * channels : (shift + 1) * channels] = field[
                :, shift : shift + extent_z
            ].astype(lines.dtype)
    depth = 3 * channels
    total = jnp.zeros((extent_x * extent_y * extent_z, channels), jnp.float32)
    for shift_x in range(3):
        for shift_y in range(3):
            start = (shift_x * 3 + shift_y) * depth
            window = lines[shift_x : shift_x + extent_x, shift_y : shift_y + extent_y]
            taps = jnp.concatenate(
                [weights[0, start : start + depth, :], weights[1, start : start + depth, :]], axis=1
            )
            total = total + jnp.dot(
                window.reshape(-1, depth), taps, preferred_element_type=jnp.float32
            )
    out_ref[...] = jax.nn.gelu(total, approximate=True).astype(out_ref.dtype).reshape(out_ref.shape)


def convolve(extended, pieces, places, span):
    shape = (extended.shape[0] - 2, extended.shape[1] - 2, extended.shape[2] - 2, extended.shape[3])
    channels = shape[3]
    cells = shape[0] * shape[1] * shape[2]
    rows = 27 * channels
    return pl.pallas_call(
        functools.partial(conv_kernel, places, span),
        out_shape=jax.ShapeDtypeStruct(shape, jnp.bfloat16),
        in_specs=[pl.BlockSpec(memory_space=pltpu.VMEM)] * (1 + len(pieces)),
        out_specs=pl.BlockSpec(memory_space=pltpu.VMEM),
        scratch_shapes=[
            pltpu.VMEM((2, rows, channels // 2), jnp.bfloat16),
            pltpu.VMEM((shape[0] + 2, shape[1] + 2, shape[2], 3 * channels), jnp.bfloat16),
        ],
        compiler_params=pltpu.CompilerParams(vmem_limit_bytes=16 * 2**20),
        cost_estimate=pl.CostEstimate(
            flops=2 * cells * rows * channels,
            bytes_accessed=2 * rows * channels + 4 * cells * channels,
            transcendentals=cells * channels,
        ),
    )(extended, *pieces)


def split_kernel(index, *refs):
    arrays, all_owners, (kept_ref, sent_ref) = refs[:3], refs[3], refs[-8:-6]
    buffers, owners, sems, owner_sem = refs[-6:-3], refs[-3], refs[-2], refs[-1]
    panels = buffers[0].shape[0]
    space_pos, rep_pos = lax.axis_index("space"), lax.axis_index("rep")
    left = rep_pos & 1 == 0
    half = kept_ref.shape[2]
    copy_owners = pltpu.make_async_copy(all_owners, owners, owner_sem)
    copy_owners.start()
    copies = []
    for panel in range(panels):
        rows = pl.ds(panel * PANEL_ROWS, PANEL_ROWS)
        for slot in range(3):
            copies.append(
                pltpu.make_async_copy(
                    arrays[slot].at[0, index, rows, :],
                    buffers[slot].at[panel],
                    sems.at[panel, slot],
                )
            )
            copies[-1].start()
    copy_owners.wait()
    for panel in range(panels):
        owned = owners[index, space_pos * panels + panel] == rep_pos
        rows = slice(panel * PANEL_ROWS, (panel + 1) * PANEL_ROWS)
        for slot in range(3):
            copies[3 * panel + slot].wait()
            part = buffers[slot][panel].astype(jnp.float32)
            if slot:
                part = jnp.where(owned, part, 0.0)
            one, other = part[:, :half], part[:, half:]
            kept_ref[slot, rows, :] = jnp.where(left, one, other).astype(kept_ref.dtype)
            sent_ref[slot, rows, :] = jnp.where(left, other, one).astype(sent_ref.dtype)


def split_state(index, owner, *arrays, after=()):
    rows, channels = arrays[0].shape[2:]
    half = channels // 2
    panels = rows // PANEL_ROWS
    shape = jax.ShapeDtypeStruct((3, rows, half), jnp.bfloat16)
    vmem = pl.BlockSpec(memory_space=pltpu.VMEM)
    held = [pltpu.with_memory_space_constraint(array, pltpu.HBM) for array in (*arrays, owner)]
    return pl.pallas_call(
        functools.partial(split_kernel, index),
        out_shape=(shape, shape),
        in_specs=[pl.BlockSpec(memory_space=pltpu.HBM)] * len(held)
        + [pl.BlockSpec(memory_space=pl.ANY)] * len(after),
        out_specs=(vmem, vmem),
        scratch_shapes=[
            pltpu.VMEM((panels, PANEL_ROWS, channels), array.dtype) for array in arrays
        ]
        + [
            pltpu.SMEM(owner.shape, owner.dtype),
            pltpu.SemaphoreType.DMA((panels, 3)),
            pltpu.SemaphoreType.DMA,
        ],
        compiler_params=pltpu.CompilerParams(vmem_limit_bytes=6 * 2**20),
        cost_estimate=pl.CostEstimate(
            flops=4 * rows * channels, bytes_accessed=16 * rows * channels, transcendentals=0
        ),
    )(*held, *after)


def across_kernel(kept_ref, came_ref, sent_ref):
    height = sent_ref.shape[1]
    row_pos = place_of(2)[1]
    rows = pl.ds(pl.multiple_of((1 - row_pos) * height, 8), height)
    for slot in range(3):
        total = kept_ref[slot, rows, :].astype(jnp.float32) + came_ref[slot, rows, :].astype(jnp.float32)
        sent_ref[slot] = total.astype(sent_ref.dtype)


def across(kept, came, height):
    vmem = pl.BlockSpec(memory_space=pltpu.VMEM)
    return pl.pallas_call(
        across_kernel,
        out_shape=jax.ShapeDtypeStruct((3, height, kept.shape[2]), jnp.bfloat16),
        in_specs=[vmem, vmem],
        out_specs=vmem,
        compiler_params=pltpu.CompilerParams(vmem_limit_bytes=4 * 2**20),
        cost_estimate=pl.CostEstimate(
            flops=3 * height * kept.shape[2],
            bytes_accessed=18 * height * kept.shape[2],
            transcendentals=0,
        ),
    )(kept, came)


def update_kernel(index, all_master, kept_ref, came_ref, *refs):
    piece_ref, sum_ref, master_ref, sem = refs[-4:]
    height, half = piece_ref.shape
    _, row_pos, col_pos = place_of(kept_ref.shape[1] // height)
    rows = pl.ds(pl.multiple_of(row_pos * height, 8), height)
    columns = pl.ds(pl.multiple_of(col_pos * half, 128), half)
    copy = pltpu.make_async_copy(all_master.at[index, rows, columns], master_ref, sem)
    copy.start()
    state = []
    for slot in range(3):
        total = kept_ref[slot, rows, :].astype(jnp.float32) + came_ref[slot, rows, :].astype(jnp.float32)
        for crossed_ref in refs[:-4]:
            total = total + crossed_ref[slot].astype(jnp.float32)
        state.append(total)
    grad, first, second = state
    first = 0.9 * first + 0.1 * grad
    second = 0.95 * second + 0.05 * (grad * grad)
    corr_one = 1.0 - 0.9**10
    corr_two = 1.0 - 0.95**10
    sum_ref[...] = grad.astype(sum_ref.dtype)
    ratio = first / corr_one / (jnp.sqrt(second / corr_two) + 1e-08)
    copy.wait()
    master = master_ref[...]
    piece_ref[...] = (master - 0.004 * (ratio + 0.1 * master)).astype(piece_ref.dtype)


def updated(index, height, master, kept, came, crossed):
    vmem = pl.BlockSpec(memory_space=pltpu.VMEM)
    half = kept.shape[2]
    rounded = jax.ShapeDtypeStruct((height, half), jnp.bfloat16)
    size = height * half
    return pl.pallas_call(
        functools.partial(update_kernel, index),
        out_shape=(rounded, rounded),
        in_specs=[pl.BlockSpec(memory_space=pltpu.HBM)] + [vmem] * (2 + len(crossed)),
        out_specs=(vmem, vmem),
        scratch_shapes=[pltpu.VMEM((height, half), jnp.float32), pltpu.SemaphoreType.DMA],
        compiler_params=pltpu.CompilerParams(vmem_limit_bytes=4 * 2**20),
        cost_estimate=pl.CostEstimate(
            flops=20 * size, bytes_accessed=30 * size, transcendentals=2 * size
        ),
    )(pltpu.with_memory_space_constraint(master, pltpu.HBM), kept, came, *crossed)


def gathered(piece, row_shares, last):
    strides = []
    stride = lax.axis_size("space") // 2
    while stride:
        strides.append(stride)
        stride //= 2
    held, masks = piece[None], [(0, 0)]
    for stride in strides[:-2]:
        held = jnp.concatenate([held, swap(held, "space", stride)])
        masks = masks + [(space ^ stride, row) for space, row in masks]

    def moved(found, way):
        array, places = found
        if way == "x":
            array = swap(array, "rep", 2)
            places = [(space, row ^ 1) for space, row in places]
        else:
            stride = strides[-1] if way == "y" else strides[-2]
            array = swap(array, "space", stride)
            places = [(space ^ stride, row) for space, row in places]
        return array, places

    own = (held, masks)
    z, y = moved(own, "z"), moved(own, "y")
    yz = moved(y, "z")
    found = [own, z, y, yz]
    if row_shares == 2:
        x = moved(own, "x")
        xy, zx = moved(x, "y"), moved(z, "x")
        corner = moved({"y": zx, "z": xy, "x": yz}[last], last)
        found += [x, xy, zx, corner]
    arrays, places = [], []
    for array, place in found:
        arrays += [array, swap(array, "rep", 1)]
        places += [tuple((s, r, c) for s, r in place) for c in range(2)]
    return arrays, tuple(places)


def shards(volumes, grad_parts, master_weights, moment_first, moment_second, owner):
    filter_count, rows_dev, channels = master_weights.shape
    panels_dev = rows_dev // PANEL_ROWS
    replicas = lax.axis_size("rep")
    row_shares = 2 if replicas % 4 == 0 and rows_dev % 16 == 0 else 1
    height = rows_dev // row_shares
    space_pos = lax.axis_index("space")
    rep_pos = lax.axis_index("rep")
    col_pos = rep_pos & 1
    row_pos = (rep_pos >> 1) & (row_shares - 1)
    left, top = col_pos == 0, row_pos == 0
    owner_local = lax.dynamic_slice_in_dim(owner, space_pos * panels_dev, panels_dev, 1)
    owned = (jnp.repeat(owner_local, PANEL_ROWS, axis=1) == rep_pos)[:, :, None]

    grid = (lax.axis_size("space") // (GY * GZ), GY, GZ)
    strides = (GY * GZ, GZ, 1)
    coords = (space_pos // (GY * GZ), space_pos // GZ % GY, space_pos % GZ)

    split = []
    for index in range(filter_count):
        kept, sent = split_state(
            index,
            owner,
            grad_parts,
            moment_first,
            moment_second,
            after=[split[-1][0]] if split else [],
        )
        stride = replicas // 2
        while stride >= 2 * row_shares:
            kept, sent = [
                (part.astype(jnp.float32) + swap(part, "rep", stride).astype(jnp.float32)).astype(
                    jnp.bfloat16
                )
                for part in (kept, sent)
            ]
            stride //= 2
        split.append((kept, swap(sent, "rep", 1)))
    extended = extend_brick(volumes[0, 0], coords, strides, grid)
    sums, pieces = [], []
    for index, (kept, came) in enumerate(split):
        crossed = []
        if row_shares == 2:
            crossed.append(swap(across(kept, came, height), "rep", 2))
        piece, summed = updated(index, height, master_weights, kept, came, crossed)
        pieces.append(piece)
        sums.append(summed)

    span = (rows_dev, height)

    def rebuilt(share):
        if row_shares == 2:
            came = swap(share, "rep", 2)
            share = pick(
                top, jnp.concatenate([share, came], -2), jnp.concatenate([came, share], -2)
            )
        came = swap(share, "rep", 1)
        return pick(left, jnp.concatenate([share, came], -1), jnp.concatenate([came, share], -1))

    hidden, beside = extended, []
    for index in range(filter_count):
        if index:
            hidden = extend_brick(hidden, coords, strides, grid)
        arrays, places = gathered(pieces[index], row_shares, "yz"[index % 2])
        beside.append(arrays[1][0])
        hidden = convolve(hidden, arrays, places, span)

    summed_grad = rebuilt(jnp.stack(sums)).astype(jnp.float32)
    first_new = 0.9 * moment_first[0] + 0.1 * summed_grad
    second_new = 0.95 * moment_second[0] + 0.05 * (summed_grad * summed_grad)
    first_out = jnp.where(owned, first_new, moment_first[0])[None]
    second_out = jnp.where(owned, second_new, moment_second[0])[None]

    if replicas == 2 * row_shares:
        middle = height // 2

        def own_half(array):
            return pick(left, array[:, :middle], array[:, middle:])

        kept, came = own_half(jnp.stack(pieces)), own_half(jnp.stack(beside))
        new_weights = pick(
            left, jnp.concatenate([kept, came], -1), jnp.concatenate([came, kept], -1)
        ).reshape(filter_count, -1)
    else:
        length = rows_dev * channels // replicas
        new_weights = lax.dynamic_slice_in_dim(
            rebuilt(jnp.stack(pieces)).reshape(filter_count, -1),
            rep_pos * length,
            length,
            1,
        )
    new_weights = new_weights.astype(jnp.float32)
    return (hidden[None, None], new_weights, first_out, second_out)


def solution(mesh):
    placed = (
        P("rep", "space", None, None, None, None),
        P("rep", None, "space", None),
        P(None, "space", None),
        P("rep", None, "space", None),
        P("rep", None, "space", None),
        P(),
    )
    return jax.shard_map(
        shards,
        mesh=mesh,
        in_specs=placed,
        out_specs=(
            P("rep", "space", None, None, None, None),
            P(None, ("space", "rep")),
            P("rep", None, "space", None),
            P("rep", None, "space", None),
        ),
        check_vma=False,
    )
```

profile of v0, /device:TPU:0, one launch (start us, length us, event | category | flops | bytes accessed | tf_op | source)
XLA Modules:
  0.0 95.7 jit_solution(11800580988744560608)
XLA Ops:
  0.6 1.8 %shard_map.93 = (bf16[3,864,128]{2,1,0:T(8,128)(2,1)S(1)}, bf16[3,864,128]{2,1,0:T(8,128)(2,1)S(1)}) custom-call(bf16[1,2,864,256]{3,2,1,0:T(8,128)(2,1)} %refs_0_.3, f32[1,2,864,256]{3,2,1,0:T(8,128)} %refs_1_.3, f32[1,2,864,256]{3,2,1,0:T(8,128)} %refs_2_.3, s32[2,32]{1,0:T(2,128)} %refs_3_.3), custom_call_target="tpu_custom_call" | custom-call | flops 884736 | bytes 3538944 | tf_op jit(solution)/shard_map/pallas_call | solution.py:152
  2.4 0.6 collective-permute-start.3
  3.0 2.6 %shard_map.97 = (bf16[3,864,128]{2,1,0:T(8,128)(2,1)S(1)}, bf16[3,864,128]{2,1,0:T(8,128)(2,1)}) custom-call(bf16[1,2,864,256]{3,2,1,0:T(8,128)(2,1)} %refs_0_.3, f32[1,2,864,256]{3,2,1,0:T(8,128)} %refs_1_.3, f32[1,2,864,256]{3,2,1,0:T(8,128)} %refs_2_.3, s32[2,32]{1,0:T(2,128)} %refs_3_.3, bf16[3,864,128]{2,1,0:T(8,128)(2,1)S(1)} %get-tuple-element.12.kept_ref.refs_4_), custom_call_target="tpu_custom_call" | custom-call | flops 884736 | bytes 3538944 | tf_op jit(solution)/shard_map/pallas_call | solution.py:152
  5.6 0.1 collective-permute-start.24
  5.7 0.8 select_bitcast_fusion
  6.5 4.0 %collective-permute-start = (bf16[1,4,16,256]{3,2,1,0:T(8,128)(2,1)S(1)}, bf16[1,4,16,256]{3,2,1,0:T(8,128)(2,1)S(1)}, u32[]{:S(2)}, u32[]{:S(2)}) collective-permute-start(bf16[1,4,16,256]{3,2,1,0:T(8,128)(2,1)S(1)} %select_bitcast_fusion), channel_id=1, source_target_pairs={{0,16},{4,20},{8,24},{12,28},{16,0},{20,4},{24,8},{28,12},{1,17},{... | collective-permute-start | bytes 98312 | tf_op jit(solution)/shard_map/ppermute | solution.py:18
  10.5 1.9 %collective-permute-done = bf16[1,4,16,256]{3,2,1,0:T(8,128)(2,1)S(1)} collective-permute-done((bf16[1,4,16,256]{3,2,1,0:T(8,128)(2,1)S(1)}, bf16[1,4,16,256]{3,2,1,0:T(8,128)(2,1)S(1)}, u32[]{:S(2)}, u32[]{:S(2)}) %collective-permute-start) | collective-permute-done | bytes 32800 | tf_op jit(solution)/shard_map/ppermute | solution.py:18
  12.4 0.9 fusion.10
  13.3 2.0 %collective-permute-start.1 = (bf16[10,1,16,256]{3,2,1,0:T(8,128)(2,1)S(1)}, bf16[10,1,16,256]{3,2,1,0:T(8,128)(2,1)S(1)}, u32[]{:S(2)}, u32[]{:S(2)}) collective-permute-start(bf16[10,1,16,256]{3,2,1,0:T(8,128)(2,1)S(1)} %fusion.10), channel_id=1, source_target_pairs={{0,8},{4,12},{8,0},{12,4},{16,24},{20,28},{24,16},{28,20},{1,9},{5... | collective-permute-start | bytes 245768 | tf_op jit(solution)/shard_map/ppermute | solution.py:18
  15.4 1.6 %collective-permute-start.4 = (bf16[3,432,128]{2,1,0:T(8,128)(2,1)S(1)}, bf16[3,432,128]{2,1,0:T(8,128)(2,1)}, u32[]{:S(2)}, u32[]{:S(2)}) collective-permute-start(bf16[3,432,128]{2,1,0:T(8,128)(2,1)S(1)} %shard_map.94), channel_id=1, source_target_pairs={{0,2},{1,3},{2,0},{3,1},{4,6},{5,7},{6,4},{7,5},{8,10},{9,11},{10,... | collective-permute-start | bytes 995336 | tf_op jit(solution)/shard_map/ppermute | solution.py:18
  17.0 0.6 collective-permute-start.25
  17.8 0.1 eq.41
  17.9 8.3 %collective-permute-done.4.refs_0_ = bf16[3,432,128]{2,1,0:T(8,128)(2,1)} collective-permute-done((bf16[3,432,128]{2,1,0:T(8,128)(2,1)S(1)}, bf16[3,432,128]{2,1,0:T(8,128)(2,1)}, u32[]{:S(2)}, u32[]{:S(2)}) %collective-permute-start.4) | collective-permute-done | bytes 331808 | tf_op jit(solution)/shard_map/ppermute | solution.py:18
  26.2 2.0 %shard_map.95 = (bf16[432,128]{1,0:T(8,128)(2,1)S(1)}, bf16[432,128]{1,0:T(8,128)(2,1)S(1)}) custom-call(f32[2,864,256]{2,1,0:T(8,128)} %all_master.3, bf16[3,864,128]{2,1,0:T(8,128)(2,1)S(1)} %get-tuple-element.12.kept_ref.refs_4_, bf16[3,864,128]{2,1,0:T(8,128)(2,1)S(1)} %collective-permute-done.3.came_ref, bf16[3,432,128]{2,1,0:T(8,128)(2,1)} %collective-permute-done.4.refs_0_), custom_call_target="tpu_custom_call" | custom-call | flops 1105920 | bytes 1658880 | tf_op jit(solution)/shard_map/pallas_call | solution.py:229
  28.2 2.9 %collective-permute-start.5 = (bf16[1,432,128]{2,1,0:T(8,128)(2,1)S(1)}, bf16[1,432,128]{2,1,0:T(8,128)(2,1)S(1)}, u32[]{:S(2)}, u32[]{:S(2)}) collective-permute-start(bf16[1,432,128]{2,1,0:T(8,128)(2,1)S(1)} %bitcast.20), channel_id=1, source_target_pairs={{0,16},{4,20},{8,24},{12,28},{16,0},{20,4},{24,8},{28,12},{1,17},{... | collective-permute-start | bytes 331784 | tf_op jit(solution)/shard_map/ppermute | solution.py:18
  31.1 2.0 %shard_map.99 = (bf16[432,128]{1,0:T(8,128)(2,1)S(1)}, bf16[432,128]{1,0:T(8,128)(2,1)S(1)}) custom-call(f32[2,864,256]{2,1,0:T(8,128)} %all_master.3, bf16[3,864,128]{2,1,0:T(8,128)(2,1)S(1)} %get-tuple-element.15.kept_ref, bf16[3,864,128]{2,1,0:T(8,128)(2,1)S(1)} %collective-permute-done.24.came_ref, bf16[3,432,128]{2,1,0:T(8,128)(2,1)} %collective-permute-done.25.refs_0_), custom_call_target="tpu_custom_call" | custom-call | flops 1105920 | bytes 1658880 | tf_op jit(solution)/shard_map/pallas_call | solution.py:229
  33.1 2.8 %collective-permute-start.26 = (bf16[1,432,128]{2,1,0:T(8,128)(2,1)S(1)}, bf16[1,432,128]{2,1,0:T(8,128)(2,1)S(1)}, u32[]{:S(2)}, u32[]{:S(2)}) collective-permute-start(bf16[1,432,128]{2,1,0:T(8,128)(2,1)S(1)} %bitcast.23), channel_id=1, source_target_pairs={{0,16},{4,20},{8,24},{12,28},{16,0},{20,4},{24,8},{28,12},{1,17},{... | collective-permute-start | bytes 331784 | tf_op jit(solution)/shard_map/ppermute | solution.py:18
  35.9 1.6 %collective-permute-start.42 = (bf16[2,432,128]{2,1,0:T(8,128)(2,1)S(1)}, bf16[2,432,128]{2,1,0:T(8,128)(2,1)S(1)}, u32[]{:S(2)}, u32[]{:S(2)}) collective-permute-start(bf16[2,432,128]{2,1,0:T(8,128)(2,1)S(1)} %pad_maximum_fusion.4), channel_id=1, source_target_pairs={{0,2},{1,3},{2,0},{3,1},{4,6},{5,7},{6,4},{7,5},{8,10},{9,11},{10,... | collective-permute-start | bytes 663560 | tf_op jit(solution)/shard_map/ppermute | solution.py:18
  37.5 0.4 collective-permute-start.7
  37.8 0.1 broadcast_select_fusion.5
  37.9 1.6 %collective-permute-start.2 = (bf16[10,6,1,256]{3,2,1,0:T(2,128)(2,1)S(1)}, bf16[10,6,1,256]{3,2,1,0:T(2,128)(2,1)S(1)}, u32[]{:S(2)}, u32[]{:S(2)}) collective-permute-start(bf16[10,6,1,256]{3,2,1,0:T(2,128)(2,1)S(1)} %broadcast_select_fusion.5), channel_id=1, source_target_pairs={{0,4},{4,0},{8,12},{12,8},{16,20},{20,16},{24,28},{28,24},{1,5},{5... | collective-permute-start | bytes 92168 | tf_op jit(solution)/shard_map/ppermute | solution.py:18
  39.5 0.5 collective-permute-start.9
  40.0 1.3 %collective-permute-start.13 = (bf16[2,432,128]{2,1,0:T(8,128)(2,1)S(1)}, bf16[2,432,128]{2,1,0:T(8,128)(2,1)S(1)}, u32[]{:S(2)}, u32[]{:S(2)}) collective-permute-start(bf16[2,432,128]{2,1,0:T(8,128)(2,1)S(1)} %pad_maximum_fusion.2.refs_0_), channel_id=1, source_target_pairs={{0,2},{1,3},{2,0},{3,1},{4,6},{5,7},{6,4},{7,5},{8,10},{9,11},{10,... | collective-permute-start | bytes 663560 | tf_op jit(solution)/shard_map/ppermute | solution.py:18
  41.4 0.9 collective-permute-done.2
  42.2 1.7 %collective-permute-done.42 = bf16[2,432,128]{2,1,0:T(8,128)(2,1)S(1)} collective-permute-done((bf16[2,432,128]{2,1,0:T(8,128)(2,1)S(1)}, bf16[2,432,128]{2,1,0:T(8,128)(2,1)S(1)}, u32[]{:S(2)}, u32[]{:S(2)}) %collective-permute-start.42) | collective-permute-done | bytes 221216 | tf_op jit(solution)/shard_map/ppermute | solution.py:18
  44.0 1.2 %collective-permute-start.17 = (bf16[2,432,128]{2,1,0:T(8,128)(2,1)S(1)}, bf16[2,432,128]{2,1,0:T(8,128)(2,1)S(1)}, u32[]{:S(2)}, u32[]{:S(2)}) collective-permute-start(bf16[2,432,128]{2,1,0:T(8,128)(2,1)S(1)} %collective-permute-done.7.refs_2_), channel_id=1, source_target_pairs={{0,2},{1,3},{2,0},{3,1},{4,6},{5,7},{6,4},{7,5},{8,10},{9,11},{10,... | collective-permute-start | bytes 663560 | tf_op jit(solution)/shard_map/ppermute | solution.py:18
  45.2 0.1 broadcast_select_fusion.4
  45.3 0.1 collective-permute-done.9.refs_4_
  45.5 1.7 %collective-permute-start.11 = (bf16[2,432,128]{2,1,0:T(8,128)(2,1)S(1)}, bf16[2,432,128]{2,1,0:T(8,128)(2,1)S(1)}, u32[]{:S(2)}, u32[]{:S(2)}) collective-permute-start(bf16[2,432,128]{2,1,0:T(8,128)(2,1)S(1)} %collective-permute-done.9.refs_4_), channel_id=1, source_target_pairs={{0,8},{4,12},{8,0},{12,4},{16,24},{20,28},{24,16},{28,20},{1,9},{5... | collective-permute-start | bytes 663560 | tf_op jit(solution)/shard_map/ppermute | solution.py:18
  47.2 1.0 collective-permute-start.15
  48.1 0.2 collective-permute-start.14
  48.4 3.4 %collective-permute-done.17.refs_12_ = bf16[2,432,128]{2,1,0:T(8,128)(2,1)S(1)} collective-permute-done((bf16[2,432,128]{2,1,0:T(8,128)(2,1)S(1)}, bf16[2,432,128]{2,1,0:T(8,128)(2,1)S(1)}, u32[]{:S(2)}, u32[]{:S(2)}) %collective-permute-start.17) | collective-permute-done | bytes 221216 | tf_op jit(solution)/shard_map/ppermute | solution.py:18
  51.8 1.3 %collective-permute-start.19 = (bf16[2,432,128]{2,1,0:T(8,128)(2,1)S(1)}, bf16[2,432,128]{2,1,0:T(8,128)(2,1)S(1)}, u32[]{:S(2)}, u32[]{:S(2)}) collective-permute-start(bf16[2,432,128]{2,1,0:T(8,128)(2,1)S(1)} %collective-permute-done.17.refs_12_), channel_id=1, source_target_pairs={{0,4},{4,0},{8,12},{12,8},{16,20},{20,16},{24,28},{28,24},{1,5},{5... | collective-permute-start | bytes 663560 | tf_op jit(solution)/shard_map/ppermute | solution.py:18
  53.1 0.5 pad_maximum_fusion.field_ref
  53.7 1.9 %collective-permute-done.15.refs_10_ = bf16[2,432,128]{2,1,0:T(8,128)(2,1)S(1)} collective-permute-done((bf16[2,432,128]{2,1,0:T(8,128)(2,1)S(1)}, bf16[2,432,128]{2,1,0:T(8,128)(2,1)S(1)}, u32[]{:S(2)}, u32[]{:S(2)}) %collective-permute-start.15) | collective-permute-done | bytes 221216 | tf_op jit(solution)/shard_map/ppermute | solution.py:18
  55.6 0.5 collective-permute-start.12
  56.1 3.6 %collective-permute-done.19.refs_14_ = bf16[2,432,128]{2,1,0:T(8,128)(2,1)S(1)} collective-permute-done((bf16[2,432,128]{2,1,0:T(8,128)(2,1)S(1)}, bf16[2,432,128]{2,1,0:T(8,128)(2,1)S(1)}, u32[]{:S(2)}, u32[]{:S(2)}) %collective-permute-start.19) | collective-permute-done | bytes 221216 | tf_op jit(solution)/shard_map/ppermute | solution.py:18
  59.8 0.1 maximum_select_fusion.1
  59.9 0.1 fusion.11
  60.1 1.3 %collective-permute-start.34 = (bf16[2,432,128]{2,1,0:T(8,128)(2,1)S(1)}, bf16[2,432,128]{2,1,0:T(8,128)(2,1)S(1)}, u32[]{:S(2)}, u32[]{:S(2)}) collective-permute-start(bf16[2,432,128]{2,1,0:T(8,128)(2,1)S(1)} %pad_maximum_fusion.3.refs_0_), channel_id=1, source_target_pairs={{0,2},{1,3},{2,0},{3,1},{4,6},{5,7},{6,4},{7,5},{8,10},{9,11},{10,... | collective-permute-start | bytes 663560 | tf_op jit(solution)/shard_map/ppermute | solution.py:18
  61.4 1.2 %collective-permute-start.30 = (bf16[2,432,128]{2,1,0:T(8,128)(2,1)S(1)}, bf16[2,432,128]{2,1,0:T(8,128)(2,1)S(1)}, u32[]{:S(2)}, u32[]{:S(2)}) collective-permute-start(bf16[2,432,128]{2,1,0:T(8,128)(2,1)S(1)} %pad_maximum_fusion.3.refs_0_), channel_id=1, source_target_pairs={{0,4},{4,0},{8,12},{12,8},{16,20},{20,16},{24,28},{28,24},{1,5},{5... | collective-permute-start | bytes 663560 | tf_op jit(solution)/shard_map/ppermute | solution.py:18
  62.6 0.9 collective-permute-start.28
  63.5 2.3 %shard_map.96 = bf16[8,4,16,256]{3,2,1,0:T(8,128)(2,1)S(1)} custom-call(bf16[10,6,18,256]{3,2,1,0:T(8,128)(2,1)S(1)} %pad_maximum_fusion.field_ref, bf16[2,432,128]{2,1,0:T(8,128)(2,1)S(1)} %pad_maximum_fusion.2.refs_0_, bf16[2,432,128]{2,1,0:T(8,128)(2,1)S(1)} %collective-permute-done.6.refs_1_, bf16[2,432,128]{2,1,0:T(8,128)(2,1)S(1)} %collective-permute-done.7.refs_2_, ...), custom_call_target="tpu_custom_call" | custom-call | flops 1811939328 | bytes 4063232 | tf_op jit(solution)/shard_map/pallas_call | solution.py:92
  65.8 1.7 %collective-permute-start.21 = (bf16[1,4,16,256]{3,2,1,0:T(8,128)(2,1)S(1)}, bf16[1,4,16,256]{3,2,1,0:T(8,128)(2,1)S(1)}, u32[]{:S(2)}, u32[]{:S(2)}) collective-permute-start(bf16[1,4,16,256]{3,2,1,0:T(8,128)(2,1)S(1)} %slice_select_fusion), channel_id=1, source_target_pairs={{0,16},{4,20},{8,24},{12,28},{16,0},{20,4},{24,8},{28,12},{1,17},{... | collective-permute-start | bytes 98312 | tf_op jit(solution)/shard_map/ppermute | solution.py:18
  67.6 3.2 %collective-permute-done.21 = bf16[1,4,16,256]{3,2,1,0:T(8,128)(2,1)S(1)} collective-permute-done((bf16[1,4,16,256]{3,2,1,0:T(8,128)(2,1)S(1)}, bf16[1,4,16,256]{3,2,1,0:T(8,128)(2,1)S(1)}, u32[]{:S(2)}, u32[]{:S(2)}) %collective-permute-start.21) | collective-permute-done | bytes 32800 | tf_op jit(solution)/shard_map/ppermute | solution.py:18
  70.9 2.1 %collective-permute-start.22 = (bf16[10,1,16,256]{3,2,1,0:T(8,128)(2,1)S(1)}, bf16[10,1,16,256]{3,2,1,0:T(8,128)(2,1)S(1)}, u32[]{:S(2)}, u32[]{:S(2)}) collective-permute-start(bf16[10,1,16,256]{3,2,1,0:T(8,128)(2,1)S(1)} %fusion.9), channel_id=1, source_target_pairs={{0,8},{4,12},{8,0},{12,4},{16,24},{20,28},{24,16},{28,20},{1,9},{5... | collective-permute-start | bytes 245768 | tf_op jit(solution)/shard_map/ppermute | solution.py:18
  73.0 1.0 %copy.10 = f32[1,2,216,256]{3,1,2,0:T(2,128)} copy(f32[1,2,216,256]{3,2,1,0:T(8,128)S(1)} %convert_bitcast_fusion) | data formatting | bytes 884736
  74.0 1.2 %collective-permute-start.38 = (bf16[2,432,128]{2,1,0:T(8,128)(2,1)S(1)}, bf16[2,432,128]{2,1,0:T(8,128)(2,1)S(1)}, u32[]{:S(2)}, u32[]{:S(2)}) collective-permute-start(bf16[2,432,128]{2,1,0:T(8,128)(2,1)S(1)} %collective-permute-done.28.refs_2_), channel_id=1, source_target_pairs={{0,2},{1,3},{2,0},{3,1},{4,6},{5,7},{6,4},{7,5},{8,10},{9,11},{10,... | collective-permute-start | bytes 663560 | tf_op jit(solution)/shard_map/ppermute | solution.py:18
  75.2 0.6 collective-permute-start.36
  75.8 1.6 %collective-permute-start.32 = (bf16[2,432,128]{2,1,0:T(8,128)(2,1)S(1)}, bf16[2,432,128]{2,1,0:T(8,128)(2,1)S(1)}, u32[]{:S(2)}, u32[]{:S(2)}) collective-permute-start(bf16[2,432,128]{2,1,0:T(8,128)(2,1)S(1)} %collective-permute-done.30.refs_4_), channel_id=1, source_target_pairs={{0,8},{4,12},{8,0},{12,4},{16,24},{20,28},{24,16},{28,20},{1,9},{5... | collective-permute-start | bytes 663560 | tf_op jit(solution)/shard_map/ppermute | solution.py:18
  77.4 0.1 broadcast_select_fusion.2
  77.5 5.5 %collective-permute-done.36.refs_10_ = bf16[2,432,128]{2,1,0:T(8,128)(2,1)S(1)} collective-permute-done((bf16[2,432,128]{2,1,0:T(8,128)(2,1)S(1)}, bf16[2,432,128]{2,1,0:T(8,128)(2,1)S(1)}, u32[]{:S(2)}, u32[]{:S(2)}) %collective-permute-start.36) | collective-permute-done | bytes 221216 | tf_op jit(solution)/shard_map/ppermute | solution.py:18
  83.1 0.2 collective-permute-done.32.refs_6_
  83.3 0.3 collective-permute-start.40
  83.6 1.5 %collective-permute-start.23 = (bf16[10,6,1,256]{3,2,1,0:T(2,128)(2,1)S(1)}, bf16[10,6,1,256]{3,2,1,0:T(2,128)(2,1)S(1)}, u32[]{:S(2)}, u32[]{:S(2)}) collective-permute-start(bf16[10,6,1,256]{3,2,1,0:T(2,128)(2,1)S(1)} %broadcast_select_fusion.2), channel_id=1, source_target_pairs={{0,4},{4,0},{8,12},{12,8},{16,20},{20,16},{24,28},{28,24},{1,5},{5... | collective-permute-start | bytes 92168 | tf_op jit(solution)/shard_map/ppermute | solution.py:18
  85.1 2.2 %fusion.4 = (f32[1,2,864,256]{3,2,1,0:T(8,128)}, f32[1,2,864,256]{3,2,1,0:T(8,128)}) fusion(f32[1,2,864,256]{3,2,1,0:T(8,128)S(1)} %copy-done.3, pred[2,864]{1,0:T(4,128)(4,1)S(1)} %eq.41, bf16[1,2,864,128]{3,2,1,0:T(8,128)(2,1)S(1)} %fusion.11, bf16[1,2,864,128]{3,2,1,0:T(8,128)(2,1)S(1)} %bitcast.30, pred[]{:T(512)S(6)} %eq.38, ...), kind=kLoop, calls=%fused_computation.6 | loop fusion | flops 8404992 | bytes 7964353 | tf_op jit(solution)/shard_map/jit(_where)/select_n | solution.py:351
  87.3 0.5 collective-permute-start.37
  87.9 3.0 %collective-permute-done.40.refs_14_ = bf16[2,432,128]{2,1,0:T(8,128)(2,1)S(1)} collective-permute-done((bf16[2,432,128]{2,1,0:T(8,128)(2,1)S(1)}, bf16[2,432,128]{2,1,0:T(8,128)(2,1)S(1)}, u32[]{:S(2)}, u32[]{:S(2)}) %collective-permute-start.40) | collective-permute-done | bytes 221216 | tf_op jit(solution)/shard_map/ppermute | solution.py:18
  90.9 0.5 collective-permute-start.41
  91.4 0.1 broadcast_select_fusion.1
  91.5 0.5 pad_maximum_fusion.1.field_ref
  92.0 0.4 collective-permute-done.39.refs_13_
  92.4 0.3 collective-permute-done.41.refs_15_
  92.7 3.0 %shard_map.100 = bf16[8,4,16,256]{3,2,1,0:T(8,128)(2,1)} custom-call(bf16[10,6,18,256]{3,2,1,0:T(8,128)(2,1)S(1)} %pad_maximum_fusion.1.field_ref, bf16[2,432,128]{2,1,0:T(8,128)(2,1)S(1)} %pad_maximum_fusion.3.refs_0_, bf16[2,432,128]{2,1,0:T(8,128)(2,1)S(1)} %copy-done.1, bf16[2,432,128]{2,1,0:T(8,128)(2,1)S(1)} %collective-permute-done.28.refs_2_, ...), custom_call_target="tpu_custom_call" | custom-call | flops 1811939328 | bytes 4063232 | tf_op jit(solution)/shard_map/pallas_call | solution.py:92
  (74 shorter events, 0.9 us)
Async XLA Ops:
  2.4 12.9 %collective-permute-start.3 = (bf16[3,864,128]{2,1,0:T(8,128)(2,1)S(1)}, bf16[3,864,128]{2,1,0:T(8,128)(2,1)S(1)}, u32[]{:S(2)}, u32[]{:S(2)}) collective-permute-start(bf16[3,864,128]{2,1,0:T(8,128)(2,1)S(1)} %get-tuple-element.13), channel_id=1, source_target_pairs={{0,1},{1,0},{2,3},{3,2},{4,5},{5,4},{6,7},{7,6},{8,9},{9,8},{10,11... | collective-permute-start | bytes 1990664 | tf_op jit(solution)/shard_map/ppermute | solution.py:18
  5.6 11.4 %collective-permute-start.24 = (bf16[3,864,128]{2,1,0:T(8,128)(2,1)}, bf16[3,864,128]{2,1,0:T(8,128)(2,1)S(1)}, u32[]{:S(2)}, u32[]{:S(2)}) collective-permute-start(bf16[3,864,128]{2,1,0:T(8,128)(2,1)} %get-tuple-element.16), channel_id=1, source_target_pairs={{0,1},{1,0},{2,3},{3,2},{4,5},{5,4},{6,7},{7,6},{8,9},{9,8},{10,11... | collective-permute-start | bytes 1990664 | tf_op jit(solution)/shard_map/ppermute | solution.py:18
  6.5 5.9 %collective-permute-start = (bf16[1,4,16,256]{3,2,1,0:T(8,128)(2,1)S(1)}, bf16[1,4,16,256]{3,2,1,0:T(8,128)(2,1)S(1)}, u32[]{:S(2)}, u32[]{:S(2)}) collective-permute-start(bf16[1,4,16,256]{3,2,1,0:T(8,128)(2,1)S(1)} %select_bitcast_fusion), channel_id=1, source_target_pairs={{0,16},{4,20},{8,24},{12,28},{16,0},{20,4},{24,8},{28,12},{1,17},{... | collective-permute-start | bytes 98312 | tf_op jit(solution)/shard_map/ppermute | solution.py:18
  12.4 5.2 %copy-start.5 = (s32[2,32]{1,0:T(2,128)S(1)}, s32[2,32]{1,0:T(2,128)}, u32[]{:S(2)}) copy-start(s32[2,32]{1,0:T(2,128)} %refs_3_.3) | copy-start | bytes 772
  13.3 4.6 %collective-permute-start.1 = (bf16[10,1,16,256]{3,2,1,0:T(8,128)(2,1)S(1)}, bf16[10,1,16,256]{3,2,1,0:T(8,128)(2,1)S(1)}, u32[]{:S(2)}, u32[]{:S(2)}) collective-permute-start(bf16[10,1,16,256]{3,2,1,0:T(8,128)(2,1)S(1)} %fusion.10), channel_id=1, source_target_pairs={{0,8},{4,12},{8,0},{12,4},{16,24},{20,28},{24,16},{28,20},{1,9},{5... | collective-permute-start | bytes 245768 | tf_op jit(solution)/shard_map/ppermute | solution.py:18
  15.4 10.8 %collective-permute-start.4 = (bf16[3,432,128]{2,1,0:T(8,128)(2,1)S(1)}, bf16[3,432,128]{2,1,0:T(8,128)(2,1)}, u32[]{:S(2)}, u32[]{:S(2)}) collective-permute-start(bf16[3,432,128]{2,1,0:T(8,128)(2,1)S(1)} %shard_map.94), channel_id=1, source_target_pairs={{0,2},{1,3},{2,0},{3,1},{4,6},{5,7},{6,4},{7,5},{8,10},{9,11},{10,... | collective-permute-start | bytes 995336 | tf_op jit(solution)/shard_map/ppermute | solution.py:18
  17.0 14.1 %collective-permute-start.25 = (bf16[3,432,128]{2,1,0:T(8,128)(2,1)S(1)}, bf16[3,432,128]{2,1,0:T(8,128)(2,1)}, u32[]{:S(2)}, u32[]{:S(2)}) collective-permute-start(bf16[3,432,128]{2,1,0:T(8,128)(2,1)S(1)} %shard_map.98), channel_id=1, source_target_pairs={{0,2},{1,3},{2,0},{3,1},{4,6},{5,7},{6,4},{7,5},{8,10},{9,11},{10,... | collective-permute-start | bytes 995336 | tf_op jit(solution)/shard_map/ppermute | solution.py:18
  28.2 9.6 %copy-start.4 = (bf16[1,1,8,4,16,256]{5,4,3,2,1,0:T(8,128)(2,1)S(1)}, bf16[1,1,8,4,16,256]{5,4,3,2,1,0:T(8,128)(2,1)}, u32[]{:S(2)}) copy-start(bf16[1,1,8,4,16,256]{5,4,3,2,1,0:T(8,128)(2,1)} %param.6) | copy-start | bytes 786436
  28.2 9.2 %collective-permute-start.5 = (bf16[1,432,128]{2,1,0:T(8,128)(2,1)S(1)}, bf16[1,432,128]{2,1,0:T(8,128)(2,1)S(1)}, u32[]{:S(2)}, u32[]{:S(2)}) collective-permute-start(bf16[1,432,128]{2,1,0:T(8,128)(2,1)S(1)} %bitcast.20), channel_id=1, source_target_pairs={{0,16},{4,20},{8,24},{12,28},{16,0},{20,4},{24,8},{28,12},{1,17},{... | collective-permute-start | bytes 331784 | tf_op jit(solution)/shard_map/ppermute | solution.py:18
  33.1 7.0 %collective-permute-start.26 = (bf16[1,432,128]{2,1,0:T(8,128)(2,1)S(1)}, bf16[1,432,128]{2,1,0:T(8,128)(2,1)S(1)}, u32[]{:S(2)}, u32[]{:S(2)}) collective-permute-start(bf16[1,432,128]{2,1,0:T(8,128)(2,1)S(1)} %bitcast.23), channel_id=1, source_target_pairs={{0,16},{4,20},{8,24},{12,28},{16,0},{20,4},{24,8},{28,12},{1,17},{... | collective-permute-start | bytes 331784 | tf_op jit(solution)/shard_map/ppermute | solution.py:18
  35.9 8.1 %collective-permute-start.42 = (bf16[2,432,128]{2,1,0:T(8,128)(2,1)S(1)}, bf16[2,432,128]{2,1,0:T(8,128)(2,1)S(1)}, u32[]{:S(2)}, u32[]{:S(2)}) collective-permute-start(bf16[2,432,128]{2,1,0:T(8,128)(2,1)S(1)} %pad_maximum_fusion.4), channel_id=1, source_target_pairs={{0,2},{1,3},{2,0},{3,1},{4,6},{5,7},{6,4},{7,5},{8,10},{9,11},{10,... | collective-permute-start | bytes 663560 | tf_op jit(solution)/shard_map/ppermute | solution.py:18
  37.5 6.5 %collective-permute-start.7 = (bf16[2,432,128]{2,1,0:T(8,128)(2,1)S(1)}, bf16[2,432,128]{2,1,0:T(8,128)(2,1)S(1)}, u32[]{:S(2)}, u32[]{:S(2)}) collective-permute-start(bf16[2,432,128]{2,1,0:T(8,128)(2,1)S(1)} %pad_maximum_fusion.2.refs_0_), channel_id=1, source_target_pairs={{0,8},{4,12},{8,0},{12,4},{16,24},{20,28},{24,16},{28,20},{1,9},{5... | collective-permute-start | bytes 663560 | tf_op jit(solution)/shard_map/ppermute | solution.py:18
  37.9 4.3 %collective-permute-start.2 = (bf16[10,6,1,256]{3,2,1,0:T(2,128)(2,1)S(1)}, bf16[10,6,1,256]{3,2,1,0:T(2,128)(2,1)S(1)}, u32[]{:S(2)}, u32[]{:S(2)}) collective-permute-start(bf16[10,6,1,256]{3,2,1,0:T(2,128)(2,1)S(1)} %broadcast_select_fusion.5), channel_id=1, source_target_pairs={{0,4},{4,0},{8,12},{12,8},{16,20},{20,16},{24,28},{28,24},{1,5},{5... | collective-permute-start | bytes 92168 | tf_op jit(solution)/shard_map/ppermute | solution.py:18
  39.5 5.9 %collective-permute-start.9 = (bf16[2,432,128]{2,1,0:T(8,128)(2,1)S(1)}, bf16[2,432,128]{2,1,0:T(8,128)(2,1)S(1)}, u32[]{:S(2)}, u32[]{:S(2)}) collective-permute-start(bf16[2,432,128]{2,1,0:T(8,128)(2,1)S(1)} %pad_maximum_fusion.2.refs_0_), channel_id=1, source_target_pairs={{0,4},{4,0},{8,12},{12,8},{16,20},{20,16},{24,28},{28,24},{1,5},{5... | collective-permute-start | bytes 663560 | tf_op jit(solution)/shard_map/ppermute | solution.py:18
  40.0 7.1 %collective-permute-start.13 = (bf16[2,432,128]{2,1,0:T(8,128)(2,1)S(1)}, bf16[2,432,128]{2,1,0:T(8,128)(2,1)S(1)}, u32[]{:S(2)}, u32[]{:S(2)}) collective-permute-start(bf16[2,432,128]{2,1,0:T(8,128)(2,1)S(1)} %pad_maximum_fusion.2.refs_0_), channel_id=1, source_target_pairs={{0,2},{1,3},{2,0},{3,1},{4,6},{5,7},{6,4},{7,5},{8,10},{9,11},{10,... | collective-permute-start | bytes 663560 | tf_op jit(solution)/shard_map/ppermute | solution.py:18
  42.2 5.0 %collective-permute-start.6 = (bf16[2,432,128]{2,1,0:T(8,128)(2,1)S(1)}, bf16[2,432,128]{2,1,0:T(8,128)(2,1)S(1)}, u32[]{:S(2)}, u32[]{:S(2)}) collective-permute-start(bf16[2,432,128]{2,1,0:T(8,128)(2,1)S(1)} %pad_maximum_fusion.2.refs_0_), channel_id=1, source_target_pairs={{0,1},{1,0},{2,3},{3,2},{4,5},{5,4},{6,7},{7,6},{8,9},{9,8},{10,11... | collective-permute-start | bytes 663560 | tf_op jit(solution)/shard_map/ppermute | solution.py:18
  44.0 4.2 %collective-permute-start.27 = (bf16[2,432,128]{2,1,0:T(8,128)(2,1)S(1)}, bf16[2,432,128]{2,1,0:T(8,128)(2,1)S(1)}, u32[]{:S(2)}, u32[]{:S(2)}) collective-permute-start(bf16[2,432,128]{2,1,0:T(8,128)(2,1)S(1)} %pad_maximum_fusion.3.refs_0_), channel_id=1, source_target_pairs={{0,1},{1,0},{2,3},{3,2},{4,5},{5,4},{6,7},{7,6},{8,9},{9,8},{10,11... | collective-permute-start | bytes 663560 | tf_op jit(solution)/shard_map/ppermute | solution.py:18
  44.0 7.8 %collective-permute-start.17 = (bf16[2,432,128]{2,1,0:T(8,128)(2,1)S(1)}, bf16[2,432,128]{2,1,0:T(8,128)(2,1)S(1)}, u32[]{:S(2)}, u32[]{:S(2)}) collective-permute-start(bf16[2,432,128]{2,1,0:T(8,128)(2,1)S(1)} %collective-permute-done.7.refs_2_), channel_id=1, source_target_pairs={{0,2},{1,3},{2,0},{3,1},{4,6},{5,7},{6,4},{7,5},{8,10},{9,11},{10,... | collective-permute-start | bytes 663560 | tf_op jit(solution)/shard_map/ppermute | solution.py:18
  45.5 8.1 %collective-permute-start.11 = (bf16[2,432,128]{2,1,0:T(8,128)(2,1)S(1)}, bf16[2,432,128]{2,1,0:T(8,128)(2,1)S(1)}, u32[]{:S(2)}, u32[]{:S(2)}) collective-permute-start(bf16[2,432,128]{2,1,0:T(8,128)(2,1)S(1)} %collective-permute-done.9.refs_4_), channel_id=1, source_target_pairs={{0,8},{4,12},{8,0},{12,4},{16,24},{20,28},{24,16},{28,20},{1,9},{5... | collective-permute-start | bytes 663560 | tf_op jit(solution)/shard_map/ppermute | solution.py:18
  47.2 8.4 %collective-permute-start.10 = (bf16[2,432,128]{2,1,0:T(8,128)(2,1)S(1)}, bf16[2,432,128]{2,1,0:T(8,128)(2,1)S(1)}, u32[]{:S(2)}, u32[]{:S(2)}) collective-permute-start(bf16[2,432,128]{2,1,0:T(8,128)(2,1)S(1)} %collective-permute-done.9.refs_4_), channel_id=1, source_target_pairs={{0,1},{1,0},{2,3},{3,2},{4,5},{5,4},{6,7},{7,6},{8,9},{9,8},{10,11... | collective-permute-start | bytes 663560 | tf_op jit(solution)/shard_map/ppermute | solution.py:18
  47.2 8.4 %collective-permute-start.15 = (bf16[2,432,128]{2,1,0:T(8,128)(2,1)S(1)}, bf16[2,432,128]{2,1,0:T(8,128)(2,1)S(1)}, u32[]{:S(2)}, u32[]{:S(2)}) collective-permute-start(bf16[2,432,128]{2,1,0:T(8,128)(2,1)S(1)} %collective-permute-done.13.refs_8_), channel_id=1, source_target_pairs={{0,4},{4,0},{8,12},{12,8},{16,20},{20,16},{24,28},{28,24},{1,5},{5... | collective-permute-start | bytes 663560 | tf_op jit(solution)/shard_map/ppermute | solution.py:18
  48.1 11.9 %copy-start = (bf16[2,432,128]{2,1,0:T(8,128)(2,1)}, bf16[2,432,128]{2,1,0:T(8,128)(2,1)S(1)}, u32[]{:S(2)}) copy-start(bf16[2,432,128]{2,1,0:T(8,128)(2,1)S(1)} %collective-permute-done.27.refs_1_) | copy-start | bytes 663556
  48.1 7.9 %collective-permute-start.14 = (bf16[2,432,128]{2,1,0:T(8,128)(2,1)S(1)}, bf16[2,432,128]{2,1,0:T(8,128)(2,1)S(1)}, u32[]{:S(2)}, u32[]{:S(2)}) collective-permute-start(bf16[2,432,128]{2,1,0:T(8,128)(2,1)S(1)} %collective-permute-done.13.refs_8_), channel_id=1, source_target_pairs={{0,1},{1,0},{2,3},{3,2},{4,5},{5,4},{6,7},{7,6},{8,9},{9,8},{10,11... | collective-permute-start | bytes 663560 | tf_op jit(solution)/shard_map/ppermute | solution.py:18
  51.8 7.9 %collective-permute-start.19 = (bf16[2,432,128]{2,1,0:T(8,128)(2,1)S(1)}, bf16[2,432,128]{2,1,0:T(8,128)(2,1)S(1)}, u32[]{:S(2)}, u32[]{:S(2)}) collective-permute-start(bf16[2,432,128]{2,1,0:T(8,128)(2,1)S(1)} %collective-permute-done.17.refs_12_), channel_id=1, source_target_pairs={{0,4},{4,0},{8,12},{12,8},{16,20},{20,16},{24,28},{28,24},{1,5},{5... | collective-permute-start | bytes 663560 | tf_op jit(solution)/shard_map/ppermute | solution.py:18
  53.6 6.5 %collective-permute-start.8 = (bf16[2,432,128]{2,1,0:T(8,128)(2,1)S(1)}, bf16[2,432,128]{2,1,0:T(8,128)(2,1)S(1)}, u32[]{:S(2)}, u32[]{:S(2)}) collective-permute-start(bf16[2,432,128]{2,1,0:T(8,128)(2,1)S(1)} %collective-permute-done.7.refs_2_), channel_id=1, source_target_pairs={{0,1},{1,0},{2,3},{3,2},{4,5},{5,4},{6,7},{7,6},{8,9},{9,8},{10,11... | collective-permute-start | bytes 663560 | tf_op jit(solution)/shard_map/ppermute | solution.py:18
  55.6 5.9 %collective-permute-start.18 = (bf16[2,432,128]{2,1,0:T(8,128)(2,1)S(1)}, bf16[2,432,128]{2,1,0:T(8,128)(2,1)S(1)}, u32[]{:S(2)}, u32[]{:S(2)}) collective-permute-start(bf16[2,432,128]{2,1,0:T(8,128)(2,1)S(1)} %collective-permute-done.17.refs_12_), channel_id=1, source_target_pairs={{0,1},{1,0},{2,3},{3,2},{4,5},{5,4},{6,7},{7,6},{8,9},{9,8},{10,11... | collective-permute-start | bytes 663560 | tf_op jit(solution)/shard_map/ppermute | solution.py:18
  55.6 7.0 %collective-permute-start.12 = (bf16[2,432,128]{2,1,0:T(8,128)(2,1)S(1)}, bf16[2,432,128]{2,1,0:T(8,128)(2,1)S(1)}, u32[]{:S(2)}, u32[]{:S(2)}) collective-permute-start(bf16[2,432,128]{2,1,0:T(8,128)(2,1)S(1)} %collective-permute-done.11.refs_6_), channel_id=1, source_target_pairs={{0,1},{1,0},{2,3},{3,2},{4,5},{5,4},{6,7},{7,6},{8,9},{9,8},{10,11... | collective-permute-start | bytes 663560 | tf_op jit(solution)/shard_map/ppermute | solution.py:18
  56.1 7.4 %collective-permute-start.16 = (bf16[2,432,128]{2,1,0:T(8,128)(2,1)S(1)}, bf16[2,432,128]{2,1,0:T(8,128)(2,1)S(1)}, u32[]{:S(2)}, u32[]{:S(2)}) collective-permute-start(bf16[2,432,128]{2,1,0:T(8,128)(2,1)S(1)} %collective-permute-done.15.refs_10_), channel_id=1, source_target_pairs={{0,1},{1,0},{2,3},{3,2},{4,5},{5,4},{6,7},{7,6},{8,9},{9,8},{10,11... | collective-permute-start | bytes 663560 | tf_op jit(solution)/shard_map/ppermute | solution.py:18
  59.8 3.7 %collective-permute-start.20 = (bf16[2,432,128]{2,1,0:T(8,128)(2,1)S(1)}, bf16[2,432,128]{2,1,0:T(8,128)(2,1)S(1)}, u32[]{:S(2)}, u32[]{:S(2)}) collective-permute-start(bf16[2,432,128]{2,1,0:T(8,128)(2,1)S(1)} %collective-permute-done.19.refs_14_), channel_id=1, source_target_pairs={{0,1},{1,0},{2,3},{3,2},{4,5},{5,4},{6,7},{7,6},{8,9},{9,8},{10,11... | collective-permute-start | bytes 663560 | tf_op jit(solution)/shard_map/ppermute | solution.py:18
  60.0 7.5 %slice-start = ((bf16[2,432,128]{2,1,0:T(8,128)(2,1)}), bf16[1,432,128]{2,1,0:T(8,128)(2,1)S(1)}, s32[]{:S(2)}) async-start(bf16[2,432,128]{2,1,0:T(8,128)(2,1)} %copy-done), calls=%async_computation | async-start | bytes 221184 | tf_op jit(solution)/shard_map/slice | solution.py:344
  60.1 15.1 %collective-permute-start.34 = (bf16[2,432,128]{2,1,0:T(8,128)(2,1)S(1)}, bf16[2,432,128]{2,1,0:T(8,128)(2,1)S(1)}, u32[]{:S(2)}, u32[]{:S(2)}) collective-permute-start(bf16[2,432,128]{2,1,0:T(8,128)(2,1)S(1)} %pad_maximum_fusion.3.refs_0_), channel_id=1, source_target_pairs={{0,2},{1,3},{2,0},{3,1},{4,6},{5,7},{6,4},{7,5},{8,10},{9,11},{10,... | collective-permute-start | bytes 663560 | tf_op jit(solution)/shard_map/ppermute | solution.py:18
  61.4 13.8 %collective-permute-start.30 = (bf16[2,432,128]{2,1,0:T(8,128)(2,1)S(1)}, bf16[2,432,128]{2,1,0:T(8,128)(2,1)S(1)}, u32[]{:S(2)}, u32[]{:S(2)}) collective-permute-start(bf16[2,432,128]{2,1,0:T(8,128)(2,1)S(1)} %pad_maximum_fusion.3.refs_0_), channel_id=1, source_target_pairs={{0,4},{4,0},{8,12},{12,8},{16,20},{20,16},{24,28},{28,24},{1,5},{5... | collective-permute-start | bytes 663560 | tf_op jit(solution)/shard_map/ppermute | solution.py:18
  62.6 11.4 %collective-permute-start.28 = (bf16[2,432,128]{2,1,0:T(8,128)(2,1)S(1)}, bf16[2,432,128]{2,1,0:T(8,128)(2,1)S(1)}, u32[]{:S(2)}, u32[]{:S(2)}) collective-permute-start(bf16[2,432,128]{2,1,0:T(8,128)(2,1)S(1)} %pad_maximum_fusion.3.refs_0_), channel_id=1, source_target_pairs={{0,8},{4,12},{8,0},{12,4},{16,24},{20,28},{24,16},{28,20},{1,9},{5... | collective-permute-start | bytes 663560 | tf_op jit(solution)/shard_map/ppermute | solution.py:18
  63.4 20.1 %collective-permute-start.43 = (bf16[2,864,128]{2,1,0:T(8,128)(2,1)S(1)}, bf16[2,864,128]{2,1,0:T(8,128)(2,1)S(1)}, u32[]{:S(2)}, u32[]{:S(2)}) collective-permute-start(bf16[2,864,128]{2,1,0:T(8,128)(2,1)S(1)} %maximum_select_fusion.1), channel_id=1, source_target_pairs={{0,1},{1,0},{2,3},{3,2},{4,5},{5,4},{6,7},{7,6},{8,9},{9,8},{10,11... | collective-permute-start | bytes 1327112 | tf_op jit(solution)/shard_map/ppermute | solution.py:18
  63.5 21.6 %copy-start.3 = (f32[1,2,864,256]{3,2,1,0:T(8,128)S(1)}, f32[1,2,864,256]{3,2,1,0:T(8,128)}, u32[]{:S(2)}) copy-start(f32[1,2,864,256]{3,2,1,0:T(8,128)} %refs_2_.3) | copy-start | bytes 5308420
  65.8 19.3 %copy-start.2 = (f32[1,2,864,256]{3,2,1,0:T(8,128)S(1)}, f32[1,2,864,256]{3,2,1,0:T(8,128)}, u32[]{:S(2)}) copy-start(f32[1,2,864,256]{3,2,1,0:T(8,128)} %refs_1_.3) | copy-start | bytes 5308420
  65.8 5.0 %collective-permute-start.21 = (bf16[1,4,16,256]{3,2,1,0:T(8,128)(2,1)S(1)}, bf16[1,4,16,256]{3,2,1,0:T(8,128)(2,1)S(1)}, u32[]{:S(2)}, u32[]{:S(2)}) collective-permute-start(bf16[1,4,16,256]{3,2,1,0:T(8,128)(2,1)S(1)} %slice_select_fusion), channel_id=1, source_target_pairs={{0,16},{4,20},{8,24},{12,28},{16,0},{20,4},{24,8},{28,12},{1,17},{... | collective-permute-start | bytes 98312 | tf_op jit(solution)/shard_map/ppermute | solution.py:18
  70.9 4.9 %collective-permute-start.22 = (bf16[10,1,16,256]{3,2,1,0:T(8,128)(2,1)S(1)}, bf16[10,1,16,256]{3,2,1,0:T(8,128)(2,1)S(1)}, u32[]{:S(2)}, u32[]{:S(2)}) collective-permute-start(bf16[10,1,16,256]{3,2,1,0:T(8,128)(2,1)S(1)} %fusion.9), channel_id=1, source_target_pairs={{0,8},{4,12},{8,0},{12,4},{16,24},{20,28},{24,16},{28,20},{1,9},{5... | collective-permute-start | bytes 245768 | tf_op jit(solution)/shard_map/ppermute | solution.py:18
  74.0 13.3 %collective-permute-start.38 = (bf16[2,432,128]{2,1,0:T(8,128)(2,1)S(1)}, bf16[2,432,128]{2,1,0:T(8,128)(2,1)S(1)}, u32[]{:S(2)}, u32[]{:S(2)}) collective-permute-start(bf16[2,432,128]{2,1,0:T(8,128)(2,1)S(1)} %collective-permute-done.28.refs_2_), channel_id=1, source_target_pairs={{0,2},{1,3},{2,0},{3,1},{4,6},{5,7},{6,4},{7,5},{8,10},{9,11},{10,... | collective-permute-start | bytes 663560 | tf_op jit(solution)/shard_map/ppermute | solution.py:18
  75.2 12.1 %collective-permute-start.29 = (bf16[2,432,128]{2,1,0:T(8,128)(2,1)S(1)}, bf16[2,432,128]{2,1,0:T(8,128)(2,1)S(1)}, u32[]{:S(2)}, u32[]{:S(2)}) collective-permute-start(bf16[2,432,128]{2,1,0:T(8,128)(2,1)S(1)} %collective-permute-done.28.refs_2_), channel_id=1, source_target_pairs={{0,1},{1,0},{2,3},{3,2},{4,5},{5,4},{6,7},{7,6},{8,9},{9,8},{10,11... | collective-permute-start | bytes 663560 | tf_op jit(solution)/shard_map/ppermute | solution.py:18
  75.2 7.8 %collective-permute-start.36 = (bf16[2,432,128]{2,1,0:T(8,128)(2,1)S(1)}, bf16[2,432,128]{2,1,0:T(8,128)(2,1)S(1)}, u32[]{:S(2)}, u32[]{:S(2)}) collective-permute-start(bf16[2,432,128]{2,1,0:T(8,128)(2,1)S(1)} %collective-permute-done.34.refs_8_), channel_id=1, source_target_pairs={{0,4},{4,0},{8,12},{12,8},{16,20},{20,16},{24,28},{28,24},{1,5},{5... | collective-permute-start | bytes 663560 | tf_op jit(solution)/shard_map/ppermute | solution.py:18
  75.8 7.5 %collective-permute-start.32 = (bf16[2,432,128]{2,1,0:T(8,128)(2,1)S(1)}, bf16[2,432,128]{2,1,0:T(8,128)(2,1)S(1)}, u32[]{:S(2)}, u32[]{:S(2)}) collective-permute-start(bf16[2,432,128]{2,1,0:T(8,128)(2,1)S(1)} %collective-permute-done.30.refs_4_), channel_id=1, source_target_pairs={{0,8},{4,12},{8,0},{12,4},{16,24},{20,28},{24,16},{28,20},{1,9},{5... | collective-permute-start | bytes 663560 | tf_op jit(solution)/shard_map/ppermute | solution.py:18
  83.1 4.8 %collective-permute-start.31 = (bf16[2,432,128]{2,1,0:T(8,128)(2,1)S(1)}, bf16[2,432,128]{2,1,0:T(8,128)(2,1)S(1)}, u32[]{:S(2)}, u32[]{:S(2)}) collective-permute-start(bf16[2,432,128]{2,1,0:T(8,128)(2,1)S(1)} %collective-permute-done.30.refs_4_), channel_id=1, source_target_pairs={{0,1},{1,0},{2,3},{3,2},{4,5},{5,4},{6,7},{7,6},{8,9},{9,8},{10,11... | collective-permute-start | bytes 663560 | tf_op jit(solution)/shard_map/ppermute | solution.py:18
  83.3 7.6 %collective-permute-start.40 = (bf16[2,432,128]{2,1,0:T(8,128)(2,1)S(1)}, bf16[2,432,128]{2,1,0:T(8,128)(2,1)S(1)}, u32[]{:S(2)}, u32[]{:S(2)}) collective-permute-start(bf16[2,432,128]{2,1,0:T(8,128)(2,1)S(1)} %collective-permute-done.36.refs_10_), channel_id=1, source_target_pairs={{0,8},{4,12},{8,0},{12,4},{16,24},{20,28},{24,16},{28,20},{1,9},{5... | collective-permute-start | bytes 663560 | tf_op jit(solution)/shard_map/ppermute | solution.py:18
  83.6 7.3 %collective-permute-start.23 = (bf16[10,6,1,256]{3,2,1,0:T(2,128)(2,1)S(1)}, bf16[10,6,1,256]{3,2,1,0:T(2,128)(2,1)S(1)}, u32[]{:S(2)}, u32[]{:S(2)}) collective-permute-start(bf16[10,6,1,256]{3,2,1,0:T(2,128)(2,1)S(1)} %broadcast_select_fusion.2), channel_id=1, source_target_pairs={{0,4},{4,0},{8,12},{12,8},{16,20},{20,16},{24,28},{28,24},{1,5},{5... | collective-permute-start | bytes 92168 | tf_op jit(solution)/shard_map/ppermute | solution.py:18
  85.1 7.6 %copy-start.1 = (bf16[2,432,128]{2,1,0:T(8,128)(2,1)S(1)}, bf16[2,432,128]{2,1,0:T(8,128)(2,1)}, u32[]{:S(2)}) copy-start(bf16[2,432,128]{2,1,0:T(8,128)(2,1)} %copy-done) | copy-start | bytes 663556
  87.3 4.7 %collective-permute-start.35 = (bf16[2,432,128]{2,1,0:T(8,128)(2,1)S(1)}, bf16[2,432,128]{2,1,0:T(8,128)(2,1)S(1)}, u32[]{:S(2)}, u32[]{:S(2)}) collective-permute-start(bf16[2,432,128]{2,1,0:T(8,128)(2,1)S(1)} %collective-permute-done.34.refs_8_), channel_id=1, source_target_pairs={{0,1},{1,0},{2,3},{3,2},{4,5},{5,4},{6,7},{7,6},{8,9},{9,8},{10,11... | collective-permute-start | bytes 663560 | tf_op jit(solution)/shard_map/ppermute | solution.py:18
  87.3 4.7 %collective-permute-start.37 = (bf16[2,432,128]{2,1,0:T(8,128)(2,1)S(1)}, bf16[2,432,128]{2,1,0:T(8,128)(2,1)S(1)}, u32[]{:S(2)}, u32[]{:S(2)}) collective-permute-start(bf16[2,432,128]{2,1,0:T(8,128)(2,1)S(1)} %collective-permute-done.36.refs_10_), channel_id=1, source_target_pairs={{0,1},{1,0},{2,3},{3,2},{4,5},{5,4},{6,7},{7,6},{8,9},{9,8},{10,11... | collective-permute-start | bytes 663560 | tf_op jit(solution)/shard_map/ppermute | solution.py:18
  87.8 4.2 %collective-permute-start.33 = (bf16[2,432,128]{2,1,0:T(8,128)(2,1)S(1)}, bf16[2,432,128]{2,1,0:T(8,128)(2,1)S(1)}, u32[]{:S(2)}, u32[]{:S(2)}) collective-permute-start(bf16[2,432,128]{2,1,0:T(8,128)(2,1)S(1)} %collective-permute-done.32.refs_6_), channel_id=1, source_target_pairs={{0,1},{1,0},{2,3},{3,2},{4,5},{5,4},{6,7},{7,6},{8,9},{9,8},{10,11... | collective-permute-start | bytes 663560 | tf_op jit(solution)/shard_map/ppermute | solution.py:18
  90.9 1.5 %collective-permute-start.39 = (bf16[2,432,128]{2,1,0:T(8,128)(2,1)S(1)}, bf16[2,432,128]{2,1,0:T(8,128)(2,1)S(1)}, u32[]{:S(2)}, u32[]{:S(2)}) collective-permute-start(bf16[2,432,128]{2,1,0:T(8,128)(2,1)S(1)} %collective-permute-done.38.refs_12_), channel_id=1, source_target_pairs={{0,1},{1,0},{2,3},{3,2},{4,5},{5,4},{6,7},{7,6},{8,9},{9,8},{10,11... | collective-permute-start | bytes 663560 | tf_op jit(solution)/shard_map/ppermute | solution.py:18
  90.9 1.8 %collective-permute-start.41 = (bf16[2,432,128]{2,1,0:T(8,128)(2,1)S(1)}, bf16[2,432,128]{2,1,0:T(8,128)(2,1)S(1)}, u32[]{:S(2)}, u32[]{:S(2)}) collective-permute-start(bf16[2,432,128]{2,1,0:T(8,128)(2,1)S(1)} %collective-permute-done.40.refs_14_), channel_id=1, source_target_pairs={{0,1},{1,0},{2,3},{3,2},{4,5},{5,4},{6,7},{7,6},{8,9},{9,8},{10,11... | collective-permute-start | bytes 663560 | tf_op jit(solution)/shard_map/ppermute | solution.py:18
where the time goes:
time: 96.1 us; the launch traced here: 95.7 us
  starting transfers between devices  39.3 us (41%)
  waiting for transfers between devices  34.6 us (36%)
  Pallas kernels  13.8 us (14%)
  other arithmetic  5.8 us (6%)
  local copies, waits for them, and re-layouts  1.21 us (1%)
    ppermute x44, starting transfers between devices, swap(): lax.ppermute(value, axis, [(source, source ^ stride) for source in range(...  39.3 us
    ppermute x44, waiting for transfers between devices, swap(): lax.ppermute(value, axis, [(source, source ^ stride) for source in range(...  34.6 us
    pallas_call x2, Pallas kernels, convolve(): pl.pallas_call(functools.partial(conv_kernel, places, span), out_shape=ja...  5.33 us
    pallas_call x2, Pallas kernels, split_state(): pl.pallas_call(functools.partial(split_kernel, index), out_shape=(shape,...  4.38 us
    pallas_call x2, Pallas kernels, updated(): pl.pallas_call(functools.partial(update_kernel, index), out_shape=(rounde...  3.92 us
    select_n x15, other arithmetic, pick(): return jnp.where(flag, one, other)  2.38 us
    select_n x1, other arithmetic, shards(): second_out = jnp.where(owned, second_new, moment_second[0])[None]  2.21 us
  transfers between devices with their start and end apart: 44, of which 14 were waited for; matrix products, arithmetic and copies ran while one was open for 7% of the time, Pallas kernels for 9%

commit v1 on v0

--- a/solution.py
+++ b/solution.py
@@ -195,18 +195,42 @@
     )(kept, came)
 
 
-def update_kernel(index, all_master, kept_ref, came_ref, *refs):
-    piece_ref, sum_ref, master_ref, sem = refs[-4:]
-    height, half = piece_ref.shape
-    _, row_pos, col_pos = place_of(kept_ref.shape[1] // height)
+def fetch_kernel(all_master, *refs):
+    master_ref, sem = refs[-2:]
+    _, height, half = master_ref.shape
+    _, row_pos, col_pos = place_of(all_master.shape[1] // height)
     rows = pl.ds(pl.multiple_of(row_pos * height, 8), height)
     columns = pl.ds(pl.multiple_of(col_pos * half, 128), half)
-    copy = pltpu.make_async_copy(all_master.at[index, rows, columns], master_ref, sem)
+    copy = pltpu.make_async_copy(all_master.at[:, rows, columns], master_ref, sem)
     copy.start()
+    copy.wait()
+
+
+def fetched(height, half, master, after):
+    shape = (master.shape[0], height, half)
+    return pl.pallas_call(
+        fetch_kernel,
+        out_shape=jax.ShapeDtypeStruct(shape, master.dtype),
+        in_specs=[pl.BlockSpec(memory_space=pltpu.HBM)]
+        + [pl.BlockSpec(memory_space=pl.ANY)] * len(after),
+        out_specs=pl.BlockSpec(memory_space=pltpu.VMEM),
+        scratch_shapes=[pltpu.SemaphoreType.DMA],
+        compiler_params=pltpu.CompilerParams(vmem_limit_bytes=2 * 2**20),
+        cost_estimate=pl.CostEstimate(
+            flops=0, bytes_accessed=8 * master.shape[0] * height * half, transcendentals=0
+        ),
+    )(pltpu.with_memory_space_constraint(master, pltpu.HBM), *after)
+
+
+def update_kernel(index, master_ref, kept_ref, came_ref, *refs):
+    piece_ref, sum_ref = refs[-2:]
+    height = piece_ref.shape[0]
+    row_pos = place_of(kept_ref.shape[1] // height)[1]
+    rows = pl.ds(pl.multiple_of(row_pos * height, 8), height)
     state = []
     for slot in range(3):
         total = kept_ref[slot, rows, :].astype(jnp.float32) + came_ref[slot, rows, :].astype(jnp.float32)
-        for crossed_ref in refs[:-4]:
+        for crossed_ref in refs[:-2]:
             total = total + crossed_ref[slot].astype(jnp.float32)
         state.append(total)
     grad, first, second = state
@@ -215,28 +239,26 @@
     corr_one = 1.0 - 0.9**10
     corr_two = 1.0 - 0.95**10
     sum_ref[...] = grad.astype(sum_ref.dtype)
-    ratio = first / corr_one / (jnp.sqrt(second / corr_two) + 1e-08)
-    copy.wait()
-    master = master_ref[...]
-    piece_ref[...] = (master - 0.004 * (ratio + 0.1 * master)).astype(piece_ref.dtype)
-
-
-def updated(index, height, master, kept, came, crossed):
+    master = master_ref[index]
+    update = first / corr_one / (jnp.sqrt(second / corr_two) + 1e-08) + 0.1 * master
+    piece_ref[...] = (master - 0.004 * update).astype(piece_ref.dtype)
+
+
+def updated(index, master, kept, came, crossed):
     vmem = pl.BlockSpec(memory_space=pltpu.VMEM)
-    half = kept.shape[2]
+    _, height, half = master.shape
     rounded = jax.ShapeDtypeStruct((height, half), jnp.bfloat16)
     size = height * half
     return pl.pallas_call(
         functools.partial(update_kernel, index),
         out_shape=(rounded, rounded),
-        in_specs=[pl.BlockSpec(memory_space=pltpu.HBM)] + [vmem] * (2 + len(crossed)),
+        in_specs=[vmem] * (3 + len(crossed)),
         out_specs=(vmem, vmem),
-        scratch_shapes=[pltpu.VMEM((height, half), jnp.float32), pltpu.SemaphoreType.DMA],
         compiler_params=pltpu.CompilerParams(vmem_limit_bytes=4 * 2**20),
         cost_estimate=pl.CostEstimate(
             flops=20 * size, bytes_accessed=30 * size, transcendentals=2 * size
         ),
-    )(pltpu.with_memory_space_constraint(master, pltpu.HBM), kept, came, *crossed)
+    )(master, kept, came, *crossed)
 
 
 def gathered(piece, row_shares, last):
@@ -279,6 +301,7 @@
 
 def shards(volumes, grad_parts, master_weights, moment_first, moment_second, owner):
     filter_count, rows_dev, channels = master_weights.shape
+    half = channels // 2
     panels_dev = rows_dev // PANEL_ROWS
     replicas = lax.axis_size("rep")
     row_shares = 2 if replicas % 4 == 0 and rows_dev % 16 == 0 else 1
@@ -295,16 +318,9 @@
     strides = (GY * GZ, GZ, 1)
     coords = (space_pos // (GY * GZ), space_pos // GZ % GY, space_pos % GZ)
 
-    split = []
+    split, crossing, after = [], [], []
     for index in range(filter_count):
-        kept, sent = split_state(
-            index,
-            owner,
-            grad_parts,
-            moment_first,
-            moment_second,
-            after=[split[-1][0]] if split else [],
-        )
+        kept, sent = split_state(index, owner, grad_parts, moment_first, moment_second, after=after)
         stride = replicas // 2
         while stride >= 2 * row_shares:
             kept, sent = [
@@ -314,14 +330,16 @@
                 for part in (kept, sent)
             ]
             stride //= 2
-        split.append((kept, swap(sent, "rep", 1)))
+        came = swap(sent, "rep", 1)
+        split.append((kept, came))
+        crossing.append([across(kept, came, height)] if row_shares == 2 else [])
+        after = crossing[-1] or [kept]
+    master = fetched(height, half, master_weights, after=[split[-1][0]])
     extended = extend_brick(volumes[0, 0], coords, strides, grid)
     sums, pieces = [], []
     for index, (kept, came) in enumerate(split):
-        crossed = []
-        if row_shares == 2:
-            crossed.append(swap(across(kept, came, height), "rep", 2))
-        piece, summed = updated(index, height, master_weights, kept, came, crossed)
+        crossed = [swap(sent, "rep", 2) for sent in crossing[index]]
+        piece, summed = updated(index, master, kept, came, crossed)
         pieces.append(piece)
         sums.append(summed)
 
@@ -340,7 +358,7 @@
     for index in range(filter_count):
         if index:
             hidden = extend_brick(hidden, coords, strides, grid)
-        arrays, places = gathered(pieces[index], row_shares, "yz"[index % 2])
+        arrays, places = gathered(pieces[index], row_shares, "yx"[index % 2])
         beside.append(arrays[1][0])
         hidden = convolve(hidden, arrays, places, span)
 

time: 96.1 us -> 97.5 us (1.015)
  waiting for transfers between devices: 34.6 us -> 41.6 us
  starting transfers between devices: 39.3 us -> 33.6 us
  other arithmetic: 5.8 us -> 7.03 us
  Pallas kernels: 13.8 us -> 12.6 us
    ppermute x44, waiting for transfers between devices: 34.6 us -> 41.6 us  [swap(): lax.ppermute(value, axis, [(source, source ^ stride) for source in range(...]
    ppermute x44, starting transfers between devices: 39.3 us -> 33.6 us  [swap(): lax.ppermute(value, axis, [(source, source ^ stride) for source in range(...]
    pallas_call x2, Pallas kernels: 3.92 us -> 1.64 us  [updated(): pl.pallas_call(functools.partial(update_kernel, index), out_shape=(rounde...]
    pallas_call x0 -> x1, Pallas kernels: none -> 1.04 us  [fetched(): pl.pallas_call(fetch_kernel, out_shape=jax.ShapeDtypeStruct(shape, master...]
  transfers between devices with their start and end apart: 44 -> 44, of which waited for: 14 -> 14; matrix products, arithmetic and copies ran while one was open for 7% -> 8% of each run, Pallas kernels for 9% -> 8%
where the time goes in v1:
time: 97.5 us; the launch traced here: 97.1 us
  waiting for transfers between devices  41.6 us (43%)
  starting transfers between devices  33.6 us (34%)
  Pallas kernels  12.6 us (13%)
  other arithmetic  7.03 us (7%)
  local copies, waits for them, and re-layouts  1.24 us (1%)
  between operations  1.08 us (1%)
    ppermute x44, waiting for transfers between devices, swap(): lax.ppermute(value, axis, [(source, source ^ stride) for source in range(...  41.6 us
    ppermute x44, starting transfers between devices, swap(): lax.ppermute(value, axis, [(source, source ^ stride) for source in range(...  33.6 us
    pallas_call x2, Pallas kernels, convolve(): pl.pallas_call(functools.partial(conv_kernel, places, span), out_shape=ja...  5.32 us
    pallas_call x2, Pallas kernels, split_state(): pl.pallas_call(functools.partial(split_kernel, index), out_shape=(shape,...  4.41 us
    select_n x15, other arithmetic, pick(): return jnp.where(flag, one, other)  2.81 us
    select_n x1, other arithmetic, shards(): second_out = jnp.where(owned, second_new, moment_second[0])[None]  2.22 us
  transfers between devices with their start and end apart: 44, of which 14 were waited for; matrix products, arithmetic and copies ran while one was open for 8% of the time, Pallas kernels for 8%

profile of v1, /device:TPU:0, one launch (start us, length us, event | category | flops | bytes accessed | tf_op | source)
XLA Modules:
  0.0 97.1 jit_solution(5470442162348067024)
XLA Ops:
  0.6 1.8 %shard_map.93 = (bf16[3,864,128]{2,1,0:T(8,128)(2,1)S(1)}, bf16[3,864,128]{2,1,0:T(8,128)(2,1)S(1)}) custom-call(bf16[1,2,864,256]{3,2,1,0:T(8,128)(2,1)} %refs_0_.3, f32[1,2,864,256]{3,2,1,0:T(8,128)} %refs_1_.3, f32[1,2,864,256]{3,2,1,0:T(8,128)} %refs_2_.3, s32[2,32]{1,0:T(2,128)} %refs_3_.3), custom_call_target="tpu_custom_call" | custom-call | flops 884736 | bytes 3538944 | tf_op jit(solution)/shard_map/pallas_call | solution.py:152
  2.5 0.6 collective-permute-start.3
  3.0 3.7 %collective-permute-start = (bf16[1,4,16,256]{3,2,1,0:T(8,128)(2,1)S(1)}, bf16[1,4,16,256]{3,2,1,0:T(8,128)(2,1)S(1)}, u32[]{:S(2)}, u32[]{:S(2)}) collective-permute-start(bf16[1,4,16,256]{3,2,1,0:T(8,128)(2,1)S(1)} %select_bitcast_fusion), channel_id=1, source_target_pairs={{0,16},{4,20},{8,24},{12,28},{16,0},{20,4},{24,8},{28,12},{1,17},{... | collective-permute-start | bytes 98312 | tf_op jit(solution)/shard_map/ppermute | solution.py:18
  6.7 0.1 shard_map.94.refs_4_
  6.8 1.6 %collective-permute-start.4 = (bf16[3,432,128]{2,1,0:T(8,128)(2,1)S(1)}, bf16[3,432,128]{2,1,0:T(8,128)(2,1)}, u32[]{:S(2)}, u32[]{:S(2)}) collective-permute-start(bf16[3,432,128]{2,1,0:T(8,128)(2,1)S(1)} %shard_map.94.refs_4_), channel_id=1, source_target_pairs={{0,2},{1,3},{2,0},{3,1},{4,6},{5,7},{6,4},{7,5},{8,10},{9,11},{10,... | collective-permute-start | bytes 995336 | tf_op jit(solution)/shard_map/ppermute | solution.py:18
  8.4 2.6 %shard_map.95 = (bf16[3,864,128]{2,1,0:T(8,128)(2,1)S(1)}, bf16[3,864,128]{2,1,0:T(8,128)(2,1)}) custom-call(bf16[1,2,864,256]{3,2,1,0:T(8,128)(2,1)} %refs_0_.3, f32[1,2,864,256]{3,2,1,0:T(8,128)} %refs_1_.3, f32[1,2,864,256]{3,2,1,0:T(8,128)} %refs_2_.3, s32[2,32]{1,0:T(2,128)} %refs_3_.3, bf16[3,432,128]{2,1,0:T(8,128)(2,1)S(1)} %shard_map.94.refs_4_), custom_call_target="tpu_custom_call" | custom-call | flops 884736 | bytes 3538944 | tf_op jit(solution)/shard_map/pallas_call | solution.py:152
  11.1 0.7 fusion.10
  11.8 1.6 %collective-permute-start.1 = (bf16[10,1,16,256]{3,2,1,0:T(8,128)(2,1)}, bf16[10,1,16,256]{3,2,1,0:T(8,128)(2,1)S(1)}, u32[]{:S(2)}, u32[]{:S(2)}) collective-permute-start(bf16[10,1,16,256]{3,2,1,0:T(8,128)(2,1)} %fusion.10), channel_id=1, source_target_pairs={{0,8},{4,12},{8,0},{12,4},{16,24},{20,28},{24,16},{28,20},{1,9},{5... | collective-permute-start | bytes 245768 | tf_op jit(solution)/shard_map/ppermute | solution.py:18
  13.3 1.0 %shard_map.96.master_ref = f32[2,432,128]{2,1,0:T(8,128)S(1)} custom-call(f32[2,864,256]{2,1,0:T(8,128)} %all_master.1, bf16[3,864,128]{2,1,0:T(8,128)(2,1)S(1)} %get-tuple-element.14.refs_0_.kept_ref), custom_call_target="tpu_custom_call" | custom-call | bytes 884736 | tf_op jit(solution)/shard_map/pallas_call | solution.py:211
  14.4 2.4 %collective-permute-done.4.refs_0_ = bf16[3,432,128]{2,1,0:T(8,128)(2,1)} collective-permute-done((bf16[3,432,128]{2,1,0:T(8,128)(2,1)S(1)}, bf16[3,432,128]{2,1,0:T(8,128)(2,1)}, u32[]{:S(2)}, u32[]{:S(2)}) %collective-permute-start.4) | collective-permute-done | bytes 331808 | tf_op jit(solution)/shard_map/ppermute | solution.py:18
  16.9 1.3 %shard_map.97 = (bf16[432,128]{1,0:T(8,128)(2,1)S(1)}, bf16[432,128]{1,0:T(8,128)(2,1)S(1)}) custom-call(f32[2,432,128]{2,1,0:T(8,128)S(1)} %shard_map.96.master_ref, bf16[3,864,128]{2,1,0:T(8,128)(2,1)S(1)} %get-tuple-element.12.kept_ref, bf16[3,864,128]{2,1,0:T(8,128)(2,1)S(1)} %collective-permute-done.3.came_ref, ...), custom_call_target="tpu_custom_call" | custom-call | flops 1105920 | bytes 1658880 | tf_op jit(solution)/shard_map/pallas_call | solution.py:252
  18.2 2.0 %collective-permute-start.5 = (bf16[1,432,128]{2,1,0:T(8,128)(2,1)S(1)}, bf16[1,432,128]{2,1,0:T(8,128)(2,1)S(1)}, u32[]{:S(2)}, u32[]{:S(2)}) collective-permute-start(bf16[1,432,128]{2,1,0:T(8,128)(2,1)S(1)} %bitcast.20), channel_id=1, source_target_pairs={{0,16},{4,20},{8,24},{12,28},{16,0},{20,4},{24,8},{28,12},{1,17},{... | collective-permute-start | bytes 331784 | tf_op jit(solution)/shard_map/ppermute | solution.py:18
  20.2 5.6 %collective-permute-done.5 = bf16[1,432,128]{2,1,0:T(8,128)(2,1)S(1)} collective-permute-done((bf16[1,432,128]{2,1,0:T(8,128)(2,1)S(1)}, bf16[1,432,128]{2,1,0:T(8,128)(2,1)S(1)}, u32[]{:S(2)}, u32[]{:S(2)}) %collective-permute-start.5) | collective-permute-done | bytes 110624 | tf_op jit(solution)/shard_map/ppermute | solution.py:18
  25.9 1.6 %collective-permute-start.9 = (bf16[2,432,128]{2,1,0:T(8,128)(2,1)S(1)}, bf16[2,432,128]{2,1,0:T(8,128)(2,1)S(1)}, u32[]{:S(2)}, u32[]{:S(2)}) collective-permute-start(bf16[2,432,128]{2,1,0:T(8,128)(2,1)S(1)} %pad_maximum_fusion.2.refs_0_), channel_id=1, source_target_pairs={{0,4},{4,0},{8,12},{12,8},{16,20},{20,16},{24,28},{28,24},{1,5},{5... | collective-permute-start | bytes 663560 | tf_op jit(solution)/shard_map/ppermute | solution.py:18
  27.5 0.7 broadcast_select_fusion.5
  28.2 0.5 collective-permute-start.2
  28.7 0.1 shard_map.99
  28.8 1.6 %collective-permute-start.25 = (bf16[3,432,128]{2,1,0:T(8,128)(2,1)S(1)}, bf16[3,432,128]{2,1,0:T(8,128)(2,1)S(1)}, u32[]{:S(2)}, u32[]{:S(2)}) collective-permute-start(bf16[3,432,128]{2,1,0:T(8,128)(2,1)S(1)} %shard_map.99), channel_id=1, source_target_pairs={{0,2},{1,3},{2,0},{3,1},{4,6},{5,7},{6,4},{7,5},{8,10},{9,11},{10,... | collective-permute-start | bytes 995336 | tf_op jit(solution)/shard_map/ppermute | solution.py:18
  30.5 0.1 broadcast_in_dim.29
  30.5 0.1 eq.41
  30.7 3.2 %collective-permute-done.2 = bf16[10,6,1,256]{3,2,1,0:T(2,128)(2,1)} collective-permute-done((bf16[10,6,1,256]{3,2,1,0:T(2,128)(2,1)}, bf16[10,6,1,256]{3,2,1,0:T(2,128)(2,1)}, u32[]{:S(2)}, u32[]{:S(2)}) %collective-permute-start.2) | collective-permute-done | bytes 30752 | tf_op jit(solution)/shard_map/ppermute | solution.py:18
  33.9 1.5 %collective-permute-start.13 = (bf16[2,432,128]{2,1,0:T(8,128)(2,1)S(1)}, bf16[2,432,128]{2,1,0:T(8,128)(2,1)S(1)}, u32[]{:S(2)}, u32[]{:S(2)}) collective-permute-start(bf16[2,432,128]{2,1,0:T(8,128)(2,1)S(1)} %pad_maximum_fusion.2.refs_0_), channel_id=1, source_target_pairs={{0,2},{1,3},{2,0},{3,1},{4,6},{5,7},{6,4},{7,5},{8,10},{9,11},{10,... | collective-permute-start | bytes 663560 | tf_op jit(solution)/shard_map/ppermute | solution.py:18
  35.4 0.6 collective-permute-start.17
  36.0 0.9 broadcast_select_fusion.4
  37.0 2.6 %collective-permute-done.25.refs_0_ = bf16[3,432,128]{2,1,0:T(8,128)(2,1)S(1)} collective-permute-done((bf16[3,432,128]{2,1,0:T(8,128)(2,1)S(1)}, bf16[3,432,128]{2,1,0:T(8,128)(2,1)S(1)}, u32[]{:S(2)}, u32[]{:S(2)}) %collective-permute-start.25) | collective-permute-done | bytes 331808 | tf_op jit(solution)/shard_map/ppermute | solution.py:18
  39.6 0.3 shard_map.100
  39.9 0.6 collective-permute-start.11
  40.6 3.7 %collective-permute-done.13.refs_8_ = bf16[2,432,128]{2,1,0:T(8,128)(2,1)S(1)} collective-permute-done((bf16[2,432,128]{2,1,0:T(8,128)(2,1)S(1)}, bf16[2,432,128]{2,1,0:T(8,128)(2,1)S(1)}, u32[]{:S(2)}, u32[]{:S(2)}) %collective-permute-start.13) | collective-permute-done | bytes 221216 | tf_op jit(solution)/shard_map/ppermute | solution.py:18
  44.3 1.5 %collective-permute-start.15 = (bf16[2,432,128]{2,1,0:T(8,128)(2,1)S(1)}, bf16[2,432,128]{2,1,0:T(8,128)(2,1)S(1)}, u32[]{:S(2)}, u32[]{:S(2)}) collective-permute-start(bf16[2,432,128]{2,1,0:T(8,128)(2,1)S(1)} %collective-permute-done.13.refs_8_), channel_id=1, source_target_pairs={{0,4},{4,0},{8,12},{12,8},{16,20},{20,16},{24,28},{28,24},{1,5},{5... | collective-permute-start | bytes 663560 | tf_op jit(solution)/shard_map/ppermute | solution.py:18
  45.8 0.9 collective-permute-done.17.refs_12_
  46.7 1.5 %collective-permute-start.19 = (bf16[2,432,128]{2,1,0:T(8,128)(2,1)S(1)}, bf16[2,432,128]{2,1,0:T(8,128)(2,1)S(1)}, u32[]{:S(2)}, u32[]{:S(2)}) collective-permute-start(bf16[2,432,128]{2,1,0:T(8,128)(2,1)S(1)} %collective-permute-done.17.refs_12_), channel_id=1, source_target_pairs={{0,4},{4,0},{8,12},{12,8},{16,20},{20,16},{24,28},{28,24},{1,5},{5... | collective-permute-start | bytes 663560 | tf_op jit(solution)/shard_map/ppermute | solution.py:18
  48.3 1.5 %collective-permute-start.42 = (bf16[2,432,128]{2,1,0:T(8,128)(2,1)S(1)}, bf16[2,432,128]{2,1,0:T(8,128)(2,1)S(1)}, u32[]{:S(2)}, u32[]{:S(2)}) collective-permute-start(bf16[2,432,128]{2,1,0:T(8,128)(2,1)S(1)} %pad_maximum_fusion.4), channel_id=1, source_target_pairs={{0,2},{1,3},{2,0},{3,1},{4,6},{5,7},{6,4},{7,5},{8,10},{9,11},{10,... | collective-permute-start | bytes 663560 | tf_op jit(solution)/shard_map/ppermute | solution.py:18
  49.8 1.2 %pad_maximum_fusion.field_ref = bf16[10,6,18,256]{3,2,1,0:T(8,128)(2,1)S(1)} fusion(bf16[10,6,1,256]{3,2,1,0:T(2,128)(2,1)S(1)} %get-tuple-element.29, bf16[10,1,16,256]{3,2,1,0:T(8,128)(2,1)S(1)} %get-tuple-element.25, bf16[1,4,16,256]{3,2,1,0:T(8,128)(2,1)} %copy-done.8, bf16[8,4,16,256]{3,2,1,0:T(8,128)(2,1)S(1)} %bitcast.28, ...), kind=kLoop, calls=%fused_computation.8 | loop fusion | flops 3870720 | bytes 1105920 | tf_op jit(solution)/shard_map/concatenate | solution.py:48
  51.0 3.4 %collective-permute-start.26 = (bf16[1,432,128]{2,1,0:T(8,128)(2,1)S(1)}, bf16[1,432,128]{2,1,0:T(8,128)(2,1)S(1)}, u32[]{:S(2)}, u32[]{:S(2)}) collective-permute-start(bf16[1,432,128]{2,1,0:T(8,128)(2,1)S(1)} %bitcast.23), channel_id=1, source_target_pairs={{0,16},{4,20},{8,24},{12,28},{16,0},{20,4},{24,8},{28,12},{1,17},{... | collective-permute-start | bytes 331784 | tf_op jit(solution)/shard_map/ppermute | solution.py:18
  54.6 0.5 collective-permute-start.18
  55.1 0.1 collective-permute-start.12
  55.2 3.1 %collective-permute-done.26 = bf16[1,432,128]{2,1,0:T(8,128)(2,1)S(1)} collective-permute-done((bf16[1,432,128]{2,1,0:T(8,128)(2,1)S(1)}, bf16[1,432,128]{2,1,0:T(8,128)(2,1)S(1)}, u32[]{:S(2)}, u32[]{:S(2)}) %collective-permute-start.26) | collective-permute-done | bytes 110624 | tf_op jit(solution)/shard_map/ppermute | solution.py:18
  58.3 0.5 collective-permute-start.20
  58.8 0.1 fusion.11
  59.1 0.6 collective-permute-done.16.refs_11_
  59.7 0.4 collective-permute-start.30
  60.2 0.5 collective-permute-start.34
  60.7 2.3 %shard_map.98 = bf16[8,4,16,256]{3,2,1,0:T(8,128)(2,1)S(1)} custom-call(bf16[10,6,18,256]{3,2,1,0:T(8,128)(2,1)S(1)} %pad_maximum_fusion.field_ref, bf16[2,432,128]{2,1,0:T(8,128)(2,1)S(1)} %pad_maximum_fusion.2.refs_0_, bf16[2,432,128]{2,1,0:T(8,128)(2,1)S(1)} %collective-permute-done.6.refs_1_, bf16[2,432,128]{2,1,0:T(8,128)(2,1)S(1)} %collective-permute-done.7.refs_2_, ...), custom_call_target="tpu_custom_call" | custom-call | flops 1811939328 | bytes 4063232 | tf_op jit(solution)/shard_map/pallas_call | solution.py:92
  63.0 2.2 %collective-permute-start.21 = (bf16[1,4,16,256]{3,2,1,0:T(8,128)(2,1)S(1)}, bf16[1,4,16,256]{3,2,1,0:T(8,128)(2,1)S(1)}, u32[]{:S(2)}, u32[]{:S(2)}) collective-permute-start(bf16[1,4,16,256]{3,2,1,0:T(8,128)(2,1)S(1)} %slice_select_fusion), channel_id=1, source_target_pairs={{0,16},{4,20},{8,24},{12,28},{16,0},{20,4},{24,8},{28,12},{1,17},{... | collective-permute-start | bytes 98312 | tf_op jit(solution)/shard_map/ppermute | solution.py:18
  65.2 0.1 maximum_select_fusion.1
  65.4 1.8 %collective-permute-done.28.refs_2_ = bf16[2,432,128]{2,1,0:T(8,128)(2,1)S(1)} collective-permute-done((bf16[2,432,128]{2,1,0:T(8,128)(2,1)S(1)}, bf16[2,432,128]{2,1,0:T(8,128)(2,1)S(1)}, u32[]{:S(2)}, u32[]{:S(2)}) %collective-permute-start.28) | collective-permute-done | bytes 221216 | tf_op jit(solution)/shard_map/ppermute | solution.py:18
  67.2 1.4 %collective-permute-start.32 = (bf16[2,432,128]{2,1,0:T(8,128)(2,1)S(1)}, bf16[2,432,128]{2,1,0:T(8,128)(2,1)S(1)}, u32[]{:S(2)}, u32[]{:S(2)}) collective-permute-start(bf16[2,432,128]{2,1,0:T(8,128)(2,1)S(1)} %collective-permute-done.30.refs_4_), channel_id=1, source_target_pairs={{0,8},{4,12},{8,0},{12,4},{16,24},{20,28},{24,16},{28,20},{1,9},{5... | collective-permute-start | bytes 663560 | tf_op jit(solution)/shard_map/ppermute | solution.py:18
  68.7 0.9 collective-permute-start.22
  69.6 7.2 %collective-permute-done.22 = bf16[10,1,16,256]{3,2,1,0:T(8,128)(2,1)S(1)} collective-permute-done((bf16[10,1,16,256]{3,2,1,0:T(8,128)(2,1)S(1)}, bf16[10,1,16,256]{3,2,1,0:T(8,128)(2,1)S(1)}, u32[]{:S(2)}, u32[]{:S(2)}) %collective-permute-start.22) | collective-permute-done | bytes 81952 | tf_op jit(solution)/shard_map/ppermute | solution.py:18
  76.8 0.1 broadcast_select_fusion.2
  76.9 0.1 collective-permute-start.23
  77.1 1.0 %copy.10 = f32[1,2,216,256]{3,1,2,0:T(2,128)} copy(f32[1,2,216,256]{3,2,1,0:T(8,128)S(1)} %convert_bitcast_fusion) | data formatting | bytes 884736
  78.1 3.1 %collective-permute-done.23 = bf16[10,6,1,256]{3,2,1,0:T(2,128)(2,1)S(1)} collective-permute-done((bf16[10,6,1,256]{3,2,1,0:T(2,128)(2,1)S(1)}, bf16[10,6,1,256]{3,2,1,0:T(2,128)(2,1)S(1)}, u32[]{:S(2)}, u32[]{:S(2)}) %collective-permute-start.23) | collective-permute-done | bytes 30752 | tf_op jit(solution)/shard_map/ppermute | solution.py:18
  81.2 0.1 collective-permute-start.38
  81.3 1.1 %collective-permute-start.36 = (bf16[2,432,128]{2,1,0:T(8,128)(2,1)S(1)}, bf16[2,432,128]{2,1,0:T(8,128)(2,1)S(1)}, u32[]{:S(2)}, u32[]{:S(2)}) collective-permute-start(bf16[2,432,128]{2,1,0:T(8,128)(2,1)S(1)} %collective-permute-done.34.refs_8_), channel_id=1, source_target_pairs={{0,4},{4,0},{8,12},{12,8},{16,20},{20,16},{24,28},{28,24},{1,5},{5... | collective-permute-start | bytes 663560 | tf_op jit(solution)/shard_map/ppermute | solution.py:18
  82.5 0.9 collective-permute-start.40
  83.3 0.1 broadcast_select_fusion.1
  83.5 0.5 pad_maximum_fusion.1.field_ref
  84.0 3.3 %collective-permute-done.36.refs_10_ = bf16[2,432,128]{2,1,0:T(8,128)(2,1)S(1)} collective-permute-done((bf16[2,432,128]{2,1,0:T(8,128)(2,1)S(1)}, bf16[2,432,128]{2,1,0:T(8,128)(2,1)S(1)}, u32[]{:S(2)}, u32[]{:S(2)}) %collective-permute-start.36) | collective-permute-done | bytes 221216 | tf_op jit(solution)/shard_map/ppermute | solution.py:18
  87.3 2.2 %collective-permute-done.38.refs_12_ = bf16[2,432,128]{2,1,0:T(8,128)(2,1)S(1)} collective-permute-done((bf16[2,432,128]{2,1,0:T(8,128)(2,1)S(1)}, bf16[2,432,128]{2,1,0:T(8,128)(2,1)S(1)}, u32[]{:S(2)}, u32[]{:S(2)}) %collective-permute-start.38) | collective-permute-done | bytes 221216 | tf_op jit(solution)/shard_map/ppermute | solution.py:18
  89.4 0.5 collective-permute-start.39
  90.0 1.9 %collective-permute-done.40.refs_14_ = bf16[2,432,128]{2,1,0:T(8,128)(2,1)S(1)} collective-permute-done((bf16[2,432,128]{2,1,0:T(8,128)(2,1)S(1)}, bf16[2,432,128]{2,1,0:T(8,128)(2,1)S(1)}, u32[]{:S(2)}, u32[]{:S(2)}) %collective-permute-start.40) | collective-permute-done | bytes 221216 | tf_op jit(solution)/shard_map/ppermute | solution.py:18
  91.8 2.2 %fusion.4 = (f32[1,2,864,256]{3,2,1,0:T(8,128)}, f32[1,2,864,256]{3,2,1,0:T(8,128)}) fusion(f32[1,2,864,256]{3,2,1,0:T(8,128)S(1)} %copy-done.1, pred[2,864]{1,0:T(4,128)(4,1)S(1)} %eq.41, bf16[1,2,864,128]{3,2,1,0:T(8,128)(2,1)S(1)} %fusion.11, bf16[1,2,864,128]{3,2,1,0:T(8,128)(2,1)S(1)} %bitcast.30, pred[]{:T(512)S(6)} %eq.38, ...), kind=kLoop, calls=%fused_computation.6 | loop fusion | flops 8404992 | bytes 7964353 | tf_op jit(solution)/shard_map/jit(_where)/select_n | solution.py:369
  94.1 3.0 %shard_map.101 = bf16[8,4,16,256]{3,2,1,0:T(8,128)(2,1)} custom-call(bf16[10,6,18,256]{3,2,1,0:T(8,128)(2,1)S(1)} %pad_maximum_fusion.1.field_ref, bf16[2,432,128]{2,1,0:T(8,128)(2,1)S(1)} %pad_maximum_fusion.3.refs_0_, bf16[2,432,128]{2,1,0:T(8,128)(2,1)S(1)} %collective-permute-done.27.refs_1_, bf16[2,432,128]{2,1,0:T(8,128)(2,1)S(1)} %collective-permute-done.28.refs_2_, ...), custom_call_target="tpu_custom_call" | custom-call | flops 1811939328 | bytes 4063232 | tf_op jit(solution)/shard_map/pallas_call | solution.py:92
  (84 shorter events, 1.1 us)
Async XLA Ops:
  0.6 2.4 %copy-start.2 = (bf16[1,1,8,4,16,256]{5,4,3,2,1,0:T(8,128)(2,1)S(1)}, bf16[1,1,8,4,16,256]{5,4,3,2,1,0:T(8,128)(2,1)}, u32[]{:S(2)}) copy-start(bf16[1,1,8,4,16,256]{5,4,3,2,1,0:T(8,128)(2,1)} %param.6) | copy-start | bytes 786436
  2.5 4.3 %collective-permute-start.3 = (bf16[3,864,128]{2,1,0:T(8,128)(2,1)S(1)}, bf16[3,864,128]{2,1,0:T(8,128)(2,1)S(1)}, u32[]{:S(2)}, u32[]{:S(2)}) collective-permute-start(bf16[3,864,128]{2,1,0:T(8,128)(2,1)S(1)} %get-tuple-element.13), channel_id=1, source_target_pairs={{0,1},{1,0},{2,3},{3,2},{4,5},{5,4},{6,7},{7,6},{8,9},{9,8},{10,11... | collective-permute-start | bytes 1990664 | tf_op jit(solution)/shard_map/ppermute | solution.py:18
  3.0 8.0 %collective-permute-start = (bf16[1,4,16,256]{3,2,1,0:T(8,128)(2,1)S(1)}, bf16[1,4,16,256]{3,2,1,0:T(8,128)(2,1)S(1)}, u32[]{:S(2)}, u32[]{:S(2)}) collective-permute-start(bf16[1,4,16,256]{3,2,1,0:T(8,128)(2,1)S(1)} %select_bitcast_fusion), channel_id=1, source_target_pairs={{0,16},{4,20},{8,24},{12,28},{16,0},{20,4},{24,8},{28,12},{1,17},{... | collective-permute-start | bytes 98312 | tf_op jit(solution)/shard_map/ppermute | solution.py:18
  6.8 10.1 %collective-permute-start.4 = (bf16[3,432,128]{2,1,0:T(8,128)(2,1)S(1)}, bf16[3,432,128]{2,1,0:T(8,128)(2,1)}, u32[]{:S(2)}, u32[]{:S(2)}) collective-permute-start(bf16[3,432,128]{2,1,0:T(8,128)(2,1)S(1)} %shard_map.94.refs_4_), channel_id=1, source_target_pairs={{0,2},{1,3},{2,0},{3,1},{4,6},{5,7},{6,4},{7,5},{8,10},{9,11},{10,... | collective-permute-start | bytes 995336 | tf_op jit(solution)/shard_map/ppermute | solution.py:18
  11.0 17.8 %collective-permute-start.24 = (bf16[3,864,128]{2,1,0:T(8,128)(2,1)}, bf16[3,864,128]{2,1,0:T(8,128)(2,1)S(1)}, u32[]{:S(2)}, u32[]{:S(2)}) collective-permute-start(bf16[3,864,128]{2,1,0:T(8,128)(2,1)} %get-tuple-element.16), channel_id=1, source_target_pairs={{0,1},{1,0},{2,3},{3,2},{4,5},{5,4},{6,7},{7,6},{8,9},{9,8},{10,11... | collective-permute-start | bytes 1990664 | tf_op jit(solution)/shard_map/ppermute | solution.py:18
  11.1 2.3 %copy-start.5 = (bf16[1,4,16,256]{3,2,1,0:T(8,128)(2,1)}, bf16[1,4,16,256]{3,2,1,0:T(8,128)(2,1)S(1)}, u32[]{:S(2)}) copy-start(bf16[1,4,16,256]{3,2,1,0:T(8,128)(2,1)S(1)} %get-tuple-element.32) | copy-start | bytes 98308
  11.1 2.3 %copy-start.8 = (bf16[1,4,16,256]{3,2,1,0:T(8,128)(2,1)}, bf16[1,4,16,256]{3,2,1,0:T(8,128)(2,1)S(1)}, u32[]{:S(2)}) copy-start(bf16[1,4,16,256]{3,2,1,0:T(8,128)(2,1)S(1)} %get-tuple-element.33) | copy-start | bytes 98308
  11.8 8.4 %collective-permute-start.1 = (bf16[10,1,16,256]{3,2,1,0:T(8,128)(2,1)}, bf16[10,1,16,256]{3,2,1,0:T(8,128)(2,1)S(1)}, u32[]{:S(2)}, u32[]{:S(2)}) collective-permute-start(bf16[10,1,16,256]{3,2,1,0:T(8,128)(2,1)} %fusion.10), channel_id=1, source_target_pairs={{0,8},{4,12},{8,0},{12,4},{16,24},{20,28},{24,16},{28,20},{1,9},{5... | collective-permute-start | bytes 245768 | tf_op jit(solution)/shard_map/ppermute | solution.py:18
  14.4 13.1 %copy-start.3 = (bf16[1,1,8,4,16,256]{5,4,3,2,1,0:T(8,128)(2,1)S(1)}, bf16[1,1,8,4,16,256]{5,4,3,2,1,0:T(8,128)(2,1)}, u32[]{:S(2)}) copy-start(bf16[1,1,8,4,16,256]{5,4,3,2,1,0:T(8,128)(2,1)} %param.6) | copy-start | bytes 786436
  14.4 13.1 %copy-start.6 = (bf16[1,4,16,256]{3,2,1,0:T(8,128)(2,1)S(1)}, bf16[1,4,16,256]{3,2,1,0:T(8,128)(2,1)}, u32[]{:S(2)}) copy-start(bf16[1,4,16,256]{3,2,1,0:T(8,128)(2,1)} %copy-done.5) | copy-start | bytes 98308
  14.4 13.1 %copy-start.9 = (bf16[1,4,16,256]{3,2,1,0:T(8,128)(2,1)S(1)}, bf16[1,4,16,256]{3,2,1,0:T(8,128)(2,1)}, u32[]{:S(2)}) copy-start(bf16[1,4,16,256]{3,2,1,0:T(8,128)(2,1)} %copy-done.8) | copy-start | bytes 98308
  18.2 12.2 %copy-start.10 = (s32[2,32]{1,0:T(2,128)S(1)}, s32[2,32]{1,0:T(2,128)}, u32[]{:S(2)}) copy-start(s32[2,32]{1,0:T(2,128)} %refs_3_.3) | copy-start | bytes 772
  18.2 7.6 %collective-permute-start.5 = (bf16[1,432,128]{2,1,0:T(8,128)(2,1)S(1)}, bf16[1,432,128]{2,1,0:T(8,128)(2,1)S(1)}, u32[]{:S(2)}, u32[]{:S(2)}) collective-permute-start(bf16[1,432,128]{2,1,0:T(8,128)(2,1)S(1)} %bitcast.20), channel_id=1, source_target_pairs={{0,16},{4,20},{8,24},{12,28},{16,0},{20,4},{24,8},{28,12},{1,17},{... | collective-permute-start | bytes 331784 | tf_op jit(solution)/shard_map/ppermute | solution.py:18
  25.8 9.6 %collective-permute-start.7 = (bf16[2,432,128]{2,1,0:T(8,128)(2,1)S(1)}, bf16[2,432,128]{2,1,0:T(8,128)(2,1)S(1)}, u32[]{:S(2)}, u32[]{:S(2)}) collective-permute-start(bf16[2,432,128]{2,1,0:T(8,128)(2,1)S(1)} %pad_maximum_fusion.2.refs_0_), channel_id=1, source_target_pairs={{0,8},{4,12},{8,0},{12,4},{16,24},{20,28},{24,16},{28,20},{1,9},{5... | collective-permute-start | bytes 663560 | tf_op jit(solution)/shard_map/ppermute | solution.py:18
  25.9 9.5 %collective-permute-start.9 = (bf16[2,432,128]{2,1,0:T(8,128)(2,1)S(1)}, bf16[2,432,128]{2,1,0:T(8,128)(2,1)S(1)}, u32[]{:S(2)}, u32[]{:S(2)}) collective-permute-start(bf16[2,432,128]{2,1,0:T(8,128)(2,1)S(1)} %pad_maximum_fusion.2.refs_0_), channel_id=1, source_target_pairs={{0,4},{4,0},{8,12},{12,8},{16,20},{20,16},{24,28},{28,24},{1,5},{5... | collective-permute-start | bytes 663560 | tf_op jit(solution)/shard_map/ppermute | solution.py:18
  28.2 5.7 %collective-permute-start.2 = (bf16[10,6,1,256]{3,2,1,0:T(2,128)(2,1)}, bf16[10,6,1,256]{3,2,1,0:T(2,128)(2,1)}, u32[]{:S(2)}, u32[]{:S(2)}) collective-permute-start(bf16[10,6,1,256]{3,2,1,0:T(2,128)(2,1)} %broadcast_select_fusion.5), channel_id=1, source_target_pairs={{0,4},{4,0},{8,12},{12,8},{16,20},{20,16},{24,28},{28,24},{1,5},{5... | collective-permute-start | bytes 92168 | tf_op jit(solution)/shard_map/ppermute | solution.py:18
  28.8 20.9 %copy-start.7 = (bf16[1,4,16,256]{3,2,1,0:T(8,128)(2,1)S(1)}, bf16[1,4,16,256]{3,2,1,0:T(8,128)(2,1)}, u32[]{:S(2)}) copy-start(bf16[1,4,16,256]{3,2,1,0:T(8,128)(2,1)} %copy-done.5) | copy-start | bytes 98308
  28.8 10.7 %collective-permute-start.25 = (bf16[3,432,128]{2,1,0:T(8,128)(2,1)S(1)}, bf16[3,432,128]{2,1,0:T(8,128)(2,1)S(1)}, u32[]{:S(2)}, u32[]{:S(2)}) collective-permute-start(bf16[3,432,128]{2,1,0:T(8,128)(2,1)S(1)} %shard_map.99), channel_id=1, source_target_pairs={{0,2},{1,3},{2,0},{3,1},{4,6},{5,7},{6,4},{7,5},{8,10},{9,11},{10,... | collective-permute-start | bytes 995336 | tf_op jit(solution)/shard_map/ppermute | solution.py:18
  30.6 19.1 %copy-start.4 = (bf16[1,1,8,4,16,256]{5,4,3,2,1,0:T(8,128)(2,1)S(1)}, bf16[1,1,8,4,16,256]{5,4,3,2,1,0:T(8,128)(2,1)}, u32[]{:S(2)}) copy-start(bf16[1,1,8,4,16,256]{5,4,3,2,1,0:T(8,128)(2,1)} %param.6) | copy-start | bytes 786436
  30.6 9.3 %collective-permute-start.6 = (bf16[2,432,128]{2,1,0:T(8,128)(2,1)S(1)}, bf16[2,432,128]{2,1,0:T(8,128)(2,1)S(1)}, u32[]{:S(2)}, u32[]{:S(2)}) collective-permute-start(bf16[2,432,128]{2,1,0:T(8,128)(2,1)S(1)} %pad_maximum_fusion.2.refs_0_), channel_id=1, source_target_pairs={{0,1},{1,0},{2,3},{3,2},{4,5},{5,4},{6,7},{7,6},{8,9},{9,8},{10,11... | collective-permute-start | bytes 663560 | tf_op jit(solution)/shard_map/ppermute | solution.py:18
  33.9 10.4 %collective-permute-start.13 = (bf16[2,432,128]{2,1,0:T(8,128)(2,1)S(1)}, bf16[2,432,128]{2,1,0:T(8,128)(2,1)S(1)}, u32[]{:S(2)}, u32[]{:S(2)}) collective-permute-start(bf16[2,432,128]{2,1,0:T(8,128)(2,1)S(1)} %pad_maximum_fusion.2.refs_0_), channel_id=1, source_target_pairs={{0,2},{1,3},{2,0},{3,1},{4,6},{5,7},{6,4},{7,5},{8,10},{9,11},{10,... | collective-permute-start | bytes 663560 | tf_op jit(solution)/shard_map/ppermute | solution.py:18
  35.4 12.8 %collective-permute-start.8 = (bf16[2,432,128]{2,1,0:T(8,128)(2,1)S(1)}, bf16[2,432,128]{2,1,0:T(8,128)(2,1)S(1)}, u32[]{:S(2)}, u32[]{:S(2)}) collective-permute-start(bf16[2,432,128]{2,1,0:T(8,128)(2,1)S(1)} %collective-permute-done.7.refs_2_), channel_id=1, source_target_pairs={{0,1},{1,0},{2,3},{3,2},{4,5},{5,4},{6,7},{7,6},{8,9},{9,8},{10,11... | collective-permute-start | bytes 663560 | tf_op jit(solution)/shard_map/ppermute | solution.py:18
  35.4 11.3 %collective-permute-start.17 = (bf16[2,432,128]{2,1,0:T(8,128)(2,1)S(1)}, bf16[2,432,128]{2,1,0:T(8,128)(2,1)S(1)}, u32[]{:S(2)}, u32[]{:S(2)}) collective-permute-start(bf16[2,432,128]{2,1,0:T(8,128)(2,1)S(1)} %collective-permute-done.7.refs_2_), channel_id=1, source_target_pairs={{0,2},{1,3},{2,0},{3,1},{4,6},{5,7},{6,4},{7,5},{8,10},{9,11},{10,... | collective-permute-start | bytes 663560 | tf_op jit(solution)/shard_map/ppermute | solution.py:18
  39.6 11.5 %collective-permute-start.10 = (bf16[2,432,128]{2,1,0:T(8,128)(2,1)S(1)}, bf16[2,432,128]{2,1,0:T(8,128)(2,1)S(1)}, u32[]{:S(2)}, u32[]{:S(2)}) collective-permute-start(bf16[2,432,128]{2,1,0:T(8,128)(2,1)S(1)} %collective-permute-done.9.refs_4_), channel_id=1, source_target_pairs={{0,1},{1,0},{2,3},{3,2},{4,5},{5,4},{6,7},{7,6},{8,9},{9,8},{10,11... | collective-permute-start | bytes 663560 | tf_op jit(solution)/shard_map/ppermute | solution.py:18
  39.9 14.6 %collective-permute-start.11 = (bf16[2,432,128]{2,1,0:T(8,128)(2,1)S(1)}, bf16[2,432,128]{2,1,0:T(8,128)(2,1)S(1)}, u32[]{:S(2)}, u32[]{:S(2)}) collective-permute-start(bf16[2,432,128]{2,1,0:T(8,128)(2,1)S(1)} %collective-permute-done.9.refs_4_), channel_id=1, source_target_pairs={{0,8},{4,12},{8,0},{12,4},{16,24},{20,28},{24,16},{28,20},{1,9},{5... | collective-permute-start | bytes 663560 | tf_op jit(solution)/shard_map/ppermute | solution.py:18
  44.3 10.3 %collective-permute-start.15 = (bf16[2,432,128]{2,1,0:T(8,128)(2,1)S(1)}, bf16[2,432,128]{2,1,0:T(8,128)(2,1)S(1)}, u32[]{:S(2)}, u32[]{:S(2)}) collective-permute-start(bf16[2,432,128]{2,1,0:T(8,128)(2,1)S(1)} %collective-permute-done.13.refs_8_), channel_id=1, source_target_pairs={{0,4},{4,0},{8,12},{12,8},{16,20},{20,16},{24,28},{28,24},{1,5},{5... | collective-permute-start | bytes 663560 | tf_op jit(solution)/shard_map/ppermute | solution.py:18
  46.7 8.4 %collective-permute-start.19 = (bf16[2,432,128]{2,1,0:T(8,128)(2,1)S(1)}, bf16[2,432,128]{2,1,0:T(8,128)(2,1)S(1)}, u32[]{:S(2)}, u32[]{:S(2)}) collective-permute-start(bf16[2,432,128]{2,1,0:T(8,128)(2,1)S(1)} %collective-permute-done.17.refs_12_), channel_id=1, source_target_pairs={{0,4},{4,0},{8,12},{12,8},{16,20},{20,16},{24,28},{28,24},{1,5},{5... | collective-permute-start | bytes 663560 | tf_op jit(solution)/shard_map/ppermute | solution.py:18
  48.3 10.0 %collective-permute-start.42 = (bf16[2,432,128]{2,1,0:T(8,128)(2,1)S(1)}, bf16[2,432,128]{2,1,0:T(8,128)(2,1)S(1)}, u32[]{:S(2)}, u32[]{:S(2)}) collective-permute-start(bf16[2,432,128]{2,1,0:T(8,128)(2,1)S(1)} %pad_maximum_fusion.4), channel_id=1, source_target_pairs={{0,2},{1,3},{2,0},{3,1},{4,6},{5,7},{6,4},{7,5},{8,10},{9,11},{10,... | collective-permute-start | bytes 663560 | tf_op jit(solution)/shard_map/ppermute | solution.py:18
  51.0 7.2 %collective-permute-start.26 = (bf16[1,432,128]{2,1,0:T(8,128)(2,1)S(1)}, bf16[1,432,128]{2,1,0:T(8,128)(2,1)S(1)}, u32[]{:S(2)}, u32[]{:S(2)}) collective-permute-start(bf16[1,432,128]{2,1,0:T(8,128)(2,1)S(1)} %bitcast.23), channel_id=1, source_target_pairs={{0,16},{4,20},{8,24},{12,28},{16,0},{20,4},{24,8},{28,12},{1,17},{... | collective-permute-start | bytes 331784 | tf_op jit(solution)/shard_map/ppermute | solution.py:18
  54.5 4.4 %collective-permute-start.14 = (bf16[2,432,128]{2,1,0:T(8,128)(2,1)S(1)}, bf16[2,432,128]{2,1,0:T(8,128)(2,1)S(1)}, u32[]{:S(2)}, u32[]{:S(2)}) collective-permute-start(bf16[2,432,128]{2,1,0:T(8,128)(2,1)S(1)} %collective-permute-done.13.refs_8_), channel_id=1, source_target_pairs={{0,1},{1,0},{2,3},{3,2},{4,5},{5,4},{6,7},{7,6},{8,9},{9,8},{10,11... | collective-permute-start | bytes 663560 | tf_op jit(solution)/shard_map/ppermute | solution.py:18
  54.6 5.6 %collective-permute-start.18 = (bf16[2,432,128]{2,1,0:T(8,128)(2,1)S(1)}, bf16[2,432,128]{2,1,0:T(8,128)(2,1)S(1)}, u32[]{:S(2)}, u32[]{:S(2)}) collective-permute-start(bf16[2,432,128]{2,1,0:T(8,128)(2,1)S(1)} %collective-permute-done.17.refs_12_), channel_id=1, source_target_pairs={{0,1},{1,0},{2,3},{3,2},{4,5},{5,4},{6,7},{7,6},{8,9},{9,8},{10,11... | collective-permute-start | bytes 663560 | tf_op jit(solution)/shard_map/ppermute | solution.py:18
  55.1 3.9 %collective-permute-start.12 = (bf16[2,432,128]{2,1,0:T(8,128)(2,1)S(1)}, bf16[2,432,128]{2,1,0:T(8,128)(2,1)S(1)}, u32[]{:S(2)}, u32[]{:S(2)}) collective-permute-start(bf16[2,432,128]{2,1,0:T(8,128)(2,1)S(1)} %collective-permute-done.11.refs_6_), channel_id=1, source_target_pairs={{0,1},{1,0},{2,3},{3,2},{4,5},{5,4},{6,7},{7,6},{8,9},{9,8},{10,11... | collective-permute-start | bytes 663560 | tf_op jit(solution)/shard_map/ppermute | solution.py:18
  58.3 1.5 %collective-permute-start.16 = (bf16[2,432,128]{2,1,0:T(8,128)(2,1)S(1)}, bf16[2,432,128]{2,1,0:T(8,128)(2,1)S(1)}, u32[]{:S(2)}, u32[]{:S(2)}) collective-permute-start(bf16[2,432,128]{2,1,0:T(8,128)(2,1)S(1)} %collective-permute-done.15.refs_10_), channel_id=1, source_target_pairs={{0,1},{1,0},{2,3},{3,2},{4,5},{5,4},{6,7},{7,6},{8,9},{9,8},{10,11... | collective-permute-start | bytes 663560 | tf_op jit(solution)/shard_map/ppermute | solution.py:18
  58.3 2.4 %collective-permute-start.20 = (bf16[2,432,128]{2,1,0:T(8,128)(2,1)S(1)}, bf16[2,432,128]{2,1,0:T(8,128)(2,1)S(1)}, u32[]{:S(2)}, u32[]{:S(2)}) collective-permute-start(bf16[2,432,128]{2,1,0:T(8,128)(2,1)S(1)} %collective-permute-done.19.refs_14_), channel_id=1, source_target_pairs={{0,1},{1,0},{2,3},{3,2},{4,5},{5,4},{6,7},{7,6},{8,9},{9,8},{10,11... | collective-permute-start | bytes 663560 | tf_op jit(solution)/shard_map/ppermute | solution.py:18
  58.9 6.4 %collective-permute-start.27 = (bf16[2,432,128]{2,1,0:T(8,128)(2,1)S(1)}, bf16[2,432,128]{2,1,0:T(8,128)(2,1)S(1)}, u32[]{:S(2)}, u32[]{:S(2)}) collective-permute-start(bf16[2,432,128]{2,1,0:T(8,128)(2,1)S(1)} %pad_maximum_fusion.3.refs_0_), channel_id=1, source_target_pairs={{0,1},{1,0},{2,3},{3,2},{4,5},{5,4},{6,7},{7,6},{8,9},{9,8},{10,11... | collective-permute-start | bytes 663560 | tf_op jit(solution)/shard_map/ppermute | solution.py:18
  59.0 8.2 %collective-permute-start.28 = (bf16[2,432,128]{2,1,0:T(8,128)(2,1)S(1)}, bf16[2,432,128]{2,1,0:T(8,128)(2,1)S(1)}, u32[]{:S(2)}, u32[]{:S(2)}) collective-permute-start(bf16[2,432,128]{2,1,0:T(8,128)(2,1)S(1)} %pad_maximum_fusion.3.refs_0_), channel_id=1, source_target_pairs={{0,8},{4,12},{8,0},{12,4},{16,24},{20,28},{24,16},{28,20},{1,9},{5... | collective-permute-start | bytes 663560 | tf_op jit(solution)/shard_map/ppermute | solution.py:18
  59.7 7.5 %collective-permute-start.30 = (bf16[2,432,128]{2,1,0:T(8,128)(2,1)S(1)}, bf16[2,432,128]{2,1,0:T(8,128)(2,1)S(1)}, u32[]{:S(2)}, u32[]{:S(2)}) collective-permute-start(bf16[2,432,128]{2,1,0:T(8,128)(2,1)S(1)} %pad_maximum_fusion.3.refs_0_), channel_id=1, source_target_pairs={{0,4},{4,0},{8,12},{12,8},{16,20},{20,16},{24,28},{28,24},{1,5},{5... | collective-permute-start | bytes 663560 | tf_op jit(solution)/shard_map/ppermute | solution.py:18
  60.2 18.0 %collective-permute-start.34 = (bf16[2,432,128]{2,1,0:T(8,128)(2,1)S(1)}, bf16[2,432,128]{2,1,0:T(8,128)(2,1)S(1)}, u32[]{:S(2)}, u32[]{:S(2)}) collective-permute-start(bf16[2,432,128]{2,1,0:T(8,128)(2,1)S(1)} %pad_maximum_fusion.3.refs_0_), channel_id=1, source_target_pairs={{0,2},{1,3},{2,0},{3,1},{4,6},{5,7},{6,4},{7,5},{8,10},{9,11},{10,... | collective-permute-start | bytes 663560 | tf_op jit(solution)/shard_map/ppermute | solution.py:18
  63.0 5.6 %collective-permute-start.21 = (bf16[1,4,16,256]{3,2,1,0:T(8,128)(2,1)S(1)}, bf16[1,4,16,256]{3,2,1,0:T(8,128)(2,1)S(1)}, u32[]{:S(2)}, u32[]{:S(2)}) collective-permute-start(bf16[1,4,16,256]{3,2,1,0:T(8,128)(2,1)S(1)} %slice_select_fusion), channel_id=1, source_target_pairs={{0,16},{4,20},{8,24},{12,28},{16,0},{20,4},{24,8},{28,12},{1,17},{... | collective-permute-start | bytes 98312 | tf_op jit(solution)/shard_map/ppermute | solution.py:18
  65.3 24.1 %collective-permute-start.43 = (bf16[2,864,128]{2,1,0:T(8,128)(2,1)S(1)}, bf16[2,864,128]{2,1,0:T(8,128)(2,1)S(1)}, u32[]{:S(2)}, u32[]{:S(2)}) collective-permute-start(bf16[2,864,128]{2,1,0:T(8,128)(2,1)S(1)} %maximum_select_fusion.1), channel_id=1, source_target_pairs={{0,1},{1,0},{2,3},{3,2},{4,5},{5,4},{6,7},{7,6},{8,9},{9,8},{10,11... | collective-permute-start | bytes 1327112 | tf_op jit(solution)/shard_map/ppermute | solution.py:18
  67.2 14.1 %collective-permute-start.29 = (bf16[2,432,128]{2,1,0:T(8,128)(2,1)S(1)}, bf16[2,432,128]{2,1,0:T(8,128)(2,1)S(1)}, u32[]{:S(2)}, u32[]{:S(2)}) collective-permute-start(bf16[2,432,128]{2,1,0:T(8,128)(2,1)S(1)} %collective-permute-done.28.refs_2_), channel_id=1, source_target_pairs={{0,1},{1,0},{2,3},{3,2},{4,5},{5,4},{6,7},{7,6},{8,9},{9,8},{10,11... | collective-permute-start | bytes 663560 | tf_op jit(solution)/shard_map/ppermute | solution.py:18
  67.2 15.3 %collective-permute-start.32 = (bf16[2,432,128]{2,1,0:T(8,128)(2,1)S(1)}, bf16[2,432,128]{2,1,0:T(8,128)(2,1)S(1)}, u32[]{:S(2)}, u32[]{:S(2)}) collective-permute-start(bf16[2,432,128]{2,1,0:T(8,128)(2,1)S(1)} %collective-permute-done.30.refs_4_), channel_id=1, source_target_pairs={{0,8},{4,12},{8,0},{12,4},{16,24},{20,28},{24,16},{28,20},{1,9},{5... | collective-permute-start | bytes 663560 | tf_op jit(solution)/shard_map/ppermute | solution.py:18
  68.7 8.1 %collective-permute-start.22 = (bf16[10,1,16,256]{3,2,1,0:T(8,128)(2,1)S(1)}, bf16[10,1,16,256]{3,2,1,0:T(8,128)(2,1)S(1)}, u32[]{:S(2)}, u32[]{:S(2)}) collective-permute-start(bf16[10,1,16,256]{3,2,1,0:T(8,128)(2,1)S(1)} %fusion.9), channel_id=1, source_target_pairs={{0,8},{4,12},{8,0},{12,4},{16,24},{20,28},{24,16},{28,20},{1,9},{5... | collective-permute-start | bytes 245768 | tf_op jit(solution)/shard_map/ppermute | solution.py:18
  76.8 15.0 %copy-start = (f32[1,2,864,256]{3,2,1,0:T(8,128)S(1)}, f32[1,2,864,256]{3,2,1,0:T(8,128)}, u32[]{:S(2)}) copy-start(f32[1,2,864,256]{3,2,1,0:T(8,128)} %refs_1_.3) | copy-start | bytes 5308420
  76.8 15.0 %copy-start.1 = (f32[1,2,864,256]{3,2,1,0:T(8,128)S(1)}, f32[1,2,864,256]{3,2,1,0:T(8,128)}, u32[]{:S(2)}) copy-start(f32[1,2,864,256]{3,2,1,0:T(8,128)} %refs_2_.3) | copy-start | bytes 5308420
  76.9 4.3 %collective-permute-start.23 = (bf16[10,6,1,256]{3,2,1,0:T(2,128)(2,1)S(1)}, bf16[10,6,1,256]{3,2,1,0:T(2,128)(2,1)S(1)}, u32[]{:S(2)}, u32[]{:S(2)}) collective-permute-start(bf16[10,6,1,256]{3,2,1,0:T(2,128)(2,1)S(1)} %broadcast_select_fusion.2), channel_id=1, source_target_pairs={{0,4},{4,0},{8,12},{12,8},{16,20},{20,16},{24,28},{28,24},{1,5},{5... | collective-permute-start | bytes 92168 | tf_op jit(solution)/shard_map/ppermute | solution.py:18
  78.1 5.8 %collective-permute-start.31 = (bf16[2,432,128]{2,1,0:T(8,128)(2,1)S(1)}, bf16[2,432,128]{2,1,0:T(8,128)(2,1)S(1)}, u32[]{:S(2)}, u32[]{:S(2)}) collective-permute-start(bf16[2,432,128]{2,1,0:T(8,128)(2,1)S(1)} %collective-permute-done.30.refs_4_), channel_id=1, source_target_pairs={{0,1},{1,0},{2,3},{3,2},{4,5},{5,4},{6,7},{7,6},{8,9},{9,8},{10,11... | collective-permute-start | bytes 663560 | tf_op jit(solution)/shard_map/ppermute | solution.py:18
  81.2 8.2 %collective-permute-start.38 = (bf16[2,432,128]{2,1,0:T(8,128)(2,1)S(1)}, bf16[2,432,128]{2,1,0:T(8,128)(2,1)S(1)}, u32[]{:S(2)}, u32[]{:S(2)}) collective-permute-start(bf16[2,432,128]{2,1,0:T(8,128)(2,1)S(1)} %collective-permute-done.28.refs_2_), channel_id=1, source_target_pairs={{0,2},{1,3},{2,0},{3,1},{4,6},{5,7},{6,4},{7,5},{8,10},{9,11},{10,... | collective-permute-start | bytes 663560 | tf_op jit(solution)/shard_map/ppermute | solution.py:18
  81.3 5.9 %collective-permute-start.36 = (bf16[2,432,128]{2,1,0:T(8,128)(2,1)S(1)}, bf16[2,432,128]{2,1,0:T(8,128)(2,1)S(1)}, u32[]{:S(2)}, u32[]{:S(2)}) collective-permute-start(bf16[2,432,128]{2,1,0:T(8,128)(2,1)S(1)} %collective-permute-done.34.refs_8_), channel_id=1, source_target_pairs={{0,4},{4,0},{8,12},{12,8},{16,20},{20,16},{24,28},{28,24},{1,5},{5... | collective-permute-start | bytes 663560 | tf_op jit(solution)/shard_map/ppermute | solution.py:18
  82.5 9.4 %collective-permute-start.40 = (bf16[2,432,128]{2,1,0:T(8,128)(2,1)S(1)}, bf16[2,432,128]{2,1,0:T(8,128)(2,1)S(1)}, u32[]{:S(2)}, u32[]{:S(2)}) collective-permute-start(bf16[2,432,128]{2,1,0:T(8,128)(2,1)S(1)} %collective-permute-done.32.refs_6_), channel_id=1, source_target_pairs={{0,2},{1,3},{2,0},{3,1},{4,6},{5,7},{6,4},{7,5},{8,10},{9,11},{10,... | collective-permute-start | bytes 663560 | tf_op jit(solution)/shard_map/ppermute | solution.py:18
  83.9 10.1 %collective-permute-start.35 = (bf16[2,432,128]{2,1,0:T(8,128)(2,1)S(1)}, bf16[2,432,128]{2,1,0:T(8,128)(2,1)S(1)}, u32[]{:S(2)}, u32[]{:S(2)}) collective-permute-start(bf16[2,432,128]{2,1,0:T(8,128)(2,1)S(1)} %collective-permute-done.34.refs_8_), channel_id=1, source_target_pairs={{0,1},{1,0},{2,3},{3,2},{4,5},{5,4},{6,7},{7,6},{8,9},{9,8},{10,11... | collective-permute-start | bytes 663560 | tf_op jit(solution)/shard_map/ppermute | solution.py:18
  87.3 6.8 %collective-permute-start.33 = (bf16[2,432,128]{2,1,0:T(8,128)(2,1)S(1)}, bf16[2,432,128]{2,1,0:T(8,128)(2,1)S(1)}, u32[]{:S(2)}, u32[]{:S(2)}) collective-permute-start(bf16[2,432,128]{2,1,0:T(8,128)(2,1)S(1)} %collective-permute-done.32.refs_6_), channel_id=1, source_target_pairs={{0,1},{1,0},{2,3},{3,2},{4,5},{5,4},{6,7},{7,6},{8,9},{9,8},{10,11... | collective-permute-start | bytes 663560 | tf_op jit(solution)/shard_map/ppermute | solution.py:18
  89.4 4.6 %collective-permute-start.37 = (bf16[2,432,128]{2,1,0:T(8,128)(2,1)S(1)}, bf16[2,432,128]{2,1,0:T(8,128)(2,1)S(1)}, u32[]{:S(2)}, u32[]{:S(2)}) collective-permute-start(bf16[2,432,128]{2,1,0:T(8,128)(2,1)S(1)} %collective-permute-done.36.refs_10_), channel_id=1, source_target_pairs={{0,1},{1,0},{2,3},{3,2},{4,5},{5,4},{6,7},{7,6},{8,9},{9,8},{10,11... | collective-permute-start | bytes 663560 | tf_op jit(solution)/shard_map/ppermute | solution.py:18
  89.4 4.6 %collective-permute-start.39 = (bf16[2,432,128]{2,1,0:T(8,128)(2,1)S(1)}, bf16[2,432,128]{2,1,0:T(8,128)(2,1)S(1)}, u32[]{:S(2)}, u32[]{:S(2)}) collective-permute-start(bf16[2,432,128]{2,1,0:T(8,128)(2,1)S(1)} %collective-permute-done.38.refs_12_), channel_id=1, source_target_pairs={{0,1},{1,0},{2,3},{3,2},{4,5},{5,4},{6,7},{7,6},{8,9},{9,8},{10,11... | collective-permute-start | bytes 663560 | tf_op jit(solution)/shard_map/ppermute | solution.py:18
  91.8 2.3 %collective-permute-start.41 = (bf16[2,432,128]{2,1,0:T(8,128)(2,1)S(1)}, bf16[2,432,128]{2,1,0:T(8,128)(2,1)S(1)}, u32[]{:S(2)}, u32[]{:S(2)}) collective-permute-start(bf16[2,432,128]{2,1,0:T(8,128)(2,1)S(1)} %collective-permute-done.40.refs_14_), channel_id=1, source_target_pairs={{0,1},{1,0},{2,3},{3,2},{4,5},{5,4},{6,7},{7,6},{8,9},{9,8},{10,11... | collective-permute-start | bytes 663560 | tf_op jit(solution)/shard_map/ppermute | solution.py:18

commit v2 on v1

--- a/solution.py
+++ b/solution.py
@@ -261,7 +261,7 @@
     )(master, kept, came, *crossed)
 
 
-def gathered(piece, row_shares, last):
+def gathered(piece, row_shares, last, late):
     strides = []
     stride = lax.axis_size("space") // 2
     while stride:
@@ -285,11 +285,12 @@
 
     own = (held, masks)
     z, y = moved(own, "z"), moved(own, "y")
-    yz = moved(y, "z")
+    yz = moved(z, "y") if late else moved(y, "z")
     found = [own, z, y, yz]
     if row_shares == 2:
         x = moved(own, "x")
-        xy, zx = moved(x, "y"), moved(z, "x")
+        xy = moved(y, "x") if late else moved(x, "y")
+        zx = moved(z, "x")
         corner = moved({"y": zx, "z": xy, "x": yz}[last], last)
         found += [x, xy, zx, corner]
     arrays, places = [], []
@@ -358,7 +359,7 @@
     for index in range(filter_count):
         if index:
             hidden = extend_brick(hidden, coords, strides, grid)
-        arrays, places = gathered(pieces[index], row_shares, "yx"[index % 2])
+        arrays, places = gathered(pieces[index], row_shares, "y", index > 0)
         beside.append(arrays[1][0])
         hidden = convolve(hidden, arrays, places, span)
 

time: 97.5 us -> 93.2 us (0.956)
  waiting for transfers between devices: 41.6 us -> 35 us
  starting transfers between devices: 33.6 us -> 36 us
    ppermute x44, waiting for transfers between devices: 41.6 us -> 35 us  [swap(): lax.ppermute(value, axis, [(source, source ^ stride) for source in range(...]
    ppermute x44, starting transfers between devices: 33.6 us -> 36 us  [swap(): lax.ppermute(value, axis, [(source, source ^ stride) for source in range(...]
  transfers between devices with their start and end apart: 44 -> 44, of which waited for: 14 -> 14; matrix products, arithmetic and copies ran while one was open for 8% -> 9% of each run, Pallas kernels for 8% -> 8%
where the time goes in v2:
time: 93.2 us; the launch traced here: 92.8 us
  starting transfers between devices  36 us (39%)
  waiting for transfers between devices  35 us (38%)
  Pallas kernels  12.6 us (14%)
  other arithmetic  7.02 us (8%)
  local copies, waits for them, and re-layouts  1.24 us (1%)
  between operations  1.07 us (1%)
    ppermute x44, starting transfers between devices, swap(): lax.ppermute(value, axis, [(source, source ^ stride) for source in range(...  36 us
    ppermute x44, waiting for transfers between devices, swap(): lax.ppermute(value, axis, [(source, source ^ stride) for source in range(...  35 us
    pallas_call x2, Pallas kernels, convolve(): pl.pallas_call(functools.partial(conv_kernel, places, span), out_shape=ja...  5.32 us
    pallas_call x2, Pallas kernels, split_state(): pl.pallas_call(functools.partial(split_kernel, index), out_shape=(shape,...  4.41 us
    select_n x15, other arithmetic, pick(): return jnp.where(flag, one, other)  2.81 us
    select_n x1, other arithmetic, shards(): second_out = jnp.where(owned, second_new, moment_second[0])[None]  2.21 us
  transfers between devices with their start and end apart: 44, of which 14 were waited for; matrix products, arithmetic and copies ran while one was open for 9% of the time, Pallas kernels for 8%

profile of v2, /device:TPU:0, one launch (start us, length us, event | category | flops | bytes accessed | tf_op | source)
XLA Modules:
  0.0 92.8 jit_solution(11725348726971263205)
XLA Ops:
  0.6 1.8 %shard_map.93 = (bf16[3,864,128]{2,1,0:T(8,128)(2,1)S(1)}, bf16[3,864,128]{2,1,0:T(8,128)(2,1)S(1)}) custom-call(bf16[1,2,864,256]{3,2,1,0:T(8,128)(2,1)} %refs_0_.3, f32[1,2,864,256]{3,2,1,0:T(8,128)} %refs_1_.3, f32[1,2,864,256]{3,2,1,0:T(8,128)} %refs_2_.3, s32[2,32]{1,0:T(2,128)} %refs_3_.3), custom_call_target="tpu_custom_call" | custom-call | flops 884736 | bytes 3538944 | tf_op jit(solution)/shard_map/pallas_call | solution.py:152
  2.5 0.6 collective-permute-start.3
  3.0 3.7 %collective-permute-start = (bf16[1,4,16,256]{3,2,1,0:T(8,128)(2,1)S(1)}, bf16[1,4,16,256]{3,2,1,0:T(8,128)(2,1)S(1)}, u32[]{:S(2)}, u32[]{:S(2)}) collective-permute-start(bf16[1,4,16,256]{3,2,1,0:T(8,128)(2,1)S(1)} %select_bitcast_fusion), channel_id=1, source_target_pairs={{0,16},{4,20},{8,24},{12,28},{16,0},{20,4},{24,8},{28,12},{1,17},{... | collective-permute-start | bytes 98312 | tf_op jit(solution)/shard_map/ppermute | solution.py:18
  6.7 0.1 shard_map.94.refs_4_
  6.8 1.6 %collective-permute-start.4 = (bf16[3,432,128]{2,1,0:T(8,128)(2,1)S(1)}, bf16[3,432,128]{2,1,0:T(8,128)(2,1)}, u32[]{:S(2)}, u32[]{:S(2)}) collective-permute-start(bf16[3,432,128]{2,1,0:T(8,128)(2,1)S(1)} %shard_map.94.refs_4_), channel_id=1, source_target_pairs={{0,2},{1,3},{2,0},{3,1},{4,6},{5,7},{6,4},{7,5},{8,10},{9,11},{10,... | collective-permute-start | bytes 995336 | tf_op jit(solution)/shard_map/ppermute | solution.py:18
  8.4 2.6 %shard_map.95 = (bf16[3,864,128]{2,1,0:T(8,128)(2,1)S(1)}, bf16[3,864,128]{2,1,0:T(8,128)(2,1)}) custom-call(bf16[1,2,864,256]{3,2,1,0:T(8,128)(2,1)} %refs_0_.3, f32[1,2,864,256]{3,2,1,0:T(8,128)} %refs_1_.3, f32[1,2,864,256]{3,2,1,0:T(8,128)} %refs_2_.3, s32[2,32]{1,0:T(2,128)} %refs_3_.3, bf16[3,432,128]{2,1,0:T(8,128)(2,1)S(1)} %shard_map.94.refs_4_), custom_call_target="tpu_custom_call" | custom-call | flops 884736 | bytes 3538944 | tf_op jit(solution)/shard_map/pallas_call | solution.py:152
  11.1 0.7 fusion.10
  11.8 1.6 %collective-permute-start.1 = (bf16[10,1,16,256]{3,2,1,0:T(8,128)(2,1)}, bf16[10,1,16,256]{3,2,1,0:T(8,128)(2,1)S(1)}, u32[]{:S(2)}, u32[]{:S(2)}) collective-permute-start(bf16[10,1,16,256]{3,2,1,0:T(8,128)(2,1)} %fusion.10), channel_id=1, source_target_pairs={{0,8},{4,12},{8,0},{12,4},{16,24},{20,28},{24,16},{28,20},{1,9},{5... | collective-permute-start | bytes 245768 | tf_op jit(solution)/shard_map/ppermute | solution.py:18
  13.3 1.0 %shard_map.96.master_ref = f32[2,432,128]{2,1,0:T(8,128)S(1)} custom-call(f32[2,864,256]{2,1,0:T(8,128)} %all_master.1, bf16[3,864,128]{2,1,0:T(8,128)(2,1)S(1)} %get-tuple-element.14.refs_0_.kept_ref), custom_call_target="tpu_custom_call" | custom-call | bytes 884736 | tf_op jit(solution)/shard_map/pallas_call | solution.py:211
  14.4 2.4 %collective-permute-done.4.refs_0_ = bf16[3,432,128]{2,1,0:T(8,128)(2,1)} collective-permute-done((bf16[3,432,128]{2,1,0:T(8,128)(2,1)S(1)}, bf16[3,432,128]{2,1,0:T(8,128)(2,1)}, u32[]{:S(2)}, u32[]{:S(2)}) %collective-permute-start.4) | collective-permute-done | bytes 331808 | tf_op jit(solution)/shard_map/ppermute | solution.py:18
  16.9 1.3 %shard_map.97 = (bf16[432,128]{1,0:T(8,128)(2,1)S(1)}, bf16[432,128]{1,0:T(8,128)(2,1)S(1)}) custom-call(f32[2,432,128]{2,1,0:T(8,128)S(1)} %shard_map.96.master_ref, bf16[3,864,128]{2,1,0:T(8,128)(2,1)S(1)} %get-tuple-element.12.kept_ref, bf16[3,864,128]{2,1,0:T(8,128)(2,1)S(1)} %collective-permute-done.3.came_ref, ...), custom_call_target="tpu_custom_call" | custom-call | flops 1105920 | bytes 1658880 | tf_op jit(solution)/shard_map/pallas_call | solution.py:252
  18.2 2.0 %collective-permute-start.5 = (bf16[1,432,128]{2,1,0:T(8,128)(2,1)S(1)}, bf16[1,432,128]{2,1,0:T(8,128)(2,1)S(1)}, u32[]{:S(2)}, u32[]{:S(2)}) collective-permute-start(bf16[1,432,128]{2,1,0:T(8,128)(2,1)S(1)} %bitcast.20), channel_id=1, source_target_pairs={{0,16},{4,20},{8,24},{12,28},{16,0},{20,4},{24,8},{28,12},{1,17},{... | collective-permute-start | bytes 331784 | tf_op jit(solution)/shard_map/ppermute | solution.py:18
  20.2 5.6 %collective-permute-done.5 = bf16[1,432,128]{2,1,0:T(8,128)(2,1)S(1)} collective-permute-done((bf16[1,432,128]{2,1,0:T(8,128)(2,1)S(1)}, bf16[1,432,128]{2,1,0:T(8,128)(2,1)S(1)}, u32[]{:S(2)}, u32[]{:S(2)}) %collective-permute-start.5) | collective-permute-done | bytes 110624 | tf_op jit(solution)/shard_map/ppermute | solution.py:18
  25.9 1.6 %collective-permute-start.9 = (bf16[2,432,128]{2,1,0:T(8,128)(2,1)S(1)}, bf16[2,432,128]{2,1,0:T(8,128)(2,1)S(1)}, u32[]{:S(2)}, u32[]{:S(2)}) collective-permute-start(bf16[2,432,128]{2,1,0:T(8,128)(2,1)S(1)} %pad_maximum_fusion.2.refs_0_), channel_id=1, source_target_pairs={{0,4},{4,0},{8,12},{12,8},{16,20},{20,16},{24,28},{28,24},{1,5},{5... | collective-permute-start | bytes 663560 | tf_op jit(solution)/shard_map/ppermute | solution.py:18
  27.5 0.7 broadcast_select_fusion.5
  28.2 0.5 collective-permute-start.2
  28.7 0.1 shard_map.99
  28.8 1.6 %collective-permute-start.25 = (bf16[3,432,128]{2,1,0:T(8,128)(2,1)S(1)}, bf16[3,432,128]{2,1,0:T(8,128)(2,1)S(1)}, u32[]{:S(2)}, u32[]{:S(2)}) collective-permute-start(bf16[3,432,128]{2,1,0:T(8,128)(2,1)S(1)} %shard_map.99), channel_id=1, source_target_pairs={{0,2},{1,3},{2,0},{3,1},{4,6},{5,7},{6,4},{7,5},{8,10},{9,11},{10,... | collective-permute-start | bytes 995336 | tf_op jit(solution)/shard_map/ppermute | solution.py:18
  30.5 0.1 broadcast_in_dim.29
  30.5 0.1 eq.41
  30.7 3.2 %collective-permute-done.2 = bf16[10,6,1,256]{3,2,1,0:T(2,128)(2,1)} collective-permute-done((bf16[10,6,1,256]{3,2,1,0:T(2,128)(2,1)}, bf16[10,6,1,256]{3,2,1,0:T(2,128)(2,1)}, u32[]{:S(2)}, u32[]{:S(2)}) %collective-permute-start.2) | collective-permute-done | bytes 30752 | tf_op jit(solution)/shard_map/ppermute | solution.py:18
  33.9 1.5 %collective-permute-start.13 = (bf16[2,432,128]{2,1,0:T(8,128)(2,1)S(1)}, bf16[2,432,128]{2,1,0:T(8,128)(2,1)S(1)}, u32[]{:S(2)}, u32[]{:S(2)}) collective-permute-start(bf16[2,432,128]{2,1,0:T(8,128)(2,1)S(1)} %pad_maximum_fusion.2.refs_0_), channel_id=1, source_target_pairs={{0,2},{1,3},{2,0},{3,1},{4,6},{5,7},{6,4},{7,5},{8,10},{9,11},{10,... | collective-permute-start | bytes 663560 | tf_op jit(solution)/shard_map/ppermute | solution.py:18
  35.4 0.6 collective-permute-start.17
  36.0 0.9 %broadcast_select_fusion.4 = (bf16[10,6,1,256]{3,2,1,0:T(2,128)(2,1)S(1)}, bf16[10,6,1,256]{3,2,1,0:T(2,128)(2,1)S(1)}) fusion(bf16[10,6,1,256]{3,2,1,0:T(2,128)(2,1)} %collective-permute-done.2, pred[]{:T(512)S(6)} %eq.35), kind=kLoop, calls=%fused_computation.24 | loop fusion | flops 30720 | bytes 92161 | tf_op jit(solution)/shard_map/jit(_where)/select_n | solution.py:28
  37.0 2.6 %collective-permute-done.25.refs_0_ = bf16[3,432,128]{2,1,0:T(8,128)(2,1)S(1)} collective-permute-done((bf16[3,432,128]{2,1,0:T(8,128)(2,1)S(1)}, bf16[3,432,128]{2,1,0:T(8,128)(2,1)S(1)}, u32[]{:S(2)}, u32[]{:S(2)}) %collective-permute-start.25) | collective-permute-done | bytes 331808 | tf_op jit(solution)/shard_map/ppermute | solution.py:18
  39.6 0.3 shard_map.100
  39.9 0.6 collective-permute-start.11
  40.6 3.7 %collective-permute-done.13.refs_8_ = bf16[2,432,128]{2,1,0:T(8,128)(2,1)S(1)} collective-permute-done((bf16[2,432,128]{2,1,0:T(8,128)(2,1)S(1)}, bf16[2,432,128]{2,1,0:T(8,128)(2,1)S(1)}, u32[]{:S(2)}, u32[]{:S(2)}) %collective-permute-start.13) | collective-permute-done | bytes 221216 | tf_op jit(solution)/shard_map/ppermute | solution.py:18
  44.3 1.5 %collective-permute-start.15 = (bf16[2,432,128]{2,1,0:T(8,128)(2,1)S(1)}, bf16[2,432,128]{2,1,0:T(8,128)(2,1)S(1)}, u32[]{:S(2)}, u32[]{:S(2)}) collective-permute-start(bf16[2,432,128]{2,1,0:T(8,128)(2,1)S(1)} %collective-permute-done.13.refs_8_), channel_id=1, source_target_pairs={{0,4},{4,0},{8,12},{12,8},{16,20},{20,16},{24,28},{28,24},{1,5},{5... | collective-permute-start | bytes 663560 | tf_op jit(solution)/shard_map/ppermute | solution.py:18
  45.8 0.9 collective-permute-done.17.refs_12_
  46.7 1.5 %collective-permute-start.19 = (bf16[2,432,128]{2,1,0:T(8,128)(2,1)S(1)}, bf16[2,432,128]{2,1,0:T(8,128)(2,1)S(1)}, u32[]{:S(2)}, u32[]{:S(2)}) collective-permute-start(bf16[2,432,128]{2,1,0:T(8,128)(2,1)S(1)} %collective-permute-done.17.refs_12_), channel_id=1, source_target_pairs={{0,4},{4,0},{8,12},{12,8},{16,20},{20,16},{24,28},{28,24},{1,5},{5... | collective-permute-start | bytes 663560 | tf_op jit(solution)/shard_map/ppermute | solution.py:18
  48.3 1.5 %collective-permute-start.42 = (bf16[2,432,128]{2,1,0:T(8,128)(2,1)S(1)}, bf16[2,432,128]{2,1,0:T(8,128)(2,1)S(1)}, u32[]{:S(2)}, u32[]{:S(2)}) collective-permute-start(bf16[2,432,128]{2,1,0:T(8,128)(2,1)S(1)} %pad_maximum_fusion.4), channel_id=1, source_target_pairs={{0,2},{1,3},{2,0},{3,1},{4,6},{5,7},{6,4},{7,5},{8,10},{9,11},{10,... | collective-permute-start | bytes 663560 | tf_op jit(solution)/shard_map/ppermute | solution.py:18
  49.8 1.2 %pad_maximum_fusion.field_ref = bf16[10,6,18,256]{3,2,1,0:T(8,128)(2,1)S(1)} fusion(bf16[10,6,1,256]{3,2,1,0:T(2,128)(2,1)S(1)} %get-tuple-element.29, bf16[10,1,16,256]{3,2,1,0:T(8,128)(2,1)S(1)} %get-tuple-element.25, bf16[1,4,16,256]{3,2,1,0:T(8,128)(2,1)} %copy-done.8, bf16[8,4,16,256]{3,2,1,0:T(8,128)(2,1)S(1)} %bitcast.28, ...), kind=kLoop, calls=%fused_computation.8 | loop fusion | flops 3870720 | bytes 1105920 | tf_op jit(solution)/shard_map/concatenate | solution.py:48
  51.0 3.4 %collective-permute-start.26 = (bf16[1,432,128]{2,1,0:T(8,128)(2,1)S(1)}, bf16[1,432,128]{2,1,0:T(8,128)(2,1)S(1)}, u32[]{:S(2)}, u32[]{:S(2)}) collective-permute-start(bf16[1,432,128]{2,1,0:T(8,128)(2,1)S(1)} %bitcast.23), channel_id=1, source_target_pairs={{0,16},{4,20},{8,24},{12,28},{16,0},{20,4},{24,8},{28,12},{1,17},{... | collective-permute-start | bytes 331784 | tf_op jit(solution)/shard_map/ppermute | solution.py:18
  54.6 0.5 collective-permute-start.18
  55.1 0.1 collective-permute-start.12
  55.2 3.1 %collective-permute-done.26 = bf16[1,432,128]{2,1,0:T(8,128)(2,1)S(1)} collective-permute-done((bf16[1,432,128]{2,1,0:T(8,128)(2,1)S(1)}, bf16[1,432,128]{2,1,0:T(8,128)(2,1)S(1)}, u32[]{:S(2)}, u32[]{:S(2)}) %collective-permute-start.26) | collective-permute-done | bytes 110624 | tf_op jit(solution)/shard_map/ppermute | solution.py:18
  58.3 0.5 collective-permute-start.20
  58.8 0.1 fusion.11
  59.1 0.6 collective-permute-done.16.refs_11_
  59.7 0.4 collective-permute-start.30
  60.2 0.5 collective-permute-start.34
  60.7 2.3 %shard_map.98 = bf16[8,4,16,256]{3,2,1,0:T(8,128)(2,1)S(1)} custom-call(bf16[10,6,18,256]{3,2,1,0:T(8,128)(2,1)S(1)} %pad_maximum_fusion.field_ref, bf16[2,432,128]{2,1,0:T(8,128)(2,1)S(1)} %pad_maximum_fusion.2.refs_0_, bf16[2,432,128]{2,1,0:T(8,128)(2,1)S(1)} %collective-permute-done.6.refs_1_, bf16[2,432,128]{2,1,0:T(8,128)(2,1)S(1)} %collective-permute-done.7.refs_2_, ...), custom_call_target="tpu_custom_call" | custom-call | flops 1811939328 | bytes 4063232 | tf_op jit(solution)/shard_map/pallas_call | solution.py:92
  63.0 2.2 %collective-permute-start.21 = (bf16[1,4,16,256]{3,2,1,0:T(8,128)(2,1)S(1)}, bf16[1,4,16,256]{3,2,1,0:T(8,128)(2,1)S(1)}, u32[]{:S(2)}, u32[]{:S(2)}) collective-permute-start(bf16[1,4,16,256]{3,2,1,0:T(8,128)(2,1)S(1)} %slice_select_fusion), channel_id=1, source_target_pairs={{0,16},{4,20},{8,24},{12,28},{16,0},{20,4},{24,8},{28,12},{1,17},{... | collective-permute-start | bytes 98312 | tf_op jit(solution)/shard_map/ppermute | solution.py:18
  65.2 0.1 maximum_select_fusion.1
  65.4 1.8 %collective-permute-done.28.refs_2_ = bf16[2,432,128]{2,1,0:T(8,128)(2,1)S(1)} collective-permute-done((bf16[2,432,128]{2,1,0:T(8,128)(2,1)S(1)}, bf16[2,432,128]{2,1,0:T(8,128)(2,1)S(1)}, u32[]{:S(2)}, u32[]{:S(2)}) %collective-permute-start.28) | collective-permute-done | bytes 221216 | tf_op jit(solution)/shard_map/ppermute | solution.py:18
  67.2 0.9 collective-permute-done.21
  68.2 1.4 %collective-permute-start.22 = (bf16[10,1,16,256]{3,2,1,0:T(8,128)(2,1)S(1)}, bf16[10,1,16,256]{3,2,1,0:T(8,128)(2,1)S(1)}, u32[]{:S(2)}, u32[]{:S(2)}) collective-permute-start(bf16[10,1,16,256]{3,2,1,0:T(8,128)(2,1)S(1)} %fusion.9), channel_id=1, source_target_pairs={{0,8},{4,12},{8,0},{12,4},{16,24},{20,28},{24,16},{28,20},{1,9},{5... | collective-permute-start | bytes 245768 | tf_op jit(solution)/shard_map/ppermute | solution.py:18
  69.6 3.0 %collective-permute-done.22 = bf16[10,1,16,256]{3,2,1,0:T(8,128)(2,1)S(1)} collective-permute-done((bf16[10,1,16,256]{3,2,1,0:T(8,128)(2,1)S(1)}, bf16[10,1,16,256]{3,2,1,0:T(8,128)(2,1)S(1)}, u32[]{:S(2)}, u32[]{:S(2)}) %collective-permute-start.22) | collective-permute-done | bytes 81952 | tf_op jit(solution)/shard_map/ppermute | solution.py:18
  72.7 1.3 %collective-permute-start.38 = (bf16[2,432,128]{2,1,0:T(8,128)(2,1)S(1)}, bf16[2,432,128]{2,1,0:T(8,128)(2,1)S(1)}, u32[]{:S(2)}, u32[]{:S(2)}) collective-permute-start(bf16[2,432,128]{2,1,0:T(8,128)(2,1)S(1)} %collective-permute-done.28.refs_2_), channel_id=1, source_target_pairs={{0,2},{1,3},{2,0},{3,1},{4,6},{5,7},{6,4},{7,5},{8,10},{9,11},{10,... | collective-permute-start | bytes 663560 | tf_op jit(solution)/shard_map/ppermute | solution.py:18
  74.0 0.1 broadcast_select_fusion.2
  74.2 1.6 %collective-permute-start.23 = (bf16[10,6,1,256]{3,2,1,0:T(2,128)(2,1)S(1)}, bf16[10,6,1,256]{3,2,1,0:T(2,128)(2,1)S(1)}, u32[]{:S(2)}, u32[]{:S(2)}) collective-permute-start(bf16[10,6,1,256]{3,2,1,0:T(2,128)(2,1)S(1)} %broadcast_select_fusion.2), channel_id=1, source_target_pairs={{0,4},{4,0},{8,12},{12,8},{16,20},{20,16},{24,28},{28,24},{1,5},{5... | collective-permute-start | bytes 92168 | tf_op jit(solution)/shard_map/ppermute | solution.py:18
  75.8 1.0 %copy.10 = f32[1,2,216,256]{3,1,2,0:T(2,128)} copy(f32[1,2,216,256]{3,2,1,0:T(8,128)S(1)} %convert_bitcast_fusion) | data formatting | bytes 884736
  76.8 0.5 collective-permute-start.32
  77.3 1.8 %collective-permute-done.23 = bf16[10,6,1,256]{3,2,1,0:T(2,128)(2,1)S(1)} collective-permute-done((bf16[10,6,1,256]{3,2,1,0:T(2,128)(2,1)S(1)}, bf16[10,6,1,256]{3,2,1,0:T(2,128)(2,1)S(1)}, u32[]{:S(2)}, u32[]{:S(2)}) %collective-permute-start.23) | collective-permute-done | bytes 30752 | tf_op jit(solution)/shard_map/ppermute | solution.py:18
  79.1 0.7 collective-permute-start.36
  79.8 1.3 %collective-permute-start.40 = (bf16[2,432,128]{2,1,0:T(8,128)(2,1)S(1)}, bf16[2,432,128]{2,1,0:T(8,128)(2,1)S(1)}, u32[]{:S(2)}, u32[]{:S(2)}) collective-permute-start(bf16[2,432,128]{2,1,0:T(8,128)(2,1)S(1)} %collective-permute-done.38.refs_12_), channel_id=1, source_target_pairs={{0,4},{4,0},{8,12},{12,8},{16,20},{20,16},{24,28},{28,24},{1,5},{5... | collective-permute-start | bytes 663560 | tf_op jit(solution)/shard_map/ppermute | solution.py:18
  81.1 0.1 broadcast_select_fusion.1
  81.2 0.5 pad_maximum_fusion.1.field_ref
  81.8 1.1 %collective-permute-done.32.refs_6_ = bf16[2,432,128]{2,1,0:T(8,128)(2,1)S(1)} collective-permute-done((bf16[2,432,128]{2,1,0:T(8,128)(2,1)S(1)}, bf16[2,432,128]{2,1,0:T(8,128)(2,1)S(1)}, u32[]{:S(2)}, u32[]{:S(2)}) %collective-permute-start.32) | collective-permute-done | bytes 221216 | tf_op jit(solution)/shard_map/ppermute | solution.py:18
  82.9 4.1 %collective-permute-done.36.refs_10_ = bf16[2,432,128]{2,1,0:T(8,128)(2,1)S(1)} collective-permute-done((bf16[2,432,128]{2,1,0:T(8,128)(2,1)S(1)}, bf16[2,432,128]{2,1,0:T(8,128)(2,1)S(1)}, u32[]{:S(2)}, u32[]{:S(2)}) %collective-permute-start.36) | collective-permute-done | bytes 221216 | tf_op jit(solution)/shard_map/ppermute | solution.py:18
  87.0 0.5 collective-permute-start.37
  87.6 2.2 %fusion.4 = (f32[1,2,864,256]{3,2,1,0:T(8,128)}, f32[1,2,864,256]{3,2,1,0:T(8,128)}) fusion(f32[1,2,864,256]{3,2,1,0:T(8,128)S(1)} %copy-done.1, pred[2,864]{1,0:T(4,128)(4,1)S(1)} %eq.41, bf16[1,2,864,128]{3,2,1,0:T(8,128)(2,1)S(1)} %fusion.11, bf16[1,2,864,128]{3,2,1,0:T(8,128)(2,1)S(1)} %bitcast.30, pred[]{:T(512)S(6)} %eq.38, ...), kind=kLoop, calls=%fused_computation.6 | loop fusion | flops 8404992 | bytes 7964353 | tf_op jit(solution)/shard_map/jit(_where)/select_n | solution.py:370
  89.8 3.0 %shard_map.101 = bf16[8,4,16,256]{3,2,1,0:T(8,128)(2,1)} custom-call(bf16[10,6,18,256]{3,2,1,0:T(8,128)(2,1)S(1)} %pad_maximum_fusion.1.field_ref, bf16[2,432,128]{2,1,0:T(8,128)(2,1)S(1)} %pad_maximum_fusion.3.refs_0_, bf16[2,432,128]{2,1,0:T(8,128)(2,1)S(1)} %collective-permute-done.27.refs_1_, bf16[2,432,128]{2,1,0:T(8,128)(2,1)S(1)} %collective-permute-done.28.refs_2_, ...), custom_call_target="tpu_custom_call" | custom-call | flops 1811939328 | bytes 4063232 | tf_op jit(solution)/shard_map/pallas_call | solution.py:92
  (84 shorter events, 1.2 us)
Async XLA Ops:
  0.6 2.4 %copy-start.2 = (bf16[1,1,8,4,16,256]{5,4,3,2,1,0:T(8,128)(2,1)S(1)}, bf16[1,1,8,4,16,256]{5,4,3,2,1,0:T(8,128)(2,1)}, u32[]{:S(2)}) copy-start(bf16[1,1,8,4,16,256]{5,4,3,2,1,0:T(8,128)(2,1)} %param.6) | copy-start | bytes 786436
  2.5 4.3 %collective-permute-start.3 = (bf16[3,864,128]{2,1,0:T(8,128)(2,1)S(1)}, bf16[3,864,128]{2,1,0:T(8,128)(2,1)S(1)}, u32[]{:S(2)}, u32[]{:S(2)}) collective-permute-start(bf16[3,864,128]{2,1,0:T(8,128)(2,1)S(1)} %get-tuple-element.13), channel_id=1, source_target_pairs={{0,1},{1,0},{2,3},{3,2},{4,5},{5,4},{6,7},{7,6},{8,9},{9,8},{10,11... | collective-permute-start | bytes 1990664 | tf_op jit(solution)/shard_map/ppermute | solution.py:18
  3.0 8.0 %collective-permute-start = (bf16[1,4,16,256]{3,2,1,0:T(8,128)(2,1)S(1)}, bf16[1,4,16,256]{3,2,1,0:T(8,128)(2,1)S(1)}, u32[]{:S(2)}, u32[]{:S(2)}) collective-permute-start(bf16[1,4,16,256]{3,2,1,0:T(8,128)(2,1)S(1)} %select_bitcast_fusion), channel_id=1, source_target_pairs={{0,16},{4,20},{8,24},{12,28},{16,0},{20,4},{24,8},{28,12},{1,17},{... | collective-permute-start | bytes 98312 | tf_op jit(solution)/shard_map/ppermute | solution.py:18
  6.8 10.1 %collective-permute-start.4 = (bf16[3,432,128]{2,1,0:T(8,128)(2,1)S(1)}, bf16[3,432,128]{2,1,0:T(8,128)(2,1)}, u32[]{:S(2)}, u32[]{:S(2)}) collective-permute-start(bf16[3,432,128]{2,1,0:T(8,128)(2,1)S(1)} %shard_map.94.refs_4_), channel_id=1, source_target_pairs={{0,2},{1,3},{2,0},{3,1},{4,6},{5,7},{6,4},{7,5},{8,10},{9,11},{10,... | collective-permute-start | bytes 995336 | tf_op jit(solution)/shard_map/ppermute | solution.py:18
  11.0 17.8 %collective-permute-start.24 = (bf16[3,864,128]{2,1,0:T(8,128)(2,1)}, bf16[3,864,128]{2,1,0:T(8,128)(2,1)S(1)}, u32[]{:S(2)}, u32[]{:S(2)}) collective-permute-start(bf16[3,864,128]{2,1,0:T(8,128)(2,1)} %get-tuple-element.16), channel_id=1, source_target_pairs={{0,1},{1,0},{2,3},{3,2},{4,5},{5,4},{6,7},{7,6},{8,9},{9,8},{10,11... | collective-permute-start | bytes 1990664 | tf_op jit(solution)/shard_map/ppermute | solution.py:18
  11.1 2.3 %copy-start.5 = (bf16[1,4,16,256]{3,2,1,0:T(8,128)(2,1)}, bf16[1,4,16,256]{3,2,1,0:T(8,128)(2,1)S(1)}, u32[]{:S(2)}) copy-start(bf16[1,4,16,256]{3,2,1,0:T(8,128)(2,1)S(1)} %get-tuple-element.32) | copy-start | bytes 98308
  11.1 2.3 %copy-start.8 = (bf16[1,4,16,256]{3,2,1,0:T(8,128)(2,1)}, bf16[1,4,16,256]{3,2,1,0:T(8,128)(2,1)S(1)}, u32[]{:S(2)}) copy-start(bf16[1,4,16,256]{3,2,1,0:T(8,128)(2,1)S(1)} %get-tuple-element.33) | copy-start | bytes 98308
  11.8 8.4 %collective-permute-start.1 = (bf16[10,1,16,256]{3,2,1,0:T(8,128)(2,1)}, bf16[10,1,16,256]{3,2,1,0:T(8,128)(2,1)S(1)}, u32[]{:S(2)}, u32[]{:S(2)}) collective-permute-start(bf16[10,1,16,256]{3,2,1,0:T(8,128)(2,1)} %fusion.10), channel_id=1, source_target_pairs={{0,8},{4,12},{8,0},{12,4},{16,24},{20,28},{24,16},{28,20},{1,9},{5... | collective-permute-start | bytes 245768 | tf_op jit(solution)/shard_map/ppermute | solution.py:18
  14.4 13.1 %copy-start.3 = (bf16[1,1,8,4,16,256]{5,4,3,2,1,0:T(8,128)(2,1)S(1)}, bf16[1,1,8,4,16,256]{5,4,3,2,1,0:T(8,128)(2,1)}, u32[]{:S(2)}) copy-start(bf16[1,1,8,4,16,256]{5,4,3,2,1,0:T(8,128)(2,1)} %param.6) | copy-start | bytes 786436
  14.4 13.1 %copy-start.6 = (bf16[1,4,16,256]{3,2,1,0:T(8,128)(2,1)S(1)}, bf16[1,4,16,256]{3,2,1,0:T(8,128)(2,1)}, u32[]{:S(2)}) copy-start(bf16[1,4,16,256]{3,2,1,0:T(8,128)(2,1)} %copy-done.5) | copy-start | bytes 98308
  14.4 13.1 %copy-start.9 = (bf16[1,4,16,256]{3,2,1,0:T(8,128)(2,1)S(1)}, bf16[1,4,16,256]{3,2,1,0:T(8,128)(2,1)}, u32[]{:S(2)}) copy-start(bf16[1,4,16,256]{3,2,1,0:T(8,128)(2,1)} %copy-done.8) | copy-start | bytes 98308
  18.2 12.2 %copy-start.10 = (s32[2,32]{1,0:T(2,128)S(1)}, s32[2,32]{1,0:T(2,128)}, u32[]{:S(2)}) copy-start(s32[2,32]{1,0:T(2,128)} %refs_3_.3) | copy-start | bytes 772
  18.2 7.6 %collective-permute-start.5 = (bf16[1,432,128]{2,1,0:T(8,128)(2,1)S(1)}, bf16[1,432,128]{2,1,0:T(8,128)(2,1)S(1)}, u32[]{:S(2)}, u32[]{:S(2)}) collective-permute-start(bf16[1,432,128]{2,1,0:T(8,128)(2,1)S(1)} %bitcast.20), channel_id=1, source_target_pairs={{0,16},{4,20},{8,24},{12,28},{16,0},{20,4},{24,8},{28,12},{1,17},{... | collective-permute-start | bytes 331784 | tf_op jit(solution)/shard_map/ppermute | solution.py:18
  25.8 9.6 %collective-permute-start.7 = (bf16[2,432,128]{2,1,0:T(8,128)(2,1)S(1)}, bf16[2,432,128]{2,1,0:T(8,128)(2,1)S(1)}, u32[]{:S(2)}, u32[]{:S(2)}) collective-permute-start(bf16[2,432,128]{2,1,0:T(8,128)(2,1)S(1)} %pad_maximum_fusion.2.refs_0_), channel_id=1, source_target_pairs={{0,8},{4,12},{8,0},{12,4},{16,24},{20,28},{24,16},{28,20},{1,9},{5... | collective-permute-start | bytes 663560 | tf_op jit(solution)/shard_map/ppermute | solution.py:18
  25.9 9.5 %collective-permute-start.9 = (bf16[2,432,128]{2,1,0:T(8,128)(2,1)S(1)}, bf16[2,432,128]{2,1,0:T(8,128)(2,1)S(1)}, u32[]{:S(2)}, u32[]{:S(2)}) collective-permute-start(bf16[2,432,128]{2,1,0:T(8,128)(2,1)S(1)} %pad_maximum_fusion.2.refs_0_), channel_id=1, source_target_pairs={{0,4},{4,0},{8,12},{12,8},{16,20},{20,16},{24,28},{28,24},{1,5},{5... | collective-permute-start | bytes 663560 | tf_op jit(solution)/shard_map/ppermute | solution.py:18
  28.2 5.7 %collective-permute-start.2 = (bf16[10,6,1,256]{3,2,1,0:T(2,128)(2,1)}, bf16[10,6,1,256]{3,2,1,0:T(2,128)(2,1)}, u32[]{:S(2)}, u32[]{:S(2)}) collective-permute-start(bf16[10,6,1,256]{3,2,1,0:T(2,128)(2,1)} %broadcast_select_fusion.5), channel_id=1, source_target_pairs={{0,4},{4,0},{8,12},{12,8},{16,20},{20,16},{24,28},{28,24},{1,5},{5... | collective-permute-start | bytes 92168 | tf_op jit(solution)/shard_map/ppermute | solution.py:18
  28.8 20.9 %copy-start.7 = (bf16[1,4,16,256]{3,2,1,0:T(8,128)(2,1)S(1)}, bf16[1,4,16,256]{3,2,1,0:T(8,128)(2,1)}, u32[]{:S(2)}) copy-start(bf16[1,4,16,256]{3,2,1,0:T(8,128)(2,1)} %copy-done.5) | copy-start | bytes 98308
  28.8 10.7 %collective-permute-start.25 = (bf16[3,432,128]{2,1,0:T(8,128)(2,1)S(1)}, bf16[3,432,128]{2,1,0:T(8,128)(2,1)S(1)}, u32[]{:S(2)}, u32[]{:S(2)}) collective-permute-start(bf16[3,432,128]{2,1,0:T(8,128)(2,1)S(1)} %shard_map.99), channel_id=1, source_target_pairs={{0,2},{1,3},{2,0},{3,1},{4,6},{5,7},{6,4},{7,5},{8,10},{9,11},{10,... | collective-permute-start | bytes 995336 | tf_op jit(solution)/shard_map/ppermute | solution.py:18
  30.6 19.1 %copy-start.4 = (bf16[1,1,8,4,16,256]{5,4,3,2,1,0:T(8,128)(2,1)S(1)}, bf16[1,1,8,4,16,256]{5,4,3,2,1,0:T(8,128)(2,1)}, u32[]{:S(2)}) copy-start(bf16[1,1,8,4,16,256]{5,4,3,2,1,0:T(8,128)(2,1)} %param.6) | copy-start | bytes 786436
  30.6 9.3 %collective-permute-start.6 = (bf16[2,432,128]{2,1,0:T(8,128)(2,1)S(1)}, bf16[2,432,128]{2,1,0:T(8,128)(2,1)S(1)}, u32[]{:S(2)}, u32[]{:S(2)}) collective-permute-start(bf16[2,432,128]{2,1,0:T(8,128)(2,1)S(1)} %pad_maximum_fusion.2.refs_0_), channel_id=1, source_target_pairs={{0,1},{1,0},{2,3},{3,2},{4,5},{5,4},{6,7},{7,6},{8,9},{9,8},{10,11... | collective-permute-start | bytes 663560 | tf_op jit(solution)/shard_map/ppermute | solution.py:18
  33.9 10.4 %collective-permute-start.13 = (bf16[2,432,128]{2,1,0:T(8,128)(2,1)S(1)}, bf16[2,432,128]{2,1,0:T(8,128)(2,1)S(1)}, u32[]{:S(2)}, u32[]{:S(2)}) collective-permute-start(bf16[2,432,128]{2,1,0:T(8,128)(2,1)S(1)} %pad_maximum_fusion.2.refs_0_), channel_id=1, source_target_pairs={{0,2},{1,3},{2,0},{3,1},{4,6},{5,7},{6,4},{7,5},{8,10},{9,11},{10,... | collective-permute-start | bytes 663560 | tf_op jit(solution)/shard_map/ppermute | solution.py:18
  35.4 12.8 %collective-permute-start.8 = (bf16[2,432,128]{2,1,0:T(8,128)(2,1)S(1)}, bf16[2,432,128]{2,1,0:T(8,128)(2,1)S(1)}, u32[]{:S(2)}, u32[]{:S(2)}) collective-permute-start(bf16[2,432,128]{2,1,0:T(8,128)(2,1)S(1)} %collective-permute-done.7.refs_2_), channel_id=1, source_target_pairs={{0,1},{1,0},{2,3},{3,2},{4,5},{5,4},{6,7},{7,6},{8,9},{9,8},{10,11... | collective-permute-start | bytes 663560 | tf_op jit(solution)/shard_map/ppermute | solution.py:18
  35.4 11.3 %collective-permute-start.17 = (bf16[2,432,128]{2,1,0:T(8,128)(2,1)S(1)}, bf16[2,432,128]{2,1,0:T(8,128)(2,1)S(1)}, u32[]{:S(2)}, u32[]{:S(2)}) collective-permute-start(bf16[2,432,128]{2,1,0:T(8,128)(2,1)S(1)} %collective-permute-done.7.refs_2_), channel_id=1, source_target_pairs={{0,2},{1,3},{2,0},{3,1},{4,6},{5,7},{6,4},{7,5},{8,10},{9,11},{10,... | collective-permute-start | bytes 663560 | tf_op jit(solution)/shard_map/ppermute | solution.py:18
  39.6 11.5 %collective-permute-start.10 = (bf16[2,432,128]{2,1,0:T(8,128)(2,1)S(1)}, bf16[2,432,128]{2,1,0:T(8,128)(2,1)S(1)}, u32[]{:S(2)}, u32[]{:S(2)}) collective-permute-start(bf16[2,432,128]{2,1,0:T(8,128)(2,1)S(1)} %collective-permute-done.9.refs_4_), channel_id=1, source_target_pairs={{0,1},{1,0},{2,3},{3,2},{4,5},{5,4},{6,7},{7,6},{8,9},{9,8},{10,11... | collective-permute-start | bytes 663560 | tf_op jit(solution)/shard_map/ppermute | solution.py:18
  39.9 14.6 %collective-permute-start.11 = (bf16[2,432,128]{2,1,0:T(8,128)(2,1)S(1)}, bf16[2,432,128]{2,1,0:T(8,128)(2,1)S(1)}, u32[]{:S(2)}, u32[]{:S(2)}) collective-permute-start(bf16[2,432,128]{2,1,0:T(8,128)(2,1)S(1)} %collective-permute-done.9.refs_4_), channel_id=1, source_target_pairs={{0,8},{4,12},{8,0},{12,4},{16,24},{20,28},{24,16},{28,20},{1,9},{5... | collective-permute-start | bytes 663560 | tf_op jit(solution)/shard_map/ppermute | solution.py:18
  44.3 10.3 %collective-permute-start.15 = (bf16[2,432,128]{2,1,0:T(8,128)(2,1)S(1)}, bf16[2,432,128]{2,1,0:T(8,128)(2,1)S(1)}, u32[]{:S(2)}, u32[]{:S(2)}) collective-permute-start(bf16[2,432,128]{2,1,0:T(8,128)(2,1)S(1)} %collective-permute-done.13.refs_8_), channel_id=1, source_target_pairs={{0,4},{4,0},{8,12},{12,8},{16,20},{20,16},{24,28},{28,24},{1,5},{5... | collective-permute-start | bytes 663560 | tf_op jit(solution)/shard_map/ppermute | solution.py:18
  46.7 8.4 %collective-permute-start.19 = (bf16[2,432,128]{2,1,0:T(8,128)(2,1)S(1)}, bf16[2,432,128]{2,1,0:T(8,128)(2,1)S(1)}, u32[]{:S(2)}, u32[]{:S(2)}) collective-permute-start(bf16[2,432,128]{2,1,0:T(8,128)(2,1)S(1)} %collective-permute-done.17.refs_12_), channel_id=1, source_target_pairs={{0,4},{4,0},{8,12},{12,8},{16,20},{20,16},{24,28},{28,24},{1,5},{5... | collective-permute-start | bytes 663560 | tf_op jit(solution)/shard_map/ppermute | solution.py:18
  48.3 10.0 %collective-permute-start.42 = (bf16[2,432,128]{2,1,0:T(8,128)(2,1)S(1)}, bf16[2,432,128]{2,1,0:T(8,128)(2,1)S(1)}, u32[]{:S(2)}, u32[]{:S(2)}) collective-permute-start(bf16[2,432,128]{2,1,0:T(8,128)(2,1)S(1)} %pad_maximum_fusion.4), channel_id=1, source_target_pairs={{0,2},{1,3},{2,0},{3,1},{4,6},{5,7},{6,4},{7,5},{8,10},{9,11},{10,... | collective-permute-start | bytes 663560 | tf_op jit(solution)/shard_map/ppermute | solution.py:18
  51.0 7.2 %collective-permute-start.26 = (bf16[1,432,128]{2,1,0:T(8,128)(2,1)S(1)}, bf16[1,432,128]{2,1,0:T(8,128)(2,1)S(1)}, u32[]{:S(2)}, u32[]{:S(2)}) collective-permute-start(bf16[1,432,128]{2,1,0:T(8,128)(2,1)S(1)} %bitcast.23), channel_id=1, source_target_pairs={{0,16},{4,20},{8,24},{12,28},{16,0},{20,4},{24,8},{28,12},{1,17},{... | collective-permute-start | bytes 331784 | tf_op jit(solution)/shard_map/ppermute | solution.py:18
  54.5 4.4 %collective-permute-start.14 = (bf16[2,432,128]{2,1,0:T(8,128)(2,1)S(1)}, bf16[2,432,128]{2,1,0:T(8,128)(2,1)S(1)}, u32[]{:S(2)}, u32[]{:S(2)}) collective-permute-start(bf16[2,432,128]{2,1,0:T(8,128)(2,1)S(1)} %collective-permute-done.13.refs_8_), channel_id=1, source_target_pairs={{0,1},{1,0},{2,3},{3,2},{4,5},{5,4},{6,7},{7,6},{8,9},{9,8},{10,11... | collective-permute-start | bytes 663560 | tf_op jit(solution)/shard_map/ppermute | solution.py:18
  54.6 5.6 %collective-permute-start.18 = (bf16[2,432,128]{2,1,0:T(8,128)(2,1)S(1)}, bf16[2,432,128]{2,1,0:T(8,128)(2,1)S(1)}, u32[]{:S(2)}, u32[]{:S(2)}) collective-permute-start(bf16[2,432,128]{2,1,0:T(8,128)(2,1)S(1)} %collective-permute-done.17.refs_12_), channel_id=1, source_target_pairs={{0,1},{1,0},{2,3},{3,2},{4,5},{5,4},{6,7},{7,6},{8,9},{9,8},{10,11... | collective-permute-start | bytes 663560 | tf_op jit(solution)/shard_map/ppermute | solution.py:18
  55.1 3.9 %collective-permute-start.12 = (bf16[2,432,128]{2,1,0:T(8,128)(2,1)S(1)}, bf16[2,432,128]{2,1,0:T(8,128)(2,1)S(1)}, u32[]{:S(2)}, u32[]{:S(2)}) collective-permute-start(bf16[2,432,128]{2,1,0:T(8,128)(2,1)S(1)} %collective-permute-done.11.refs_6_), channel_id=1, source_target_pairs={{0,1},{1,0},{2,3},{3,2},{4,5},{5,4},{6,7},{7,6},{8,9},{9,8},{10,11... | collective-permute-start | bytes 663560 | tf_op jit(solution)/shard_map/ppermute | solution.py:18
  58.3 1.5 %collective-permute-start.16 = (bf16[2,432,128]{2,1,0:T(8,128)(2,1)S(1)}, bf16[2,432,128]{2,1,0:T(8,128)(2,1)S(1)}, u32[]{:S(2)}, u32[]{:S(2)}) collective-permute-start(bf16[2,432,128]{2,1,0:T(8,128)(2,1)S(1)} %collective-permute-done.15.refs_10_), channel_id=1, source_target_pairs={{0,1},{1,0},{2,3},{3,2},{4,5},{5,4},{6,7},{7,6},{8,9},{9,8},{10,11... | collective-permute-start | bytes 663560 | tf_op jit(solution)/shard_map/ppermute | solution.py:18
  58.3 2.4 %collective-permute-start.20 = (bf16[2,432,128]{2,1,0:T(8,128)(2,1)S(1)}, bf16[2,432,128]{2,1,0:T(8,128)(2,1)S(1)}, u32[]{:S(2)}, u32[]{:S(2)}) collective-permute-start(bf16[2,432,128]{2,1,0:T(8,128)(2,1)S(1)} %collective-permute-done.19.refs_14_), channel_id=1, source_target_pairs={{0,1},{1,0},{2,3},{3,2},{4,5},{5,4},{6,7},{7,6},{8,9},{9,8},{10,11... | collective-permute-start | bytes 663560 | tf_op jit(solution)/shard_map/ppermute | solution.py:18
  58.9 6.4 %collective-permute-start.27 = (bf16[2,432,128]{2,1,0:T(8,128)(2,1)S(1)}, bf16[2,432,128]{2,1,0:T(8,128)(2,1)S(1)}, u32[]{:S(2)}, u32[]{:S(2)}) collective-permute-start(bf16[2,432,128]{2,1,0:T(8,128)(2,1)S(1)} %pad_maximum_fusion.3.refs_0_), channel_id=1, source_target_pairs={{0,1},{1,0},{2,3},{3,2},{4,5},{5,4},{6,7},{7,6},{8,9},{9,8},{10,11... | collective-permute-start | bytes 663560 | tf_op jit(solution)/shard_map/ppermute | solution.py:18
  59.0 8.2 %collective-permute-start.28 = (bf16[2,432,128]{2,1,0:T(8,128)(2,1)S(1)}, bf16[2,432,128]{2,1,0:T(8,128)(2,1)S(1)}, u32[]{:S(2)}, u32[]{:S(2)}) collective-permute-start(bf16[2,432,128]{2,1,0:T(8,128)(2,1)S(1)} %pad_maximum_fusion.3.refs_0_), channel_id=1, source_target_pairs={{0,8},{4,12},{8,0},{12,4},{16,24},{20,28},{24,16},{28,20},{1,9},{5... | collective-permute-start | bytes 663560 | tf_op jit(solution)/shard_map/ppermute | solution.py:18
  59.7 14.4 %collective-permute-start.30 = (bf16[2,432,128]{2,1,0:T(8,128)(2,1)S(1)}, bf16[2,432,128]{2,1,0:T(8,128)(2,1)S(1)}, u32[]{:S(2)}, u32[]{:S(2)}) collective-permute-start(bf16[2,432,128]{2,1,0:T(8,128)(2,1)S(1)} %pad_maximum_fusion.3.refs_0_), channel_id=1, source_target_pairs={{0,4},{4,0},{8,12},{12,8},{16,20},{20,16},{24,28},{28,24},{1,5},{5... | collective-permute-start | bytes 663560 | tf_op jit(solution)/shard_map/ppermute | solution.py:18
  60.2 16.7 %collective-permute-start.34 = (bf16[2,432,128]{2,1,0:T(8,128)(2,1)S(1)}, bf16[2,432,128]{2,1,0:T(8,128)(2,1)S(1)}, u32[]{:S(2)}, u32[]{:S(2)}) collective-permute-start(bf16[2,432,128]{2,1,0:T(8,128)(2,1)S(1)} %pad_maximum_fusion.3.refs_0_), channel_id=1, source_target_pairs={{0,2},{1,3},{2,0},{3,1},{4,6},{5,7},{6,4},{7,5},{8,10},{9,11},{10,... | collective-permute-start | bytes 663560 | tf_op jit(solution)/shard_map/ppermute | solution.py:18
  63.0 5.1 %collective-permute-start.21 = (bf16[1,4,16,256]{3,2,1,0:T(8,128)(2,1)S(1)}, bf16[1,4,16,256]{3,2,1,0:T(8,128)(2,1)S(1)}, u32[]{:S(2)}, u32[]{:S(2)}) collective-permute-start(bf16[1,4,16,256]{3,2,1,0:T(8,128)(2,1)S(1)} %slice_select_fusion), channel_id=1, source_target_pairs={{0,16},{4,20},{8,24},{12,28},{16,0},{20,4},{24,8},{28,12},{1,17},{... | collective-permute-start | bytes 98312 | tf_op jit(solution)/shard_map/ppermute | solution.py:18
  65.3 21.6 %collective-permute-start.43 = (bf16[2,864,128]{2,1,0:T(8,128)(2,1)S(1)}, bf16[2,864,128]{2,1,0:T(8,128)(2,1)S(1)}, u32[]{:S(2)}, u32[]{:S(2)}) collective-permute-start(bf16[2,864,128]{2,1,0:T(8,128)(2,1)S(1)} %maximum_select_fusion.1), channel_id=1, source_target_pairs={{0,1},{1,0},{2,3},{3,2},{4,5},{5,4},{6,7},{7,6},{8,9},{9,8},{10,11... | collective-permute-start | bytes 1327112 | tf_op jit(solution)/shard_map/ppermute | solution.py:18
  67.2 11.9 %collective-permute-start.29 = (bf16[2,432,128]{2,1,0:T(8,128)(2,1)S(1)}, bf16[2,432,128]{2,1,0:T(8,128)(2,1)S(1)}, u32[]{:S(2)}, u32[]{:S(2)}) collective-permute-start(bf16[2,432,128]{2,1,0:T(8,128)(2,1)S(1)} %collective-permute-done.28.refs_2_), channel_id=1, source_target_pairs={{0,1},{1,0},{2,3},{3,2},{4,5},{5,4},{6,7},{7,6},{8,9},{9,8},{10,11... | collective-permute-start | bytes 663560 | tf_op jit(solution)/shard_map/ppermute | solution.py:18
  68.2 4.5 %collective-permute-start.22 = (bf16[10,1,16,256]{3,2,1,0:T(8,128)(2,1)S(1)}, bf16[10,1,16,256]{3,2,1,0:T(8,128)(2,1)S(1)}, u32[]{:S(2)}, u32[]{:S(2)}) collective-permute-start(bf16[10,1,16,256]{3,2,1,0:T(8,128)(2,1)S(1)} %fusion.9), channel_id=1, source_target_pairs={{0,8},{4,12},{8,0},{12,4},{16,24},{20,28},{24,16},{28,20},{1,9},{5... | collective-permute-start | bytes 245768 | tf_op jit(solution)/shard_map/ppermute | solution.py:18
  72.7 7.1 %collective-permute-start.38 = (bf16[2,432,128]{2,1,0:T(8,128)(2,1)S(1)}, bf16[2,432,128]{2,1,0:T(8,128)(2,1)S(1)}, u32[]{:S(2)}, u32[]{:S(2)}) collective-permute-start(bf16[2,432,128]{2,1,0:T(8,128)(2,1)S(1)} %collective-permute-done.28.refs_2_), channel_id=1, source_target_pairs={{0,2},{1,3},{2,0},{3,1},{4,6},{5,7},{6,4},{7,5},{8,10},{9,11},{10,... | collective-permute-start | bytes 663560 | tf_op jit(solution)/shard_map/ppermute | solution.py:18
  74.0 13.5 %copy-start = (f32[1,2,864,256]{3,2,1,0:T(8,128)S(1)}, f32[1,2,864,256]{3,2,1,0:T(8,128)}, u32[]{:S(2)}) copy-start(f32[1,2,864,256]{3,2,1,0:T(8,128)} %refs_1_.3) | copy-start | bytes 5308420
  74.0 13.5 %copy-start.1 = (f32[1,2,864,256]{3,2,1,0:T(8,128)S(1)}, f32[1,2,864,256]{3,2,1,0:T(8,128)}, u32[]{:S(2)}) copy-start(f32[1,2,864,256]{3,2,1,0:T(8,128)} %refs_2_.3) | copy-start | bytes 5308420
  74.2 4.9 %collective-permute-start.23 = (bf16[10,6,1,256]{3,2,1,0:T(2,128)(2,1)S(1)}, bf16[10,6,1,256]{3,2,1,0:T(2,128)(2,1)S(1)}, u32[]{:S(2)}, u32[]{:S(2)}) collective-permute-start(bf16[10,6,1,256]{3,2,1,0:T(2,128)(2,1)S(1)} %broadcast_select_fusion.2), channel_id=1, source_target_pairs={{0,4},{4,0},{8,12},{12,8},{16,20},{20,16},{24,28},{28,24},{1,5},{5... | collective-permute-start | bytes 92168 | tf_op jit(solution)/shard_map/ppermute | solution.py:18
  76.8 6.1 %collective-permute-start.32 = (bf16[2,432,128]{2,1,0:T(8,128)(2,1)S(1)}, bf16[2,432,128]{2,1,0:T(8,128)(2,1)S(1)}, u32[]{:S(2)}, u32[]{:S(2)}) collective-permute-start(bf16[2,432,128]{2,1,0:T(8,128)(2,1)S(1)} %collective-permute-done.28.refs_2_), channel_id=1, source_target_pairs={{0,4},{4,0},{8,12},{12,8},{16,20},{20,16},{24,28},{28,24},{1,5},{5... | collective-permute-start | bytes 663560 | tf_op jit(solution)/shard_map/ppermute | solution.py:18
  79.1 2.6 %collective-permute-start.31 = (bf16[2,432,128]{2,1,0:T(8,128)(2,1)S(1)}, bf16[2,432,128]{2,1,0:T(8,128)(2,1)S(1)}, u32[]{:S(2)}, u32[]{:S(2)}) collective-permute-start(bf16[2,432,128]{2,1,0:T(8,128)(2,1)S(1)} %collective-permute-done.30.refs_4_), channel_id=1, source_target_pairs={{0,1},{1,0},{2,3},{3,2},{4,5},{5,4},{6,7},{7,6},{8,9},{9,8},{10,11... | collective-permute-start | bytes 663560 | tf_op jit(solution)/shard_map/ppermute | solution.py:18
  79.1 7.8 %collective-permute-start.36 = (bf16[2,432,128]{2,1,0:T(8,128)(2,1)S(1)}, bf16[2,432,128]{2,1,0:T(8,128)(2,1)S(1)}, u32[]{:S(2)}, u32[]{:S(2)}) collective-permute-start(bf16[2,432,128]{2,1,0:T(8,128)(2,1)S(1)} %collective-permute-done.30.refs_4_), channel_id=1, source_target_pairs={{0,2},{1,3},{2,0},{3,1},{4,6},{5,7},{6,4},{7,5},{8,10},{9,11},{10,... | collective-permute-start | bytes 663560 | tf_op jit(solution)/shard_map/ppermute | solution.py:18
  79.8 7.7 %collective-permute-start.40 = (bf16[2,432,128]{2,1,0:T(8,128)(2,1)S(1)}, bf16[2,432,128]{2,1,0:T(8,128)(2,1)S(1)}, u32[]{:S(2)}, u32[]{:S(2)}) collective-permute-start(bf16[2,432,128]{2,1,0:T(8,128)(2,1)S(1)} %collective-permute-done.38.refs_12_), channel_id=1, source_target_pairs={{0,4},{4,0},{8,12},{12,8},{16,20},{20,16},{24,28},{28,24},{1,5},{5... | collective-permute-start | bytes 663560 | tf_op jit(solution)/shard_map/ppermute | solution.py:18
  81.7 8.1 %collective-permute-start.35 = (bf16[2,432,128]{2,1,0:T(8,128)(2,1)S(1)}, bf16[2,432,128]{2,1,0:T(8,128)(2,1)S(1)}, u32[]{:S(2)}, u32[]{:S(2)}) collective-permute-start(bf16[2,432,128]{2,1,0:T(8,128)(2,1)S(1)} %collective-permute-done.34.refs_8_), channel_id=1, source_target_pairs={{0,1},{1,0},{2,3},{3,2},{4,5},{5,4},{6,7},{7,6},{8,9},{9,8},{10,11... | collective-permute-start | bytes 663560 | tf_op jit(solution)/shard_map/ppermute | solution.py:18
  82.9 6.9 %collective-permute-start.39 = (bf16[2,432,128]{2,1,0:T(8,128)(2,1)S(1)}, bf16[2,432,128]{2,1,0:T(8,128)(2,1)S(1)}, u32[]{:S(2)}, u32[]{:S(2)}) collective-permute-start(bf16[2,432,128]{2,1,0:T(8,128)(2,1)S(1)} %collective-permute-done.38.refs_12_), channel_id=1, source_target_pairs={{0,1},{1,0},{2,3},{3,2},{4,5},{5,4},{6,7},{7,6},{8,9},{9,8},{10,11... | collective-permute-start | bytes 663560 | tf_op jit(solution)/shard_map/ppermute | solution.py:18
  87.0 2.8 %collective-permute-start.33 = (bf16[2,432,128]{2,1,0:T(8,128)(2,1)S(1)}, bf16[2,432,128]{2,1,0:T(8,128)(2,1)S(1)}, u32[]{:S(2)}, u32[]{:S(2)}) collective-permute-start(bf16[2,432,128]{2,1,0:T(8,128)(2,1)S(1)} %collective-permute-done.32.refs_6_), channel_id=1, source_target_pairs={{0,1},{1,0},{2,3},{3,2},{4,5},{5,4},{6,7},{7,6},{8,9},{9,8},{10,11... | collective-permute-start | bytes 663560 | tf_op jit(solution)/shard_map/ppermute | solution.py:18
  87.0 2.8 %collective-permute-start.37 = (bf16[2,432,128]{2,1,0:T(8,128)(2,1)S(1)}, bf16[2,432,128]{2,1,0:T(8,128)(2,1)S(1)}, u32[]{:S(2)}, u32[]{:S(2)}) collective-permute-start(bf16[2,432,128]{2,1,0:T(8,128)(2,1)S(1)} %collective-permute-done.36.refs_10_), channel_id=1, source_target_pairs={{0,1},{1,0},{2,3},{3,2},{4,5},{5,4},{6,7},{7,6},{8,9},{9,8},{10,11... | collective-permute-start | bytes 663560 | tf_op jit(solution)/shard_map/ppermute | solution.py:18
  87.5 2.3 %collective-permute-start.41 = (bf16[2,432,128]{2,1,0:T(8,128)(2,1)S(1)}, bf16[2,432,128]{2,1,0:T(8,128)(2,1)S(1)}, u32[]{:S(2)}, u32[]{:S(2)}) collective-permute-start(bf16[2,432,128]{2,1,0:T(8,128)(2,1)S(1)} %collective-permute-done.40.refs_14_), channel_id=1, source_target_pairs={{0,1},{1,0},{2,3},{3,2},{4,5},{5,4},{6,7},{7,6},{8,9},{9,8},{10,11... | collective-permute-start | bytes 663560 | tf_op jit(solution)/shard_map/ppermute | solution.py:18
